TPU v7x, 32 devices: a whole 2x2x4 slice. The times are simulated.
32 devices in a mesh: dp: 4 (over y, x), mp: 8 (over z, core).
Axes of the slice: x: 2, y: 2, z: 4, core: 2. Of those that a mesh axis runs over, the one named last changes fastest.
Arguments:
- tokens: bfloat16 [16384, 768], P(('dp', 'mp')), may hold values from -6 to 6
- segment_ids: int32 [32, 512], P('dp'), may hold values from 0 to 15, never falling along the last dimension, each value on 1 to 256 neighbouring positions
- gain_one: float32 [768], replicated, may hold values from 0.5 to 1.5
- gain_two: float32 [768], replicated, may hold values from 0.5 to 1.5
- value_weight: bfloat16 [768, 768], P('dp', 'mp'), may hold values from -0.21875 to 0.21875
- mixgate_weight: bfloat16 [768, 768], P('dp', 'mp'), may hold values from -0.21875 to 0.21875
- condition_weight: bfloat16 [768, 48], P('dp', 'mp'), may hold values from -5 to 5
- filter_base: bfloat16 [48, 1024], P('mp', 'dp'), may hold values from -0.8984375 to 0.8984375
- filter_shift: bfloat16 [48, 1024], P('mp', 'dp'), may hold values from -0.8984375 to 0.8984375
- mixout_weight: bfloat16 [768, 768], P('mp', 'dp'), may hold values from -0.21875 to 0.21875
- gate_weight: bfloat16 [768, 3072], P('dp', 'mp'), may hold values from -0.21875 to 0.21875
- up_weight: bfloat16 [768, 3072], P('dp', 'mp'), may hold values from -0.21875 to 0.21875
- down_weight: bfloat16 [3072, 768], P('mp', 'dp'), may hold values from -0.109375 to 0.109375
- output_grad: bfloat16 [16384, 768], P(('dp', 'mp')), may hold values from -6 to 6
Outputs:
- output: bfloat16 [16384, 768], P(('dp', 'mp'))
- input_grad: bfloat16 [16384, 768], P(('dp', 'mp'))
- gain_one_grad: float32 [768], replicated
- gain_two_grad: float32 [768], replicated
- value_grad: float32 [768, 768], P('dp', 'mp')
- mixgate_grad: float32 [768, 768], P('dp', 'mp')
- condition_grad: float32 [768, 48], P('dp', 'mp')
- filter_base_grad: float32 [48, 1024], P('mp', 'dp')
- filter_shift_grad: float32 [48, 1024], P('mp', 'dp')
- mixout_grad: float32 [768, 768], P('mp', 'dp')
- gate_grad: float32 [768, 3072], P('dp', 'mp')
- up_grad: float32 [768, 3072], P('dp', 'mp')
- down_grad: float32 [3072, 768], P('mp', 'dp')
Inputs may be any that keep to these rules, and one draw needn't show every extreme that they name: `segment_ids`: in each row the ids start at 0, never fall and rise by one at each new sentence, up to 15; a sentence has 1 to 256 tokens.
All inputs are finite; a program needn't handle non-finite values.
Results may differ from a plain program's by a relative error of at most 0.024.
Values may be sent and summed in bfloat16 or wider, within the bound.
No kernel may reach another device: no remote copies, remote signals or barrier semaphores. Data moves between devices by JAX's collectives and lax.ppermute only.
A program may use at most 192 MiB of HBM per device.

v0:
```python
from functools import partial

import jax
import jax.numpy as jnp
from jax import lax
from jax.sharding import PartitionSpec as P

epsilon = 1e-05
highest = lax.Precision.HIGHEST


def normalize(token_rows, scale_gain):
    centre = jnp.mean(token_rows, axis=-1, keepdims=True)
    centred = token_rows - centre
    spread = jnp.mean(centred * centred, axis=-1, keepdims=True)
    return centred * lax.rsqrt(spread + epsilon) * scale_gain


def band(kernel):
    groups, double_len = kernel.shape
    length = double_len // 2
    flipped = jnp.roll(kernel[:, ::-1], 1 - length, axis=1)
    flat_taps = jnp.tile(flipped, (1, length))[:, : length * (double_len - 1)]
    return flat_taps.reshape(groups, length, double_len - 1)[:, :, :length]


def band_back(gradient):
    groups, length, _ = gradient.shape
    padded = jnp.pad(gradient, ((0, 0), (0, 0), (0, length - 1)))
    flat_taps = padded.reshape(groups, length * (2 * length - 1))
    flat_taps = jnp.pad(flat_taps, ((0, 0), (0, length)))
    folded = jnp.sum(flat_taps.reshape(groups, length, 2 * length), axis=1)
    return jnp.roll(folded, length - 1, axis=1)[:, ::-1]


def row_band(segment_row, cond_row, taps_first, taps_second):
    kernel = taps_first + cond_row[:, None] * taps_second
    same_doc = (segment_row[:, None] == segment_row[None, :]).astype(jnp.float32)
    return ((band(kernel) * same_doc[None]).astype(jnp.bfloat16), same_doc)


def row_forward(member, taps_first, taps_second):
    values_row, segment_row, cond_row = member
    band_matrix, same_doc = row_band(segment_row, cond_row, taps_first, taps_second)
    length, channels = values_row.shape
    groups = taps_first.shape[0]
    split_values = values_row.reshape(length, groups, channels // groups)
    result = jnp.einsum(
        "gij,jgc->igc", band_matrix, split_values, preferred_element_type=jnp.float32
    )
    return result.reshape(length, channels)


def row_backward(member, taps_first, taps_second):
    values_row, segment_row, cond_row, grad_row = member
    band_matrix, same_doc = row_band(segment_row, cond_row, taps_first, taps_second)
    length, channels = values_row.shape
    groups = taps_first.shape[0]
    split_values = values_row.reshape(length, groups, channels // groups)
    split_grad = grad_row.reshape(length, groups, channels // groups)
    grad_values = jnp.einsum(
        "gij,igc->jgc", band_matrix, split_grad, preferred_element_type=jnp.float32
    )
    grad_band = jnp.einsum(
        "igc,jgc->gij", split_grad, split_values, preferred_element_type=jnp.float32
    )
    grad_kernel = band_back(grad_band * same_doc[None])
    return (grad_values.astype(jnp.bfloat16).reshape(length, channels), grad_kernel)


def mix_inputs(gathered, value_full, mixgate_full, condition_full, row_total, length):
    values_mix = jnp.dot(gathered, value_full, preferred_element_type=jnp.float32).astype(
        jnp.bfloat16
    )
    gates_mix = jnp.dot(gathered, mixgate_full, preferred_element_type=jnp.float32)
    summary = jnp.sum(gathered.reshape(row_total, length, -1), axis=1, dtype=jnp.float32) / length
    cond_tanh = jnp.tanh(jnp.dot(summary, condition_full.astype(jnp.float32), precision=highest))
    return (values_mix, gates_mix, summary, cond_tanh)


def mlp_inputs(gathered, gate_full, up_full):
    gate_pre = jnp.dot(gathered, gate_full, preferred_element_type=jnp.float32)
    up_pre = jnp.dot(gathered, up_full, preferred_element_type=jnp.float32)
    hidden = (jax.nn.silu(gate_pre) * up_pre).astype(jnp.bfloat16)
    return (gate_pre, up_pre, hidden)


def body(
    tokens,
    segment_ids,
    gain_one,
    gain_two,
    value_weight,
    mixgate_weight,
    condition_weight,
    filter_base,
    filter_shift,
    mixout_weight,
    gate_weight,
    up_weight,
    down_weight,
    output_grad,
):
    (
        value_full,
        mixgate_full,
        condition_full,
        gate_full,
        up_full,
        base_full,
        shift_full,
        mixout_full,
        down_full,
    ) = (
        lax.all_gather(value_weight, "dp", axis=0, tiled=True),
        lax.all_gather(mixgate_weight, "dp", axis=0, tiled=True),
        lax.all_gather(condition_weight, "dp", axis=0, tiled=True),
        lax.all_gather(gate_weight, "dp", axis=0, tiled=True),
        lax.all_gather(up_weight, "dp", axis=0, tiled=True),
        lax.all_gather(filter_base, "dp", axis=1, tiled=True),
        lax.all_gather(filter_shift, "dp", axis=1, tiled=True),
        lax.all_gather(mixout_weight, "dp", axis=1, tiled=True),
        lax.all_gather(down_weight, "dp", axis=1, tiled=True),
    )
    local_rows = tokens.shape[0]
    length = segment_ids.shape[1]
    row_total = segment_ids.shape[0]
    taps_first = base_full.astype(jnp.float32)
    taps_second = shift_full.astype(jnp.float32)
    input_float = tokens.astype(jnp.float32)
    normed_one = normalize(input_float, gain_one).astype(jnp.bfloat16)
    gathered_one = lax.all_gather(normed_one, "mp", axis=0, tiled=True)
    values_mix, gates_mix, summary, cond_tanh = mix_inputs(
        gathered_one, value_full, mixgate_full, condition_full, row_total, length
    )
    channels = values_mix.shape[1]
    conv_rows = lax.map(
        partial(row_forward, taps_first=taps_first, taps_second=taps_second),
        (values_mix.reshape(row_total, length, channels), segment_ids, cond_tanh),
    )
    conv_rows = conv_rows.reshape(row_total * length, channels)
    mixed = (conv_rows * gates_mix).astype(jnp.bfloat16)
    picked = mixed
    branch = lax.psum_scatter(
        jnp.dot(picked, mixout_full, preferred_element_type=jnp.float32).astype(jnp.bfloat16),
        "mp",
        scatter_dimension=0,
        tiled=True,
    ).astype(jnp.float32)
    middle = input_float + branch
    normed_two = normalize(middle, gain_two).astype(jnp.bfloat16)
    grad_float = output_grad.astype(jnp.float32)
    gathered_two = lax.all_gather(normed_two, "mp", axis=0, tiled=True)
    gate_pre, up_pre, hidden = mlp_inputs(gathered_two, gate_full, up_full)
    picked = hidden
    feed = lax.psum_scatter(
        jnp.dot(picked, down_full, preferred_element_type=jnp.float32).astype(jnp.bfloat16),
        "mp",
        scatter_dimension=0,
        tiled=True,
    ).astype(jnp.float32)
    output = (middle + feed).astype(jnp.bfloat16)
    grad_rows = lax.all_gather(output_grad, "mp", axis=0, tiled=True)
    grad_hidden = jnp.dot(grad_rows, down_full.T, preferred_element_type=jnp.float32)
    sigmoid_gate = jax.nn.sigmoid(gate_pre)
    grad_gate_pre = (
        grad_hidden * up_pre * sigmoid_gate * (1.0 + gate_pre * (1.0 - sigmoid_gate))
    ).astype(jnp.bfloat16)
    grad_up_pre = (grad_hidden * gate_pre * sigmoid_gate).astype(jnp.bfloat16)
    down_grad = jnp.dot(hidden.T, grad_rows, preferred_element_type=jnp.float32)
    gate_grad = jnp.dot(gathered_two.T, grad_gate_pre, preferred_element_type=jnp.float32)
    up_grad = jnp.dot(gathered_two.T, grad_up_pre, preferred_element_type=jnp.float32)
    grad_normed_two = lax.psum_scatter(
        (
            jnp.dot(grad_gate_pre, gate_full.T, preferred_element_type=jnp.float32)
            + jnp.dot(grad_up_pre, up_full.T, preferred_element_type=jnp.float32)
        ).astype(jnp.bfloat16),
        "mp",
        scatter_dimension=0,
        tiled=True,
    ).astype(jnp.float32)
    _, pull_two = jax.vjp(normalize, middle, gain_two)
    grad_middle_norm, gain_two_part = pull_two(grad_normed_two)
    grad_middle = grad_float + grad_middle_norm
    grad_branch = lax.all_gather(grad_middle.astype(jnp.bfloat16), "mp", axis=0, tiled=True)
    grad_mixed = jnp.dot(grad_branch, mixout_full.T, preferred_element_type=jnp.float32)
    grad_conv = (grad_mixed * gates_mix).astype(jnp.bfloat16)
    grad_values, grad_kernel = lax.map(
        partial(row_backward, taps_first=taps_first, taps_second=taps_second),
        (
            values_mix.reshape(row_total, length, channels),
            segment_ids,
            cond_tanh,
            grad_conv.reshape(row_total, length, channels),
        ),
    )
    grad_values = grad_values.reshape(row_total * length, channels)
    grad_gates = (grad_mixed * conv_rows).astype(jnp.bfloat16)
    mixout_grad = jnp.dot(mixed.T, grad_branch, preferred_element_type=jnp.float32)
    base_grad = jnp.sum(grad_kernel, axis=0)
    shift_grad = jnp.sum(grad_kernel * cond_tanh[:, :, None], axis=0)
    grad_cond = jnp.sum(grad_kernel * taps_second[None], axis=2) * (1.0 - cond_tanh * cond_tanh)
    condition_grad = jnp.dot(summary.T, grad_cond, precision=highest)
    grad_summary = (
        jnp.dot(grad_cond, condition_full.astype(jnp.float32).T, precision=highest) / length
    )
    value_grad = jnp.dot(gathered_one.T, grad_values, preferred_element_type=jnp.float32)
    mixgate_grad = jnp.dot(gathered_one.T, grad_gates, preferred_element_type=jnp.float32)
    row_of = lax.iota(jnp.int32, lax.axis_size("mp") * local_rows) // length
    onehot = (row_of[:, None] == lax.iota(jnp.int32, row_total)[None, :]).astype(jnp.float32)
    grad_normed_one = lax.psum_scatter(
        (
            jnp.dot(grad_values, value_full.T, preferred_element_type=jnp.float32)
            + jnp.dot(grad_gates, mixgate_full.T, preferred_element_type=jnp.float32)
            + jnp.dot(onehot, grad_summary, precision=highest)
        ).astype(jnp.bfloat16),
        "mp",
        scatter_dimension=0,
        tiled=True,
    ).astype(jnp.float32)
    _, pull_one = jax.vjp(normalize, input_float, gain_one)
    grad_input_norm, gain_one_part = pull_one(grad_normed_one)
    input_grad = (grad_middle + grad_input_norm).astype(jnp.bfloat16)
    gain_one_grad, gain_two_grad = lax.psum((gain_one_part, gain_two_part), ("dp", "mp"))
    (
        value_sum,
        mixgate_sum,
        condition_sum,
        gate_sum,
        up_sum,
        base_sum,
        shift_sum,
        mixout_sum,
        down_sum,
    ) = (
        lax.psum_scatter(
            value_grad.astype(jnp.bfloat16), "dp", scatter_dimension=0, tiled=True
        ).astype(jnp.float32),
        lax.psum_scatter(
            mixgate_grad.astype(jnp.bfloat16), "dp", scatter_dimension=0, tiled=True
        ).astype(jnp.float32),
        lax.psum_scatter(
            condition_grad.astype(jnp.bfloat16), "dp", scatter_dimension=0, tiled=True
        ).astype(jnp.float32),
        lax.psum_scatter(
            gate_grad.astype(jnp.bfloat16), "dp", scatter_dimension=0, tiled=True
        ).astype(jnp.float32),
        lax.psum_scatter(
            up_grad.astype(jnp.bfloat16), "dp", scatter_dimension=0, tiled=True
        ).astype(jnp.float32),
        lax.psum_scatter(
            base_grad.astype(jnp.bfloat16), "dp", scatter_dimension=1, tiled=True
        ).astype(jnp.float32),
        lax.psum_scatter(
            shift_grad.astype(jnp.bfloat16), "dp", scatter_dimension=1, tiled=True
        ).astype(jnp.float32),
        lax.psum_scatter(
            mixout_grad.astype(jnp.bfloat16), "dp", scatter_dimension=1, tiled=True
        ).astype(jnp.float32),
        lax.psum_scatter(
            down_grad.astype(jnp.bfloat16), "dp", scatter_dimension=1, tiled=True
        ).astype(jnp.float32),
    )
    return (
        output,
        input_grad,
        gain_one_grad,
        gain_two_grad,
        value_sum,
        mixgate_sum,
        condition_sum,
        base_sum,
        shift_sum,
        mixout_sum,
        gate_sum,
        up_sum,
        down_sum,
    )


def solution(mesh):
    in_specs = (
        P(("dp", "mp"), None),
        P("dp", None),
        P(),
        P(),
        P("dp", "mp"),
        P("dp", "mp"),
        P("dp", "mp"),
        P("mp", "dp"),
        P("mp", "dp"),
        P("mp", "dp"),
        P("dp", "mp"),
        P("dp", "mp"),
        P("mp", "dp"),
        P(("dp", "mp"), None),
    )
    out_specs = (
        P(("dp", "mp"), None),
        P(("dp", "mp"), None),
        P(),
        P(),
        P("dp", "mp"),
        P("dp", "mp"),
        P("dp", "mp"),
        P("mp", "dp"),
        P("mp", "dp"),
        P("mp", "dp"),
        P("dp", "mp"),
        P("dp", "mp"),
        P("mp", "dp"),
    )
    return jax.shard_map(body, mesh=mesh, in_specs=in_specs, out_specs=out_specs, check_vma=False)
```

profile of v0, /device:TPU:0, one launch (start us, length us, event | category | flops | bytes accessed | tf_op | source)
XLA Modules:
  0.0 2454.1 jit_solution(5315738766540864973)
XLA Ops:
  64.5 15.6 all-gather.6.cloned.1.call-done
  86.7 581.0 %while.24 = (s32[]{:T(128)}, f32[8,512,96]{1,0,2:T(8,128)}, bf16[8,512,96]{1,2,0:T(8,128)(2,1)S(1)}, f32[8,6]{1,0:T(8,128)S(1)}, f32[6,1024]{1,0:T(8,128)S(1)}, ...) while((s32[]{:T(128)}, f32[8,512,96]{1,0,2:T(8,128)}, ...), condition=%wide.region_4.5_spmd, body=%wide.region_3.4_spmd.sunk | while | flops 54020096 | bytes 123146416 | solution.py:137
  95.3 17.9 copy.87
  136.7 14.0 reshape.262
  167.9 17.9 copy.87
  209.3 14.0 reshape.262
  240.4 17.9 copy.87
  281.8 14.0 reshape.262
  312.9 17.9 copy.87
  354.4 14.0 reshape.262
  385.5 17.9 copy.87
  426.9 14.0 reshape.262
  458.0 17.9 copy.87
  499.4 14.0 reshape.262
  530.6 17.9 copy.87
  572.0 14.0 reshape.262
  603.1 17.9 copy.87
  644.5 14.0 reshape.262
  682.7 68.6 %reduce-scatter.18.cloned.1.call-done = bf16[512,768]{1,0:T(8,128)(2,1)} async-done(((bf16[4096,768]{1,0:T(8,128)(2,1)}), bf16[512,768]{1,0:T(8,128)(2,1)}) %reduce-scatter.18.cloned.1.call-update) | async-done | bytes 786448 | tf_op jit(solution)/shard_map/reduce_scatter | solution.py:144
  792.0 28.7 %all-gather.8.cloned.1.call-done = bf16[4096,768]{1,0:T(8,128)(2,1)} async-done(((bf16[512,768]{1,0:T(8,128)(2,1)}), bf16[4096,768]{1,0:T(8,128)(2,1)}) %all-gather.8.cloned.1.call-update) | async-done | bytes 6291472 | tf_op jit(solution)/shard_map/all_gather | solution.py:153
  835.6 50.1 %all-gather.10.cloned.1.call-done = bf16[4096,768]{1,0:T(8,128)(2,1)} async-done(((bf16[512,768]{1,0:T(8,128)(2,1)}), bf16[4096,768]{1,0:T(8,128)(2,1)}) %all-gather.10.cloned.1.call-update) | async-done | bytes 6291472 | tf_op jit(solution)/shard_map/all_gather | solution.py:163
  916.6 59.9 %reduce-scatter.22.cloned.1.call-done = bf16[512,768]{1,0:T(8,128)(2,1)} async-done(((bf16[4096,768]{1,0:T(8,128)(2,1)}), bf16[512,768]{1,0:T(8,128)(2,1)}) %reduce-scatter.22.cloned.1.call-update) | async-done | bytes 786448 | tf_op jit(solution)/shard_map/reduce_scatter | solution.py:173
  979.1 67.8 %reduce-scatter.20.cloned.1.call-done = bf16[512,768]{1,0:T(8,128)(2,1)} async-done(((bf16[4096,768]{1,0:T(8,128)(2,1)}), bf16[512,768]{1,0:T(8,128)(2,1)}) %reduce-scatter.20.cloned.1.call-update) | async-done | bytes 786448 | tf_op jit(solution)/shard_map/reduce_scatter | solution.py:156
  1077.2 38.4 %all-gather.12.cloned.1.call-done = bf16[4096,768]{1,0:T(8,128)(2,1)} async-done(((bf16[512,768]{1,0:T(8,128)(2,1)}), bf16[4096,768]{1,0:T(8,128)(2,1)}) %all-gather.12.cloned.1.call-update) | async-done | bytes 6291472 | tf_op jit(solution)/shard_map/all_gather | solution.py:185
  1121.9 1050.8 %while.25 = (s32[]{:T(128)}, bf16[8,512,96]{1,2,0:T(8,128)(2,1)}, f32[8,6,1024]{2,1,0:T(8,128)}, bf16[8,512,96]{1,2,0:T(8,128)(2,1)S(1)}, f32[8,6]{1,0:T(8,128)S...) while((s32[]{:T(128)}, bf16[8,512,96]{1,2,0:T(8,128)(2,1)}, ...), condition=%wide.region_14.15_spmd, body=%wide.region_12.14_spmd.sunk | while | flops 109119488 | bytes 237301968 | solution.py:188
  1149.2 18.1 copy.90
  1191.1 14.0 reshape.264
  1217.1 13.5 reshape.265
  1230.6 14.1 reshape.266
  1277.6 18.0 copy.90
  1319.2 14.0 reshape.264
  1345.1 13.5 reshape.265
  1358.7 14.1 reshape.266
  1405.7 18.0 copy.90
  1447.2 14.0 reshape.264
  1473.2 13.5 reshape.265
  1486.7 14.1 reshape.266
  1533.8 18.0 copy.90
  1575.3 14.0 reshape.264
  1601.3 13.5 reshape.265
  1614.8 14.1 reshape.266
  1661.8 18.0 copy.90
  1703.4 14.0 reshape.264
  1729.3 13.5 reshape.265
  1742.9 14.1 reshape.266
  1789.9 18.0 copy.90
  1831.4 14.0 reshape.264
  1857.4 13.5 reshape.265
  1870.9 14.1 reshape.266
  1918.0 18.0 copy.90
  1959.5 14.0 reshape.264
  1985.5 13.5 reshape.265
  1999.0 14.1 reshape.266
  2046.1 18.0 copy.90
  2087.6 14.0 reshape.264
  2113.5 13.5 reshape.265
  2127.1 14.1 reshape.266
  2204.3 13.0 add_convert_fusion
  2225.3 24.4 reduce-scatter.32.cloned.1.call-done
  2251.0 25.6 %reduce-scatter.42.cloned.1.call-done = bf16[192,96]{1,0:T(8,128)(2,1)} async-done(((bf16[768,96]{1,0:T(8,128)(2,1)}), bf16[192,96]{1,0:T(8,128)(2,1)}) %reduce-scatter.42.cloned.1.call-update) | async-done | bytes 36880
  2278.1 25.9 %reduce-scatter.26.cloned.1.call-done = bf16[192,96]{1,0:T(8,128)(2,1)} async-done(((bf16[768,96]{1,0:T(8,128)(2,1)}), bf16[192,96]{1,0:T(8,128)(2,1)}) %reduce-scatter.26.cloned.1.call-update) | async-done | bytes 36880 | tf_op jit(solution)/shard_map/reduce_scatter | solution.py:236
  2305.5 25.4 %reduce-scatter.28.cloned.1.call-done = bf16[192,96]{1,0:T(8,128)(2,1)} async-done(((bf16[768,96]{1,0:T(8,128)(2,1)}), bf16[192,96]{1,0:T(8,128)(2,1)}) %reduce-scatter.28.cloned.1.call-update) | async-done | bytes 36880 | tf_op jit(solution)/shard_map/reduce_scatter | solution.py:239
  2332.3 70.6 %reduce-scatter.24.cloned.1.call-done = bf16[512,768]{1,0:T(8,128)(2,1)} async-done(((bf16[4096,768]{1,0:T(8,128)(2,1)}), bf16[512,768]{1,0:T(8,128)(2,1)}) %reduce-scatter.24.cloned.1.call-update) | async-done | bytes 786448 | tf_op jit(solution)/shard_map/reduce_scatter | solution.py:211
  2406.7 37.9 %all-reduce.2 = (f32[768]{0:T(1024)}, f32[768]{0:T(1024)}) all-reduce(f32[768]{0:T(1024)S(1)} %get-tuple-element.233, f32[768]{0:T(1024)S(1)} %copy-done.49), channel_id=1, replica_groups=mesh['dp'=4,'mp'=8] {'dp','mp'}, use_global_device_ids=true, to_apply=%region_20.21 | all-reduce | flops 1536 | bytes 12288 | tf_op jit(solution)/shard_map/psum | solution.py:224
  (577 shorter events, 1128.7 us)
Async XLA Ops:
  7.2 5.4 copy-start.50
  7.2 15.1 copy-start.51
  7.2 23.2 copy-start.52
  7.2 30.4 %copy-start.33 = (bf16[96,192]{1,0:T(8,128)(2,1)S(1)}, bf16[96,192]{1,0:T(8,128)(2,1)}, u32[]{:S(2)}) copy-start(bf16[96,192]{1,0:T(8,128)(2,1)} %param.27) | copy-start | bytes 110596
  7.2 40.2 %copy-start.34 = (bf16[192,96]{1,0:T(8,128)(2,1)S(1)}, bf16[192,96]{1,0:T(8,128)(2,1)}, u32[]{:S(2)}) copy-start(bf16[192,96]{1,0:T(8,128)(2,1)} %param.22) | copy-start | bytes 110596
  7.2 48.0 %copy-start.35 = (bf16[192,96]{1,0:T(8,128)(2,1)S(1)}, bf16[192,96]{1,0:T(8,128)(2,1)}, u32[]{:S(2)}) copy-start(bf16[192,96]{1,0:T(8,128)(2,1)} %param.23) | copy-start | bytes 110596
  7.2 72.9 %all-gather.6.cloned.1.call-start = ((), (), s32[]{:S(2)}) async-start(), calls=%async_computation.13 | async-start | bytes 7077888 | tf_op jit(solution)/shard_map/all_gather | solution.py:132
  8.6 1.5 copy-start.27
  10.1 27.6 %copy-start.45 = (f32[512]{0:T(512)}, f32[512]{0:T(512)S(1)}, u32[]{:S(2)}) copy-start(f32[512]{0:T(512)S(1)} %fusion.25) | copy-start | bytes 6148
  10.2 27.6 %copy-start.39 = (f32[512]{0:T(512)}, f32[512]{0:T(512)S(1)}, u32[]{:S(2)}) copy-start(f32[512]{0:T(512)S(1)} %fusion.39) | copy-start | bytes 6148
  12.5 738.8 %reduce-scatter.18.cloned.1.call-start = ((), (), s32[]{:S(2)}) async-start(), calls=%async_computation.14 | async-start | bytes 7077888 | tf_op jit(solution)/shard_map/reduce_scatter | solution.py:144
  22.3 63.8 %copy-start.23 = (bf16[768,6]{0,1:T(8,128)(2,1)}, bf16[768,6]{0,1:T(8,128)(2,1)S(1)}, u32[]{:S(2)}) copy-start(bf16[768,6]{0,1:T(8,128)(2,1)S(1)} %reshape.244) | copy-start | bytes 27652
  55.2 29.9 %copy-start.18 = (bf16[768,96]{1,0:T(8,128)(2,1)}, bf16[768,96]{1,0:T(8,128)(2,1)S(1)}, u32[]{:S(2)}) copy-start(bf16[768,96]{1,0:T(8,128)(2,1)S(1)} %all_gather.40) | copy-start | bytes 442372
  80.1 5.1 copy-start
  667.7 3.4 copy-start.16
  671.1 7.1 copy-start.20
  682.6 68.6 %copy-start.1 = (bf16[512,768]{1,0:T(8,128)(2,1)S(1)}, bf16[512,768]{1,0:T(8,128)(2,1)}, u32[]{:S(2)}) copy-start(bf16[512,768]{1,0:T(8,128)(2,1)} %param.18) | copy-start | bytes 2359300
  682.6 138.1 %all-gather.8.cloned.1.call-start = ((), (), s32[]{:S(2)}) async-start(), calls=%async_computation.15 | async-start | bytes 7077888 | tf_op jit(solution)/shard_map/all_gather | solution.py:153
  751.3 4.3 copy-start.3
  752.8 5.4 copy-start.22
  752.8 2.2 copy-start.31
  757.5 128.2 %all-gather.10.cloned.1.call-start = ((), (), s32[]{:S(2)}) async-start(), calls=%async_computation.17 | async-start | bytes 7077888 | tf_op jit(solution)/shard_map/all_gather | solution.py:163
  758.1 218.5 %reduce-scatter.22.cloned.1.call-start = ((), (), s32[]{:S(2)}) async-start(), calls=%async_computation.18 | async-start | bytes 7077888 | tf_op jit(solution)/shard_map/reduce_scatter | solution.py:173
  820.8 9.4 copy-start.14
  820.8 9.4 copy-start.53
  885.7 12.1 copy-start.15
  897.7 3.5 copy-start.13
  897.7 3.5 copy-start.8
  907.9 139.0 %reduce-scatter.20.cloned.1.call-start = ((), (), s32[]{:S(2)}) async-start(), calls=%async_computation.16 | async-start | bytes 7077888 | tf_op jit(solution)/shard_map/reduce_scatter | solution.py:156
  916.2 60.4 %copy-start.32 = (f32[512]{0:T(512)S(1)}, f32[512]{0:T(512)}, u32[]{:S(2)}) copy-start(f32[512]{0:T(512)} %copy-done.31) | copy-start | bytes 6148
  916.2 60.4 %copy-start.36 = (f32[768]{0:T(1024)S(1)}, f32[768]{0:T(1024)}, u32[]{:S(2)}) copy-start(f32[768]{0:T(1024)} %param.21) | copy-start | bytes 9220
  916.2 60.4 %copy-start.42 = (f32[512]{0:T(512)S(1)}, f32[512]{0:T(512)}, u32[]{:S(2)}) copy-start(f32[512]{0:T(512)} %copy-done.41) | copy-start | bytes 6148
  916.2 63.0 %copy-start.48 = (f32[512]{0:T(512)S(1)}, f32[512]{0:T(512)}, u32[]{:S(2)}) copy-start(f32[512]{0:T(512)} %copy-done.47) | copy-start | bytes 6148
  916.2 199.4 %all-gather.12.cloned.1.call-start = ((), (), s32[]{:S(2)}) async-start(), calls=%async_computation.19 | async-start | bytes 7077888 | tf_op jit(solution)/shard_map/all_gather | solution.py:185
  1046.9 4.3 copy-start.10
  1050.0 10.4 copy-start.43
  1052.3 1165.1 %reduce-scatter.38.cloned.1.call-start = ((), (), s32[]{:S(2)}) async-start(), calls=%async_computation.27 | async-start | bytes 737280 | tf_op jit(solution)/shard_map/reduce_scatter | solution.py:260
  1060.5 1158.8 %reduce-scatter.36.cloned.1.call-start = ((), (), s32[]{:S(2)}) async-start(), calls=%async_computation.26 | async-start | bytes 737280 | tf_op jit(solution)/shard_map/reduce_scatter | solution.py:248
  1068.5 1152.4 %reduce-scatter.34.cloned.1.call-start = ((), (), s32[]{:S(2)}) async-start(), calls=%async_computation.25 | async-start | bytes 737280 | tf_op jit(solution)/shard_map/reduce_scatter | solution.py:245
  1077.2 1145.4 %reduce-scatter.40.cloned.1.call-start = ((), (), s32[]{:S(2)}) async-start(), calls=%async_computation.28 | async-start | bytes 245760
  1115.6 6.3 copy-start.38
  1121.9 1052.5 %copy-start.26 = (f32[8,768]{1,0:T(8,128)S(1)}, f32[8,768]{1,0:T(8,128)}, u32[]{:S(2)}) copy-start(f32[8,768]{1,0:T(8,128)} %copy-done.25) | copy-start | bytes 73732
  1121.9 1053.6 %copy-start.9 = (bf16[4096,96]{0,1:T(8,128)(2,1)S(1)}, bf16[4096,96]{0,1:T(8,128)(2,1)}, u32[]{:S(2)}) copy-start(bf16[4096,96]{0,1:T(8,128)(2,1)} %get-tuple-element.279) | copy-start | bytes 2359300
  1121.9 1053.6 %copy-start.17 = (bf16[768,96]{1,0:T(8,128)(2,1)S(1)}, bf16[768,96]{1,0:T(8,128)(2,1)}, u32[]{:S(2)}) copy-start(bf16[768,96]{1,0:T(8,128)(2,1)} %all_gather.44) | copy-start | bytes 442372
  2175.5 48.6 %reduce-scatter.30.cloned.1.call-start = ((), (), s32[]{:S(2)}) async-start(), calls=%async_computation.23 | async-start | bytes 20480 | tf_op jit(solution)/shard_map/reduce_scatter | solution.py:251
  2175.6 6.4 copy-start.21
  2175.6 6.6 copy-start.19
  2182.1 67.6 %reduce-scatter.32.cloned.1.call-start = ((), (), s32[]{:S(2)}) async-start(), calls=%async_computation.24 | async-start | bytes 20480 | tf_op jit(solution)/shard_map/reduce_scatter | solution.py:254
  2182.1 6.4 copy-start.5
  2188.5 88.1 %reduce-scatter.42.cloned.1.call-start = ((), (), s32[]{:S(2)}) async-start(), calls=%async_computation.29 | async-start | bytes 245760
  2193.3 110.7 %reduce-scatter.26.cloned.1.call-start = ((), (), s32[]{:S(2)}) async-start(), calls=%async_computation.21 | async-start | bytes 245760 | tf_op jit(solution)/shard_map/reduce_scatter | solution.py:236
  2198.7 5.4 copy-start.24
  2198.7 5.6 copy-start.29
  2198.8 132.1 %reduce-scatter.28.cloned.1.call-start = ((), (), s32[]{:S(2)}) async-start(), calls=%async_computation.22 | async-start | bytes 245760 | tf_op jit(solution)/shard_map/reduce_scatter | solution.py:239
  2204.3 198.7 %reduce-scatter.24.cloned.1.call-start = ((), (), s32[]{:S(2)}) async-start(), calls=%async_computation.20 | async-start | bytes 7077888 | tf_op jit(solution)/shard_map/reduce_scatter | solution.py:211
  2217.4 185.6 %copy-start.2 = (bf16[512,768]{1,0:T(8,128)(2,1)S(1)}, bf16[512,768]{1,0:T(8,128)(2,1)}, u32[]{:S(2)}) copy-start(bf16[512,768]{1,0:T(8,128)(2,1)} %param.18) | copy-start | bytes 2359300
  2217.4 185.6 %copy-start.28 = (f32[512]{0:T(512)S(1)}, f32[512]{0:T(512)}, u32[]{:S(2)}) copy-start(f32[512]{0:T(512)} %copy-done.27) | copy-start | bytes 6148
  2217.4 185.6 %copy-start.30 = (f32[768]{0:T(1024)S(1)}, f32[768]{0:T(1024)}, u32[]{:S(2)}) copy-start(f32[768]{0:T(1024)} %param.20) | copy-start | bytes 9220
  2217.4 187.2 %copy-start.46 = (f32[512]{0:T(512)S(1)}, f32[512]{0:T(512)}, u32[]{:S(2)}) copy-start(f32[512]{0:T(512)} %copy-done.45) | copy-start | bytes 6148
  2217.4 187.2 %copy-start.40 = (f32[512]{0:T(512)S(1)}, f32[512]{0:T(512)}, u32[]{:S(2)}) copy-start(f32[512]{0:T(512)} %copy-done.39) | copy-start | bytes 6148
  2217.4 189.3 %copy-start.49 = (f32[768]{0:T(1024)S(1)}, f32[768]{0:T(1024)}, u32[]{:S(2)}) copy-start(f32[768]{0:T(1024)} %get-tuple-element.231) | copy-start | bytes 9220
  2217.4 227.2 %copy-start.7 = (f32[512,768]{1,0:T(8,128)S(1)}, f32[512,768]{1,0:T(8,128)}, u32[]{:S(2)}) copy-start(f32[512,768]{1,0:T(8,128)} %copy-done.6) | copy-start | bytes 4718596
  2217.4 227.2 %copy-start.11 = (bf16[512,768]{1,0:T(8,128)(2,1)S(1)}, bf16[512,768]{1,0:T(8,128)(2,1)}, u32[]{:S(2)}) copy-start(bf16[512,768]{1,0:T(8,128)(2,1)} %param.31) | copy-start | bytes 2359300
  2217.4 227.2 %copy-start.44 = (f32[512]{0:T(512)S(1)}, f32[512]{0:T(512)}, u32[]{:S(2)}) copy-start(f32[512]{0:T(512)} %copy-done.43) | copy-start | bytes 6148
  (7 other events, 5.7 us)
Sparse Core Ops, SparseCore 0:
  12.6 67.4 all-gather.5
  682.8 68.4 reduce-scatter.17
  757.6 63.1 all-gather.7
  822.2 63.3 all-gather.9
  908.0 68.4 reduce-scatter.21
  978.7 68.1 reduce-scatter.19
  1052.5 63.1 all-gather.11
  1118.5 23.7 reduce-scatter.37
  1145.4 25.1 reduce-scatter.35
  1173.2 25.0 reduce-scatter.33
  2175.6 22.4 reduce-scatter.39
  2201.5 22.2 reduce-scatter.29
  2227.4 22.3 reduce-scatter.31
  2252.6 23.9 reduce-scatter.41
  2280.0 23.9 reduce-scatter.25
  2306.8 23.9 reduce-scatter.27
  2333.1 69.7 reduce-scatter.23
where the time goes:
time: 2470 us; the launch traced here: 2450 us
  local copies, waits for them, and re-layouts  1450 us (59%)
  waiting for transfers between devices  502 us (20%)
  matrix products  197 us (8%)
  other arithmetic  142 us (6%)
  blocking collectives  124 us (5%)
  loops' own time  27 us (1%)
    while x120, local copies, waits for them, and re-layouts  700 us
    reshape x16, local copies, waits for them, and re-layouts, band(): return flat_taps.reshape(groups, length, double_len - 1)[:, :, :length]  224 us
    slice x16, local copies, waits for them, and re-layouts, band(): flat_taps = jnp.tile(flipped, (1, length))[:, :length * (double_len - 1)]  182 us
    reshape x8, local copies, waits for them, and re-layouts, band_back(): flat_taps = padded.reshape(groups, length * (2 * length - 1))  113 us
    reduce_sum x8, other arithmetic, band_back(): folded = jnp.sum(flat_taps.reshape(groups, length, 2 * length), axis=1)  98.3 us
    pad x8, local copies, waits for them, and re-layouts, band_back(): flat_taps = jnp.pad(flat_taps, ((0, 0), (0, length)))  90.7 us
    reduce_scatter x1, waiting for transfers between devices, body(): lax.psum_scatter((jnp.dot(grad_values, value_full.T, preferred_element_ty...  70.6 us
    reduce_scatter x1, waiting for transfers between devices, body(): lax.psum_scatter(jnp.dot(picked, mixout_full, preferred_element_type=jnp....  68.6 us
  transfers between devices with their start and end apart: 17, of which 12 were waited for; matrix products, arithmetic and copies ran while one was open for 46% of the time, Pallas kernels for 0%

commit v1 on v0

v1 whole, which is shorter than its diff:
```python
import functools

import jax
import jax.numpy as jnp
from jax import lax
from jax.experimental import pallas as pl
from jax.experimental.pallas import tpu as pltpu
from jax.sharding import PartitionSpec as P

epsilon = 1e-05
highest = lax.Precision.HIGHEST
BF = jnp.bfloat16
F32 = jnp.float32
BLOCK = 128
SENTENCE = 256


def build_band(taps_row, mask_ref, band_ref, length, reach):
    blocks = length // BLOCK
    low = length - (reach + 1) * BLOCK
    width = (2 * reach + 2) * BLOCK
    spread = jnp.broadcast_to(taps_row[:, low : low + width], (BLOCK, width))
    shifted = pltpu.roll(spread, 0, 1, stride=1, stride_axis=0).astype(BF)
    for i in range(blocks):
        first, last = max(0, i - reach), min(blocks, i + reach + 1)
        rows = slice(i * BLOCK, (i + 1) * BLOCK)
        columns = slice(first * BLOCK, last * BLOCK)
        offset = (first - i + reach + 1) * BLOCK
        band_ref[rows, columns] = (
            shifted[:, offset : offset + (last - first) * BLOCK] * mask_ref[rows, columns]
        )


def conv_forward_kernel(
    unroll, channels, reach, column_ref, row_ref, cond_ref, base_ref, shift_ref, values_ref,
    conv_ref, mask_ref, taps_ref, band_ref,
):
    length = row_ref.shape[1]
    filters = base_ref.shape[0]
    mask_ref[...] = (column_ref[...] == row_ref[...]).astype(BF)
    taps_ref[...] = base_ref[...].astype(F32) + cond_ref[...] * shift_ref[...].astype(F32)
    band_ref[...] = jnp.zeros_like(band_ref)

    def some(step, carry):
        for u in range(unroll):
            f = step * unroll + u
            build_band(taps_ref[pl.ds(f, 1), :], mask_ref, band_ref.at[u], length, reach)
            rows = pl.ds(pl.multiple_of(f * channels, channels), channels)
            conv_ref[rows, :] = jnp.dot(
                values_ref[rows, :], band_ref[u], preferred_element_type=F32
            )
        return carry

    lax.fori_loop(0, filters // unroll, some, 0)


def conv_forward(segments, cond, base, shift, values, unroll=8):
    filters, length = base.shape[0], segments.shape[0]
    channels = values.shape[0] // filters
    unroll = next(u for u in range(unroll, 0, -1) if filters % u == 0)
    vmem = pl.BlockSpec(memory_space=pltpu.VMEM)
    flops = 2 * values.shape[0] * length * length
    return pl.pallas_call(
        functools.partial(conv_forward_kernel, unroll, channels, SENTENCE // BLOCK),
        out_shape=jax.ShapeDtypeStruct(values.shape, F32),
        in_specs=[vmem] * 6,
        out_specs=vmem,
        scratch_shapes=[
            pltpu.VMEM((length, length), BF),
            pltpu.VMEM(base.shape, F32),
            pltpu.VMEM((unroll, length, length), BF),
        ],
        compiler_params=pltpu.CompilerParams(vmem_limit_bytes=40 << 20),
        cost_estimate=pl.CostEstimate(
            flops=flops * 16, bytes_accessed=values.size * 6, transcendentals=0
        ),
        name="conv_forward",
    )(segments[:, None], segments[None, :], cond[:, None], base, shift, values)


def conv_backward_kernel(
    unroll, channels, reach, column_ref, turned_ref, row_ref, cond_ref, base_ref, shift_ref,
    values_ref, grad_ref, grad_values_ref, grad_taps_ref, mask_ref, mask_turned_ref, taps_ref,
    band_ref, grad_turned_ref,
):
    length = row_ref.shape[1]
    filters = base_ref.shape[0]
    blocks = length // BLOCK
    mask_ref[...] = (column_ref[...] == row_ref[...]).astype(BF)
    mask_turned_ref[...] = (turned_ref[...] == row_ref[...]).astype(F32)
    taps_ref[...] = base_ref[...].astype(F32) + cond_ref[...] * shift_ref[...].astype(F32)
    band_ref[...] = jnp.zeros_like(band_ref)
    turn = (
        lax.broadcasted_iota(jnp.int32, (length, length), 0)
        + lax.broadcasted_iota(jnp.int32, (length, length), 1)
        == length - 1
    ).astype(BF)
    grad_turned_ref[...] = jnp.dot(grad_ref[...], turn, preferred_element_type=F32)

    def some(step, carry):
        for u in range(unroll):
            f = step * unroll + u
            build_band(taps_ref[pl.ds(f, 1), :], mask_ref, band_ref.at[u], length, reach)
            rows = pl.ds(pl.multiple_of(f * channels, channels), channels)
            grad_values_ref[rows, :] = jnp.dot(
                grad_ref[rows, :], band_ref[u], preferred_element_type=F32
            ).astype(BF)
            turned = grad_turned_ref[rows, :].T.astype(BF)
            product = jnp.dot(turned, values_ref[rows, :], preferred_element_type=F32)
            parts = [jnp.zeros((BLOCK, BLOCK), F32)] + [None] * (2 * reach + 1)
            for i in range(blocks):
                back = blocks - 1 - i
                for j in range(max(0, back - reach), min(blocks, back + reach + 1)):
                    here = (
                        slice(i * BLOCK, (i + 1) * BLOCK),
                        slice(j * BLOCK, (j + 1) * BLOCK),
                    )
                    block = product[here] * mask_turned_ref[here]
                    d = j - back + reach + 1
                    parts[d] = block if parts[d] is None else parts[d] + block
            aligned = pltpu.roll(jnp.concatenate(parts, axis=1), 0, 1, stride=1, stride_axis=0)
            grad_taps_ref[pl.ds(f, 1), :] = jnp.sum(aligned, axis=0, keepdims=True)
        return carry

    lax.fori_loop(0, filters // unroll, some, 0)


def conv_backward(segments, cond, base_turned, shift_turned, values, grad, unroll=4):
    filters, length = base_turned.shape[0], segments.shape[0]
    channels = values.shape[0] // filters
    reach = SENTENCE // BLOCK
    width = (2 * reach + 2) * BLOCK
    unroll = next(u for u in range(unroll, 0, -1) if filters % u == 0)
    vmem = pl.BlockSpec(memory_space=pltpu.VMEM)
    flops = 2 * values.shape[0] * length * length
    grad_values, grad_taps = pl.pallas_call(
        functools.partial(conv_backward_kernel, unroll, channels, reach),
        out_shape=(
            jax.ShapeDtypeStruct(values.shape, BF),
            jax.ShapeDtypeStruct((filters, width), F32),
        ),
        in_specs=[vmem] * 8,
        out_specs=(vmem, vmem),
        scratch_shapes=[
            pltpu.VMEM((length, length), BF),
            pltpu.VMEM((length, length), F32),
            pltpu.VMEM(base_turned.shape, F32),
            pltpu.VMEM((unroll, length, length), BF),
            pltpu.VMEM(values.shape, F32),
        ],
        compiler_params=pltpu.CompilerParams(vmem_limit_bytes=48 << 20),
        cost_estimate=pl.CostEstimate(
            flops=flops * 32, bytes_accessed=values.size * 6, transcendentals=0
        ),
        name="conv_backward",
    )(
        segments[:, None],
        segments[::-1][:, None],
        segments[None, :],
        cond[:, None],
        base_turned,
        shift_turned,
        values,
        grad,
    )
    lags = jnp.roll(grad_taps, -(BLOCK - 1), axis=1)[:, ::-1]
    start = length + (reach + 1) * BLOCK - (width - 1)
    full = jnp.pad(lags, ((0, 0), (start, 2 * length - start - width + 1)))
    return grad_values, full[:, : 2 * length]


def swap(value, axis, mask):
    return lax.ppermute(value, axis, [(i, i ^ mask) for i in range(lax.axis_size(axis))])


def bits_of(count):
    return [1 << b for b in range(count.bit_length() - 1)]


def gather_dp(block):
    bits = bits_of(lax.axis_size("dp"))
    half = block.shape[1] // 2
    found = []
    for part, order in ((block[:, :half], bits), (block[:, half:], bits[::-1])):
        held, masks = part[None], [0]
        for bit in order:
            held = jnp.concatenate([held, swap(held, "dp", bit)], axis=0)
            masks = masks + [m | bit for m in masks]
        found.append({m: held[i] for i, m in enumerate(masks)})
    return [jnp.concatenate([f[m] for f in found], axis=1) for m in range(lax.axis_size("dp"))]


def natural(pieces, me):
    held = jnp.stack(pieces)
    return jnp.concatenate(
        [lax.dynamic_index_in_dim(held, j ^ me, 0, keepdims=False) for j in range(len(pieces))],
        axis=1,
    )


def scatter_dp(pieces):
    bits = bits_of(lax.axis_size("dp"))
    half = pieces[0].shape[1] // 2
    done = []
    for part, order in ((slice(None, half), bits[::-1]), (slice(half, None), bits)):
        held = {m: p[:, part] for m, p in enumerate(pieces)}
        for bit in order:
            stay = [m for m in held if not m & bit]
            got = swap(jnp.stack([held[m | bit] for m in stay]), "dp", bit)
            held = {m: held[m] + got[i] for i, m in enumerate(stay)}
        done.append(held[0])
    return jnp.concatenate(done, axis=1)


def everywhere(value):
    for bit in bits_of(lax.axis_size("mp")):
        value = value + swap(value, "mp", bit)
    for bit in bits_of(lax.axis_size("dp")):
        value = value + swap(value, "dp", bit)
    return value


def statistics(value):
    centred = value - jnp.mean(value, axis=-1, keepdims=True)
    scale = lax.rsqrt(jnp.mean(centred * centred, axis=-1, keepdims=True) + epsilon)
    return centred * scale, scale


def normalize_back(normal, scale, gain, grad):
    scaled = grad * gain
    return scale * (
        scaled
        - jnp.mean(scaled, axis=-1, keepdims=True)
        - normal * jnp.mean(scaled * normal, axis=-1, keepdims=True)
    )


def mm(left, right, dims):
    return lax.dot_general(left, right, (dims, ((), ())), preferred_element_type=F32)


def body(
    tokens, segment_ids, gain_one, gain_two, value_weight, mixgate_weight, condition_weight,
    filter_base, filter_shift, mixout_weight, gate_weight, up_weight, down_weight, output_grad,
):
    dp_size, mp_size = lax.axis_size("dp"), lax.axis_size("mp")
    dp, mp = lax.axis_index("dp"), lax.axis_index("mp")
    core = mp & 1
    chips = mp_size // 2
    local, width = tokens.shape
    length = segment_ids.shape[1]
    whole_rows = local % length == 0
    total = 2 * local
    rows = total // length

    def pair(own, other):
        if whole_rows:
            return jnp.concatenate([own, other], axis=0)
        first = core == 0
        return jnp.concatenate([jnp.where(first, own, other), jnp.where(first, other, own)], axis=0)

    def mine(value):
        return value[:local] if whole_rows else lax.dynamic_slice_in_dim(value, core * local, local)

    def others(value):
        if whole_rows:
            return value[local:]
        return lax.dynamic_slice_in_dim(value, (1 - core) * local, local)

    def pair_sum(value):
        got = swap(value, "mp", 1)
        if whole_rows:
            got = jnp.concatenate([got[local:], got[:local]], axis=0)
        return value.astype(F32) + got.astype(F32)

    def pair_scatter(value):
        return mine(value) + swap(others(value).astype(BF), "mp", 1).astype(F32)

    block_c = value_weight.shape[1]
    block_g = condition_weight.shape[1]
    block_f = gate_weight.shape[1]
    taps = filter_base.shape[1]
    mixer_pack = jnp.stack([value_weight, mixgate_weight, mixout_weight.T])
    filter_pack = jnp.stack([filter_base.T, filter_shift.T])
    ffn_pack = jnp.stack([gate_weight, up_weight, down_weight.T])

    tokens_all = pair(tokens, swap(tokens, "mp", 1))
    grad_all = pair(output_grad, swap(output_grad, "mp", 1))
    if whole_rows:
        per = local // length
        seg_rows = jnp.concatenate(
            [
                lax.dynamic_slice_in_dim(segment_ids, mp * per, per),
                lax.dynamic_slice_in_dim(segment_ids, (mp ^ 1) * per, per),
            ]
        )
    else:
        seg_rows = lax.dynamic_slice_in_dim(segment_ids, (mp // 2) * rows, rows)

    def gather(block):
        found = [block] + [swap(block, "mp", 2 * k) for k in range(1, chips)]
        return [natural(gather_dp(b), dp) for b in found]

    mixer = jnp.concatenate(gather(mixer_pack), axis=2)
    small = jnp.concatenate(gather(jnp.pad(condition_weight, ((0, 0), (0, 0)))[None]), axis=2)[0]
    filters = jnp.concatenate(gather(filter_pack), axis=2)
    ffn = gather(ffn_pack)
    value_full, mixgate_full, mixout_full = mixer
    base, shift = jnp.swapaxes(filters, 1, 2)
    base_turned = jnp.roll(base[:, ::-1], 1, axis=1)
    shift_turned = jnp.roll(shift[:, ::-1], 1, axis=1)

    xf = tokens_all.astype(F32)
    normal_one, scale_one = statistics(xf)
    normed_one = (normal_one * gain_one).astype(BF)
    values = mm(value_full, normed_one, ((0,), (1,))).astype(BF)
    gates = mm(mixgate_full, normed_one, ((0,), (1,)))
    summary = jnp.mean(normed_one.astype(F32).reshape(rows, length, width), axis=1)
    condition = small.astype(F32)
    cond = jnp.tanh(jnp.dot(summary, condition, precision=highest))
    cuts = [slice(r * length, (r + 1) * length) for r in range(rows)]
    conv = jnp.concatenate(
        [conv_forward(seg_rows[r], cond[r], base, shift, values[:, cuts[r]]) for r in range(rows)],
        axis=1,
    )
    mixed = (conv * gates).astype(BF)
    branch = pair_sum(mm(mixed, mixout_full, ((0,), (1,))).astype(BF))
    middle = xf + branch
    normal_two, scale_two = statistics(middle)
    normed_two = (normal_two * gain_two).astype(BF)

    feed = jnp.zeros((total, width), F32)
    grad_two = jnp.zeros((total, width), F32)
    ffn_grads = []
    for k in range(chips):
        gate_full, up_full, down_full = ffn[k]
        gate_pre = mm(normed_two, gate_full, ((1,), (0,)))
        up_pre = mm(normed_two, up_full, ((1,), (0,)))
        grad_hidden = mm(grad_all, down_full, ((1,), (0,)))
        sigmoid = jax.nn.sigmoid(gate_pre)
        silu = gate_pre * sigmoid
        hidden = (silu * up_pre).astype(BF)
        grad_gate = (grad_hidden * up_pre * (sigmoid + silu * (1.0 - sigmoid))).astype(BF)
        grad_up = (grad_hidden * silu).astype(BF)
        feed = feed + mm(hidden, down_full, ((1,), (1,)))
        grad_two = (
            grad_two + mm(grad_gate, gate_full, ((1,), (1,))) + mm(grad_up, up_full, ((1,), (1,)))
        )
        ffn_grads.append(
            jnp.stack(
                [
                    mm(normed_two, grad_gate, ((0,), (0,))).astype(BF),
                    mm(normed_two, grad_up, ((0,), (0,))).astype(BF),
                    mm(grad_all, hidden, ((0,), (0,))).astype(BF),
                ]
            )
        )

    def scatter(grads):
        sums = None
        for k, grad in enumerate(grads):
            size = grad.shape[1] // dp_size
            pieces = [
                lax.dynamic_slice_in_dim(grad, (dp ^ m) * size, size, axis=1)
                for m in range(dp_size)
            ]
            part = scatter_dp(pieces)
            part = part if k == 0 else swap(part, "mp", 2 * k)
            sums = part.astype(F32) if sums is None else sums + part.astype(F32)
        return sums

    gate_sum, up_sum, down_sum = scatter(ffn_grads)
    output = (mine(middle) + pair_scatter(feed)).astype(BF)

    grad_normed_two = pair_sum(grad_two.astype(BF))
    gain_two_part = jnp.sum(mine(grad_normed_two * normal_two), axis=0)
    grad_middle = grad_all.astype(F32) + normalize_back(
        normal_two, scale_two, gain_two, grad_normed_two
    )
    grad_branch = grad_middle.astype(BF)

    mixout_grad = mm(grad_branch, mixed, ((0,), (1,)))
    grad_mixed = mm(mixout_full, grad_branch, ((0,), (1,)))
    grad_conv = (grad_mixed * gates).astype(BF)
    grad_gates = (grad_mixed * conv).astype(BF)
    backs = [
        conv_backward(
            seg_rows[r], cond[r], base_turned, shift_turned, values[:, cuts[r]],
            grad_conv[:, cuts[r]],
        )
        for r in range(rows)
    ]
    grad_values = jnp.concatenate([b[0] for b in backs], axis=1)
    grad_taps = jnp.stack([b[1] for b in backs])
    base_grad = jnp.sum(grad_taps, axis=0)
    shift_grad = jnp.sum(grad_taps * cond[:, :, None], axis=0)
    grad_cond = jnp.sum(grad_taps * shift.astype(F32)[None], axis=2) * (1.0 - cond * cond)
    condition_grad = mm(summary, grad_cond, ((0,), (0,)))
    grad_summary = jnp.dot(grad_cond, condition.T, precision=highest) / length
    value_grad = mm(normed_one, grad_values, ((0,), (1,)))
    mixgate_grad = mm(normed_one, grad_gates, ((0,), (1,)))
    grad_one = mm(grad_values, value_full, ((0,), (1,))) + mm(
        grad_gates, mixgate_full, ((0,), (1,))
    )
    grad_one = (grad_one.reshape(rows, length, width) + grad_summary[:, None, :]).reshape(
        total, width
    )
    grad_normed_one = pair_scatter(grad_one)
    input_grad = (
        mine(grad_middle)
        + normalize_back(mine(normal_one), mine(scale_one), gain_one, grad_normed_one)
    ).astype(BF)
    gain_one_part = jnp.sum(grad_normed_one * mine(normal_one), axis=0)
    gain_one_grad, gain_two_grad = everywhere(jnp.stack([gain_one_part, gain_two_part]))

    def split(grad, size):
        return [grad[..., k * size : (k + 1) * size].astype(BF) for k in range(chips)]

    value_sum, mixgate_sum, mixout_sum = scatter(
        split(jnp.stack([value_grad, mixgate_grad, mixout_grad]), block_c)
    )
    condition_sum = scatter(split(condition_grad[None], block_g))[0]
    base_sum, shift_sum = scatter(
        split(jnp.swapaxes(jnp.stack([base_grad, shift_grad]), 1, 2), block_g)
    )
    return (
        output, input_grad, gain_one_grad, gain_two_grad, value_sum, mixgate_sum, condition_sum,
        base_sum.T, shift_sum.T, mixout_sum.T, gate_sum, up_sum, down_sum.T,
    )


def solution(mesh):
    sides = P(("dp", "mp"), None)
    columns, rows = P("dp", "mp"), P("mp", "dp")
    in_specs = (
        sides, P("dp", None), P(), P(), columns, columns, columns, rows, rows, rows, columns,
        columns, rows, sides,
    )
    out_specs = (
        sides, sides, P(), P(), columns, columns, columns, rows, rows, rows, columns, columns, rows,
    )
    return jax.shard_map(body, mesh=mesh, in_specs=in_specs, out_specs=out_specs, check_vma=False)
```

time: 2470 us -> 678 us (0.27)
  local copies, waits for them, and re-layouts: 1450 us -> 55.6 us
  waiting for transfers between devices: 502 us -> 260 us
  starting transfers between devices: 1.08 us -> 151 us
  blocking collectives: 124 us -> 0 us
  matrix products: 197 us -> 77.9 us
  other arithmetic: 142 us -> 99.6 us
  loops' own time: 27 us -> 0 us
    while x120 -> x0, local copies, waits for them, and re-layouts: 700 us -> none
    reduce_scatter x11 -> x0, waiting for transfers between devices: 343 us -> none  [the longest x1 70.6 us: body(): lax.psum_scatter((jnp.dot(grad_values, value_full.T, preferred_element_ty...]
    reshape x27 -> x1, local copies, waits for them, and re-layouts: 337 us -> 2.38 us  [body(): grad_one.reshape(rows, length, width) + grad_summary[:, None, :]]
    ppermute x0 -> x163, waiting for transfers between devices: none -> 260 us  [swap(): lax.ppermute(value, axis, [(i, i ^ mask) for i in range(lax.axis_size(axi...]
    slice x64 -> x18, local copies, waits for them, and re-layouts: 184 us -> 3.34 us  [the longest x2 1.73 us: pair_sum(): got = jnp.concatenate([got[local:], got[:local]], axis=0)]
    ppermute x0 -> x163, starting transfers between devices: none -> 151 us  [swap(): lax.ppermute(value, axis, [(i, i ^ mask) for i in range(lax.axis_size(axi...]
    pad x16 -> x0, local copies, waits for them, and re-layouts: 139 us -> none  [the longest x8 90.7 us: band_back(): flat_taps = jnp.pad(flat_taps, ((0, 0), (0, length)))]
    all_gather x4 -> x0, waiting for transfers between devices: 133 us -> none  [the longest x1 50.1 us: body(): grad_rows = lax.all_gather(output_grad, 'mp', axis=0, tiled=True)]
  transfers between devices with their start and end apart: 17 -> 163, of which waited for: 12 -> 98; matrix products, arithmetic and copies ran while one was open for 46% -> 28% of each run, Pallas kernels for 0% -> 3%
where the time goes in v1:
time: 678 us; the launch traced here: 671 us
  waiting for transfers between devices  260 us (38%)
  starting transfers between devices  151 us (22%)
  other arithmetic  99.6 us (15%)
  matrix products  77.9 us (11%)
  local copies, waits for them, and re-layouts  55.6 us (8%)
  Pallas kernels  22.7 us (3%)
    ppermute x163, waiting for transfers between devices, swap(): lax.ppermute(value, axis, [(i, i ^ mask) for i in range(lax.axis_size(axi...  260 us
    ppermute x163, starting transfers between devices, swap(): lax.ppermute(value, axis, [(i, i ^ mask) for i in range(lax.axis_size(axi...  151 us
    dot_general x46, matrix products, mm(): lax.dot_general(left, right, (dims, ((), ())), preferred_element_type=F32)  77.1 us
    another operation x64, other arithmetic, scatter_dp(): got = swap(jnp.stack([held[m | bit] for m in stay]), 'dp', bit)  21.6 us
    unnamed x287, local copies, waits for them, and re-layouts  20.7 us
    add x32, other arithmetic, scatter_dp(): held = {m: held[m] + got[i] for i, m in enumerate(stay)}  16.5 us
    pallas_call x2, Pallas kernels, conv_backward(): pl.pallas_call(functools.partial(conv_backward_kernel, unroll, channels,...  16.4 us
  transfers between devices with their start and end apart: 163, of which 98 were waited for; matrix products, arithmetic and copies ran while one was open for 28% of the time, Pallas kernels for 3%

profile of v1, /device:TPU:0, one launch (start us, length us, event | category | flops | bytes accessed | tf_op | source)
XLA Modules:
  0.0 671.1 jit_solution(12526560644875580383)
XLA Ops:
  0.6 4.1 collective-permute-start.10
  29.4 3.0 collective-permute-done.20
  32.9 3.1 collective-permute-done.21
  36.5 3.1 collective-permute-done.3
  40.2 3.0 collective-permute-done.4
  47.3 3.1 collective-permute-done.12
  50.9 3.0 collective-permute-done.6
  54.5 3.1 collective-permute-done.7
  58.1 3.0 collective-permute-done.16
  61.7 3.1 collective-permute-done.17
  65.3 3.1 collective-permute-done.13
  68.9 3.0 collective-permute-done.14
  76.1 3.0 collective-permute-done.9
  83.4 3.0 collective-permute-done.19
  91.4 3.1 collective-permute-done.22
  95.0 3.1 collective-permute-done.23
  98.7 3.0 collective-permute-done.30
  102.3 3.1 collective-permute-done.31
  105.9 3.1 collective-permute-done.35
  109.5 3.1 collective-permute-done.36
  113.1 3.1 collective-permute-done.25
  116.7 3.1 collective-permute-done.26
  120.4 3.1 collective-permute-done.32
  124.0 3.1 collective-permute-done.33
  127.7 3.1 collective-permute-done.37
  131.3 3.1 collective-permute-done.38
  135.0 3.0 collective-permute-done.27
  138.6 3.1 collective-permute-done.28
  146.6 4.4 collective-permute-done.40
  156.9 5.2 collective-permute-done.41
  162.7 4.5 collective-permute-done.42
  172.1 3.8 collective-permute-done.45
  177.1 3.1 collective-permute-done.49
  180.8 3.8 collective-permute-done.50
  185.8 3.1 collective-permute-done.54
  189.5 3.8 collective-permute-done.55
  194.1 5.4 collective-permute-done.60
  201.7 3.0 collective-permute-done.46
  205.3 4.5 collective-permute-done.47
  211.5 4.7 collective-permute-done.51
  216.3 5.8 collective-permute-done.52
  223.5 3.7 collective-permute-done.56
  227.9 4.5 collective-permute-done.57
  233.0 3.1 maximum_maximum_fusion
  240.0 9.1 %collective-permute-done.61 = bf16[2,3,96,384]{3,2,1,0:T(8,128)(2,1)S(1)} collective-permute-done((bf16[2,3,96,384]{3,2,1,0:T(8,128)(2,1)S(1)}, bf16[2,3,96,384]{3,2,1,0:T(8,128)(2,1)S(1)}, u32[]{:S(2)}, u32[]{:S(2)}) %collective-permute-start.61) | collective-permute-done | bytes 442400 | tf_op jit(solution)/shard_map/ppermute | solution.py:173
  277.8 5.6 reshape.157
  283.4 5.7 convert_reduce_fusion
  290.3 2.9 conv_forward.3
  293.3 3.3 conv_forward.2
  355.7 3.8 multiply_convert_fusion.5
  390.7 5.5 add_convert_fusion
  402.5 3.4 collective-permute-done.144
  431.8 7.5 %collective-permute-done.155 = bf16[2,3,96,384]{3,2,1,0:T(8,128)(2,1)} collective-permute-done((bf16[2,3,96,384]{3,2,1,0:T(8,128)(2,1)}, bf16[2,3,96,384]{3,2,1,0:T(8,128)(2,1)}, u32[]{:S(2)}, u32[]{:S(2)}) %collective-permute-start.155) | collective-permute-done | bytes 442400 | tf_op jit(solution)/shard_map/ppermute | solution.py:173
  441.3 7.5 %collective-permute-done.150 = bf16[2,3,96,384]{3,2,1,0:T(8,128)(2,1)} collective-permute-done((bf16[2,3,96,384]{3,2,1,0:T(8,128)(2,1)}, bf16[2,3,96,384]{3,2,1,0:T(8,128)(2,1)}, u32[]{:S(2)}, u32[]{:S(2)}) %collective-permute-start.150) | collective-permute-done | bytes 442400 | tf_op jit(solution)/shard_map/ppermute | solution.py:173
  450.8 6.6 collective-permute-done.146
  472.4 3.8 multiply_reduce_fusion.3
  476.2 2.9 multiply_add_fusion
  484.7 8.2 %conv_backward.2 = (bf16[384,512]{1,0:T(8,128)(2,1)S(1)}, f32[24,768]{1,0:T(8,128)S(1)}) custom-call(s32[512,1]{1,0:T(8,128)S(1)} %copy.75.column_ref, s32[512,1]{1,0:T(8,128)S(1)} %copy.86.turned_ref, s32[1,512]{1,0:T(1,128)S(1)} %copy-done.5, f32[24,1]{1,0:T(8,128)S(1)} %copy-done.9, bf16[24,1024]{1,0:T(8,128)(2,1)S(1)} %copy-done, ...), custom_call_target="tpu_custom_call" | custom-call | flops 6442450944 | bytes 1179648 | tf_op jit(solution)/shard_map/conv_backward/pallas_call | solution.py:136
  493.1 8.2 %conv_backward.3 = (bf16[384,512]{1,0:T(8,128)(2,1)S(1)}, f32[24,768]{1,0:T(8,128)S(1)}) custom-call(s32[512,1]{1,0:T(8,128)S(1)} %copy.77.column_ref, s32[512,1]{1,0:T(8,128)S(1)} %copy.89.turned_ref, s32[1,512]{1,0:T(1,128)S(1)} %copy-done.2, f32[24,1]{1,0:T(8,128)S(1)} %copy-done.7, bf16[24,1024]{1,0:T(8,128)(2,1)S(1)} %copy-done, ...), custom_call_target="tpu_custom_call" | custom-call | flops 6442450944 | bytes 1179648 | tf_op jit(solution)/shard_map/conv_backward/pallas_call | solution.py:136
  611.2 3.1 collective-permute-done.92
  615.6 3.7 collective-permute-done.97
  620.5 3.1 collective-permute-done.102
  624.9 4.0 collective-permute-done.88
  664.5 3.5 fusion.2
  (977 shorter events, 411.7 us)
Async XLA Ops:
  0.6 25.9 %collective-permute-start.10 = (bf16[1,192,6]{1,2,0:T(8,128)(2,1)}, bf16[1,192,6]{1,2,0:T(8,128)(2,1)S(1)}, u32[]{:S(2)}, u32[]{:S(2)}) collective-permute-start(bf16[1,192,6]{1,2,0:T(8,128)(2,1)} %bitcast.1336), channel_id=1, source_target_pairs={{0,4},{1,5},{2,6},{3,7},{4,0},{5,1},{6,2},{7,3},{8,12},{9,13},{10,... | collective-permute-start | bytes 6920 | tf_op jit(solution)/shard_map/ppermute | solution.py:173
  4.7 22.5 %collective-permute-start.5 = (bf16[1,192,6]{1,2,0:T(8,128)(2,1)}, bf16[1,192,6]{1,2,0:T(8,128)(2,1)S(1)}, u32[]{:S(2)}, u32[]{:S(2)}) collective-permute-start(bf16[1,192,6]{1,2,0:T(8,128)(2,1)} %bitcast.1337), channel_id=1, source_target_pairs={{0,2},{1,3},{2,0},{3,1},{4,6},{5,7},{6,4},{7,5},{8,10},{9,11},{10,... | collective-permute-start | bytes 6920 | tf_op jit(solution)/shard_map/ppermute | solution.py:173
  6.3 22.5 %collective-permute-start.15 = (bf16[1,192,6]{1,2,0:T(8,128)(2,1)}, bf16[1,192,6]{1,2,0:T(8,128)(2,1)S(1)}, u32[]{:S(2)}, u32[]{:S(2)}) collective-permute-start(bf16[1,192,6]{1,2,0:T(8,128)(2,1)} %bitcast.1338), channel_id=1, source_target_pairs={{0,6},{1,7},{2,4},{3,5},{4,2},{5,3},{6,0},{7,1},{8,14},{9,15},{10,... | collective-permute-start | bytes 6920 | tf_op jit(solution)/shard_map/ppermute | solution.py:173
  7.2 15.6 %collective-permute-start.1 = (bf16[1,1,96,6]{2,3,1,0:T(8,128)(2,1)S(1)}, bf16[1,1,96,6]{2,3,1,0:T(8,128)(2,1)S(1)}, u32[]{:S(2)}, u32[]{:S(2)}) collective-permute-start(bf16[1,1,96,6]{2,3,1,0:T(8,128)(2,1)S(1)} %get-tuple-element.348), channel_id=1, source_target_pairs={{0,8},{8,0},{16,24},{24,16},{1,9},{9,1},{17,25},{25,17},{2,10},{10... | collective-permute-start | bytes 3464 | tf_op jit(solution)/shard_map/ppermute | solution.py:173
  8.9 15.7 %collective-permute-start.2 = (bf16[1,1,96,6]{2,3,1,0:T(8,128)(2,1)S(1)}, bf16[1,1,96,6]{2,3,1,0:T(8,128)(2,1)S(1)}, u32[]{:S(2)}, u32[]{:S(2)}) collective-permute-start(bf16[1,1,96,6]{2,3,1,0:T(8,128)(2,1)S(1)} %get-tuple-element.349), channel_id=1, source_target_pairs={{0,16},{8,24},{16,0},{24,8},{1,17},{9,25},{17,1},{25,9},{2,18},{10... | collective-permute-start | bytes 3464 | tf_op jit(solution)/shard_map/ppermute | solution.py:173
  22.8 66.6 %collective-permute-start.29 = (bf16[2,256,6]{1,2,0:T(8,128)(2,1)S(1)}, bf16[2,256,6]{1,2,0:T(8,128)(2,1)S(1)}, u32[]{:S(2)}, u32[]{:S(2)}) collective-permute-start(bf16[2,256,6]{1,2,0:T(8,128)(2,1)S(1)} %get-tuple-element.319), channel_id=1, source_target_pairs={{0,4},{1,5},{2,6},{3,7},{4,0},{5,1},{6,2},{7,3},{8,12},{9,13},{10,... | collective-permute-start | bytes 18440 | tf_op jit(solution)/shard_map/ppermute | solution.py:173
  24.5 65.8 %collective-permute-start.34 = (bf16[2,256,6]{1,2,0:T(8,128)(2,1)S(1)}, bf16[2,256,6]{1,2,0:T(8,128)(2,1)S(1)}, u32[]{:S(2)}, u32[]{:S(2)}) collective-permute-start(bf16[2,256,6]{1,2,0:T(8,128)(2,1)S(1)} %get-tuple-element.319), channel_id=1, source_target_pairs={{0,6},{1,7},{2,4},{3,5},{4,2},{5,3},{6,0},{7,1},{8,14},{9,15},{10,... | collective-permute-start | bytes 18440 | tf_op jit(solution)/shard_map/ppermute | solution.py:173
  26.5 64.3 %collective-permute-start.24 = (bf16[2,256,6]{1,2,0:T(8,128)(2,1)S(1)}, bf16[2,256,6]{1,2,0:T(8,128)(2,1)S(1)}, u32[]{:S(2)}, u32[]{:S(2)}) collective-permute-start(bf16[2,256,6]{1,2,0:T(8,128)(2,1)S(1)} %get-tuple-element.319), channel_id=1, source_target_pairs={{0,2},{1,3},{2,0},{3,1},{4,6},{5,7},{6,4},{7,5},{8,10},{9,11},{10,... | collective-permute-start | bytes 18440 | tf_op jit(solution)/shard_map/ppermute | solution.py:173
  27.2 126.1 %collective-permute-start.43 = (bf16[3,192,96]{1,2,0:T(8,128)(2,1)S(1)}, bf16[3,192,96]{1,2,0:T(8,128)(2,1)S(1)}, u32[]{:S(2)}, u32[]{:S(2)}) collective-permute-start(bf16[3,192,96]{1,2,0:T(8,128)(2,1)S(1)} %get-tuple-element.206), channel_id=1, source_target_pairs={{0,2},{1,3},{2,0},{3,1},{4,6},{5,7},{6,4},{7,5},{8,10},{9,11},{10,... | collective-permute-start | bytes 331784 | tf_op jit(solution)/shard_map/ppermute | solution.py:173
  86.4 68.1 %collective-permute-start.48 = (bf16[3,192,96]{1,2,0:T(8,128)(2,1)S(1)}, bf16[3,192,96]{1,2,0:T(8,128)(2,1)S(1)}, u32[]{:S(2)}, u32[]{:S(2)}) collective-permute-start(bf16[3,192,96]{1,2,0:T(8,128)(2,1)S(1)} %get-tuple-element.206), channel_id=1, source_target_pairs={{0,4},{1,5},{2,6},{3,7},{4,0},{5,1},{6,2},{7,3},{8,12},{9,13},{10,... | collective-permute-start | bytes 331784 | tf_op jit(solution)/shard_map/ppermute | solution.py:173
  89.4 66.5 %collective-permute-start.53 = (bf16[3,192,96]{1,2,0:T(8,128)(2,1)S(1)}, bf16[3,192,96]{1,2,0:T(8,128)(2,1)S(1)}, u32[]{:S(2)}, u32[]{:S(2)}) collective-permute-start(bf16[3,192,96]{1,2,0:T(8,128)(2,1)S(1)} %get-tuple-element.206), channel_id=1, source_target_pairs={{0,6},{1,7},{2,4},{3,5},{4,2},{5,3},{6,0},{7,1},{8,14},{9,15},{10,... | collective-permute-start | bytes 331784 | tf_op jit(solution)/shard_map/ppermute | solution.py:173
  90.3 145.8 %collective-permute-start.63 = (bf16[3,192,384]{2,1,0:T(8,128)(2,1)}, bf16[3,192,384]{2,1,0:T(8,128)(2,1)}, u32[]{:S(2)}, u32[]{:S(2)}) collective-permute-start(bf16[3,192,384]{2,1,0:T(8,128)(2,1)} %get-tuple-element.189), channel_id=1, source_target_pairs={{0,2},{1,3},{2,0},{3,1},{4,6},{5,7},{6,4},{7,5},{8,10},{9,11},{10,... | collective-permute-start | bytes 1327112 | tf_op jit(solution)/shard_map/ppermute | solution.py:173
  151.0 87.3 %collective-permute-start.68 = (bf16[3,192,384]{2,1,0:T(8,128)(2,1)}, bf16[3,192,384]{2,1,0:T(8,128)(2,1)S(1)}, u32[]{:S(2)}, u32[]{:S(2)}) collective-permute-start(bf16[3,192,384]{2,1,0:T(8,128)(2,1)} %get-tuple-element.189), channel_id=1, source_target_pairs={{0,4},{1,5},{2,6},{3,7},{4,0},{5,1},{6,2},{7,3},{8,12},{9,13},{10,... | collective-permute-start | bytes 1327112 | tf_op jit(solution)/shard_map/ppermute | solution.py:173
  153.4 85.6 %collective-permute-start.73 = (bf16[3,192,384]{2,1,0:T(8,128)(2,1)}, bf16[3,192,384]{2,1,0:T(8,128)(2,1)S(1)}, u32[]{:S(2)}, u32[]{:S(2)}) collective-permute-start(bf16[3,192,384]{2,1,0:T(8,128)(2,1)} %get-tuple-element.189), channel_id=1, source_target_pairs={{0,6},{1,7},{2,4},{3,5},{4,2},{5,3},{6,0},{7,1},{8,14},{9,15},{10,... | collective-permute-start | bytes 1327112 | tf_op jit(solution)/shard_map/ppermute | solution.py:173
  154.5 39.4 %collective-permute-start.59 = (bf16[1,3,96,384]{3,2,1,0:T(8,128)(2,1)S(1)}, bf16[1,3,96,384]{3,2,1,0:T(8,128)(2,1)S(1)}, u32[]{:S(2)}, u32[]{:S(2)}) collective-permute-start(bf16[1,3,96,384]{3,2,1,0:T(8,128)(2,1)S(1)} %get-tuple-element.194), channel_id=1, source_target_pairs={{0,8},{8,0},{16,24},{24,16},{1,9},{9,1},{17,25},{25,17},{2,10},{10... | collective-permute-start | bytes 663560 | tf_op jit(solution)/shard_map/ppermute | solution.py:173
  193.9 75.5 %collective-permute-start = (bf16[512,768]{0,1:T(8,128)(2,1)S(1)}, bf16[512,768]{0,1:T(8,128)(2,1)S(1)}, u32[]{:S(2)}, u32[]{:S(2)}) collective-permute-start(bf16[512,768]{0,1:T(8,128)(2,1)S(1)} %copy.71), channel_id=1, source_target_pairs={{0,1},{1,0},{2,3},{3,2},{4,5},{5,4},{6,7},{7,6},{8,9},{9,8},{10,11... | collective-permute-start | bytes 2359304 | tf_op jit(solution)/shard_map/ppermute | solution.py:173
  232.4 100.4 %collective-permute-start.79 = (bf16[512,768]{0,1:T(8,128)(2,1)}, bf16[512,768]{0,1:T(8,128)(2,1)}, u32[]{:S(2)}, u32[]{:S(2)}) collective-permute-start(bf16[512,768]{0,1:T(8,128)(2,1)} %copy.84), channel_id=1, source_target_pairs={{0,1},{1,0},{2,3},{3,2},{4,5},{5,4},{6,7},{7,6},{8,9},{9,8},{10,11... | collective-permute-start | bytes 2359304 | tf_op jit(solution)/shard_map/ppermute | solution.py:173
  236.1 13.0 %collective-permute-start.61 = (bf16[2,3,96,384]{3,2,1,0:T(8,128)(2,1)S(1)}, bf16[2,3,96,384]{3,2,1,0:T(8,128)(2,1)S(1)}, u32[]{:S(2)}, u32[]{:S(2)}) collective-permute-start(bf16[2,3,96,384]{3,2,1,0:T(8,128)(2,1)S(1)} %pad_maximum_fusion.20), channel_id=1, source_target_pairs={{0,8},{8,0},{16,24},{24,16},{1,9},{9,1},{17,25},{25,17},{2,10},{10... | collective-permute-start | bytes 1327112 | tf_op jit(solution)/shard_map/ppermute | solution.py:173
  238.4 12.4 %collective-permute-start.62 = (bf16[2,3,96,384]{3,2,1,0:T(8,128)(2,1)S(1)}, bf16[2,3,96,384]{3,2,1,0:T(8,128)(2,1)S(1)}, u32[]{:S(2)}, u32[]{:S(2)}) collective-permute-start(bf16[2,3,96,384]{3,2,1,0:T(8,128)(2,1)S(1)} %pad_maximum_fusion.21), channel_id=1, source_target_pairs={{0,16},{8,24},{16,0},{24,8},{1,17},{9,25},{17,1},{25,9},{2,18},{10... | collective-permute-start | bytes 1327112 | tf_op jit(solution)/shard_map/ppermute | solution.py:173
  239.0 14.8 %collective-permute-start.64 = (bf16[1,3,96,384]{3,2,1,0:T(8,128)(2,1)S(1)}, bf16[1,3,96,384]{3,2,1,0:T(8,128)(2,1)S(1)}, u32[]{:S(2)}, u32[]{:S(2)}) collective-permute-start(bf16[1,3,96,384]{3,2,1,0:T(8,128)(2,1)S(1)} %get-tuple-element.186), channel_id=1, source_target_pairs={{0,8},{8,0},{16,24},{24,16},{1,9},{9,1},{17,25},{25,17},{2,10},{10... | collective-permute-start | bytes 663560 | tf_op jit(solution)/shard_map/ppermute | solution.py:173
  249.1 6.7 collective-permute-start.65
  250.7 8.4 %collective-permute-start.69 = (bf16[1,3,96,384]{3,2,1,0:T(8,128)(2,1)S(1)}, bf16[1,3,96,384]{3,2,1,0:T(8,128)(2,1)S(1)}, u32[]{:S(2)}, u32[]{:S(2)}) collective-permute-start(bf16[1,3,96,384]{3,2,1,0:T(8,128)(2,1)S(1)} %get-tuple-element.200), channel_id=1, source_target_pairs={{0,8},{8,0},{16,24},{24,16},{1,9},{9,1},{17,25},{25,17},{2,10},{10... | collective-permute-start | bytes 663560 | tf_op jit(solution)/shard_map/ppermute | solution.py:173
  253.8 7.1 %collective-permute-start.70 = (bf16[1,3,96,384]{3,2,1,0:T(8,128)(2,1)S(1)}, bf16[1,3,96,384]{3,2,1,0:T(8,128)(2,1)S(1)}, u32[]{:S(2)}, u32[]{:S(2)}) collective-permute-start(bf16[1,3,96,384]{3,2,1,0:T(8,128)(2,1)S(1)} %get-tuple-element.201), channel_id=1, source_target_pairs={{0,16},{8,24},{16,0},{24,8},{1,17},{9,25},{17,1},{25,9},{2,18},{10... | collective-permute-start | bytes 663560 | tf_op jit(solution)/shard_map/ppermute | solution.py:173
  255.7 8.3 %collective-permute-start.74 = (bf16[1,3,96,384]{3,2,1,0:T(8,128)(2,1)S(1)}, bf16[1,3,96,384]{3,2,1,0:T(8,128)(2,1)S(1)}, u32[]{:S(2)}, u32[]{:S(2)}) collective-permute-start(bf16[1,3,96,384]{3,2,1,0:T(8,128)(2,1)S(1)} %get-tuple-element.180), channel_id=1, source_target_pairs={{0,8},{8,0},{16,24},{24,16},{1,9},{9,1},{17,25},{25,17},{2,10},{10... | collective-permute-start | bytes 663560 | tf_op jit(solution)/shard_map/ppermute | solution.py:173
  259.1 6.6 collective-permute-start.75
  260.9 38.9 %collective-permute-start.66 = (bf16[2,3,96,384]{3,2,1,0:T(8,128)(2,1)}, bf16[2,3,96,384]{3,2,1,0:T(8,128)(2,1)}, u32[]{:S(2)}, u32[]{:S(2)}) collective-permute-start(bf16[2,3,96,384]{3,2,1,0:T(8,128)(2,1)} %pad_maximum_fusion.22), channel_id=1, source_target_pairs={{0,8},{8,0},{16,24},{24,16},{1,9},{9,1},{17,25},{25,17},{2,10},{10... | collective-permute-start | bytes 1327112 | tf_op jit(solution)/shard_map/ppermute | solution.py:173
  264.0 38.1 %collective-permute-start.67 = (bf16[2,3,96,384]{3,2,1,0:T(8,128)(2,1)}, bf16[2,3,96,384]{3,2,1,0:T(8,128)(2,1)}, u32[]{:S(2)}, u32[]{:S(2)}) collective-permute-start(bf16[2,3,96,384]{3,2,1,0:T(8,128)(2,1)} %pad_maximum_fusion.23), channel_id=1, source_target_pairs={{0,16},{8,24},{16,0},{24,8},{1,17},{9,25},{17,1},{25,9},{2,18},{10... | collective-permute-start | bytes 1327112 | tf_op jit(solution)/shard_map/ppermute | solution.py:173
  265.8 38.6 %collective-permute-start.71 = (bf16[2,3,96,384]{3,2,1,0:T(8,128)(2,1)}, bf16[2,3,96,384]{3,2,1,0:T(8,128)(2,1)}, u32[]{:S(2)}, u32[]{:S(2)}) collective-permute-start(bf16[2,3,96,384]{3,2,1,0:T(8,128)(2,1)} %pad_maximum_fusion.24), channel_id=1, source_target_pairs={{0,8},{8,0},{16,24},{24,16},{1,9},{9,1},{17,25},{25,17},{2,10},{10... | collective-permute-start | bytes 1327112 | tf_op jit(solution)/shard_map/ppermute | solution.py:173
  269.4 36.2 %collective-permute-start.72 = (bf16[2,3,96,384]{3,2,1,0:T(8,128)(2,1)}, bf16[2,3,96,384]{3,2,1,0:T(8,128)(2,1)}, u32[]{:S(2)}, u32[]{:S(2)}) collective-permute-start(bf16[2,3,96,384]{3,2,1,0:T(8,128)(2,1)} %pad_maximum_fusion.25), channel_id=1, source_target_pairs={{0,16},{8,24},{16,0},{24,8},{1,17},{9,25},{17,1},{25,9},{2,18},{10... | collective-permute-start | bytes 1327112 | tf_op jit(solution)/shard_map/ppermute | solution.py:173
  300.1 9.0 %collective-permute-start.76 = (bf16[2,3,96,384]{3,2,1,0:T(8,128)(2,1)S(1)}, bf16[2,3,96,384]{3,2,1,0:T(8,128)(2,1)S(1)}, u32[]{:S(2)}, u32[]{:S(2)}) collective-permute-start(bf16[2,3,96,384]{3,2,1,0:T(8,128)(2,1)S(1)} %copy-done.87), channel_id=1, source_target_pairs={{0,8},{8,0},{16,24},{24,16},{1,9},{9,1},{17,25},{25,17},{2,10},{10... | collective-permute-start | bytes 1327112 | tf_op jit(solution)/shard_map/ppermute | solution.py:173
  302.1 8.8 %collective-permute-start.77 = (bf16[2,3,96,384]{3,2,1,0:T(8,128)(2,1)S(1)}, bf16[2,3,96,384]{3,2,1,0:T(8,128)(2,1)S(1)}, u32[]{:S(2)}, u32[]{:S(2)}) collective-permute-start(bf16[2,3,96,384]{3,2,1,0:T(8,128)(2,1)S(1)} %copy-done.86), channel_id=1, source_target_pairs={{0,16},{8,24},{16,0},{24,8},{1,17},{9,25},{17,1},{25,9},{2,18},{10... | collective-permute-start | bytes 1327112 | tf_op jit(solution)/shard_map/ppermute | solution.py:173
  304.3 12.1 %collective-permute-start.58 = (bf16[1024,768]{0,1:T(8,128)(2,1)S(1)}, bf16[1024,768]{0,1:T(8,128)(2,1)S(1)}, u32[]{:S(2)}, u32[]{:S(2)}) collective-permute-start(bf16[1024,768]{0,1:T(8,128)(2,1)S(1)} %convolution_convert_fusion), channel_id=1, source_target_pairs={{0,1},{1,0},{2,3},{3,2},{4,5},{5,4},{6,7},{7,6},{8,9},{9,8},{10,11... | collective-permute-start | bytes 4718600 | tf_op jit(solution)/shard_map/ppermute | solution.py:173
  367.8 28.3 %collective-permute-start.158 = (bf16[2,3,96,384]{3,2,1,0:T(8,128)(2,1)}, bf16[2,3,96,384]{3,2,1,0:T(8,128)(2,1)}, u32[]{:S(2)}, u32[]{:S(2)}) collective-permute-start(bf16[2,3,96,384]{3,2,1,0:T(8,128)(2,1)} %pad_maximum_fusion.36), channel_id=1, source_target_pairs={{0,16},{8,24},{16,0},{24,8},{1,17},{9,25},{17,1},{25,9},{2,18},{10... | collective-permute-start | bytes 1327112 | tf_op jit(solution)/shard_map/ppermute | solution.py:173
  373.1 24.6 %collective-permute-start.153 = (bf16[2,3,96,384]{3,2,1,0:T(8,128)(2,1)}, bf16[2,3,96,384]{3,2,1,0:T(8,128)(2,1)}, u32[]{:S(2)}, u32[]{:S(2)}) collective-permute-start(bf16[2,3,96,384]{3,2,1,0:T(8,128)(2,1)} %pad_maximum_fusion.33), channel_id=1, source_target_pairs={{0,16},{8,24},{16,0},{24,8},{1,17},{9,25},{17,1},{25,9},{2,18},{10... | collective-permute-start | bytes 1327112 | tf_op jit(solution)/shard_map/ppermute | solution.py:173
  379.1 21.1 %collective-permute-start.148 = (bf16[2,3,96,384]{3,2,1,0:T(8,128)(2,1)}, bf16[2,3,96,384]{3,2,1,0:T(8,128)(2,1)}, u32[]{:S(2)}, u32[]{:S(2)}) collective-permute-start(bf16[2,3,96,384]{3,2,1,0:T(8,128)(2,1)} %pad_maximum_fusion.30), channel_id=1, source_target_pairs={{0,16},{8,24},{16,0},{24,8},{1,17},{9,25},{17,1},{25,9},{2,18},{10... | collective-permute-start | bytes 1327112 | tf_op jit(solution)/shard_map/ppermute | solution.py:173
  384.5 21.4 %collective-permute-start.144 = (bf16[2,3,96,384]{3,2,1,0:T(8,128)(2,1)}, bf16[2,3,96,384]{3,2,1,0:T(8,128)(2,1)}, u32[]{:S(2)}, u32[]{:S(2)}) collective-permute-start(bf16[2,3,96,384]{3,2,1,0:T(8,128)(2,1)} %pad_maximum_fusion.28), channel_id=1, source_target_pairs={{0,16},{8,24},{16,0},{24,8},{1,17},{9,25},{17,1},{25,9},{2,18},{10... | collective-permute-start | bytes 1327112 | tf_op jit(solution)/shard_map/ppermute | solution.py:173
  390.6 33.3 %collective-permute-start.78 = (bf16[512,768]{0,1:T(8,128)(2,1)}, bf16[512,768]{0,1:T(8,128)(2,1)}, u32[]{:S(2)}, u32[]{:S(2)}) collective-permute-start(bf16[512,768]{0,1:T(8,128)(2,1)} %slice.1977), channel_id=1, source_target_pairs={{0,1},{1,0},{2,3},{3,2},{4,5},{5,4},{6,7},{7,6},{8,9},{9,8},{10,11... | collective-permute-start | bytes 2359304 | tf_op jit(solution)/shard_map/ppermute | solution.py:173
  396.1 73.9 %collective-permute-start.80 = (bf16[1024,768]{0,1:T(8,128)(2,1)}, bf16[1024,768]{0,1:T(8,128)(2,1)}, u32[]{:S(2)}, u32[]{:S(2)}) collective-permute-start(bf16[1024,768]{0,1:T(8,128)(2,1)} %add_convert_fusion), channel_id=1, source_target_pairs={{0,1},{1,0},{2,3},{3,2},{4,5},{5,4},{6,7},{7,6},{8,9},{9,8},{10,11... | collective-permute-start | bytes 4718600 | tf_op jit(solution)/shard_map/ppermute | solution.py:173
  397.7 10.4 %collective-permute-start.159 = (bf16[1,3,96,384]{3,2,1,0:T(8,128)(2,1)S(1)}, bf16[1,3,96,384]{3,2,1,0:T(8,128)(2,1)S(1)}, u32[]{:S(2)}, u32[]{:S(2)}) collective-permute-start(bf16[1,3,96,384]{3,2,1,0:T(8,128)(2,1)S(1)} %fusion.55), channel_id=1, source_target_pairs={{0,8},{8,0},{16,24},{24,16},{1,9},{9,1},{17,25},{25,17},{2,10},{10... | collective-permute-start | bytes 663560 | tf_op jit(solution)/shard_map/ppermute | solution.py:173
  400.2 11.3 %collective-permute-start.154 = (bf16[1,3,96,384]{3,2,1,0:T(8,128)(2,1)S(1)}, bf16[1,3,96,384]{3,2,1,0:T(8,128)(2,1)S(1)}, u32[]{:S(2)}, u32[]{:S(2)}) collective-permute-start(bf16[1,3,96,384]{3,2,1,0:T(8,128)(2,1)S(1)} %fusion.63), channel_id=1, source_target_pairs={{0,8},{8,0},{16,24},{24,16},{1,9},{9,1},{17,25},{25,17},{2,10},{10... | collective-permute-start | bytes 663560 | tf_op jit(solution)/shard_map/ppermute | solution.py:173
  405.9 9.7 %collective-permute-start.149 = (bf16[1,3,96,384]{3,2,1,0:T(8,128)(2,1)S(1)}, bf16[1,3,96,384]{3,2,1,0:T(8,128)(2,1)S(1)}, u32[]{:S(2)}, u32[]{:S(2)}) collective-permute-start(bf16[1,3,96,384]{3,2,1,0:T(8,128)(2,1)S(1)} %fusion.71), channel_id=1, source_target_pairs={{0,8},{8,0},{16,24},{24,16},{1,9},{9,1},{17,25},{25,17},{2,10},{10... | collective-permute-start | bytes 663560 | tf_op jit(solution)/shard_map/ppermute | solution.py:173
  408.1 12.2 %collective-permute-start.145 = (bf16[1,3,96,384]{3,2,1,0:T(8,128)(2,1)S(1)}, bf16[1,3,96,384]{3,2,1,0:T(8,128)(2,1)S(1)}, u32[]{:S(2)}, u32[]{:S(2)}) collective-permute-start(bf16[1,3,96,384]{3,2,1,0:T(8,128)(2,1)S(1)} %fusion.79), channel_id=1, source_target_pairs={{0,8},{8,0},{16,24},{24,16},{1,9},{9,1},{17,25},{25,17},{2,10},{10... | collective-permute-start | bytes 663560 | tf_op jit(solution)/shard_map/ppermute | solution.py:173
  411.5 18.3 %collective-permute-start.160 = (bf16[2,3,96,384]{3,2,1,0:T(8,128)(2,1)}, bf16[2,3,96,384]{3,2,1,0:T(8,128)(2,1)}, u32[]{:S(2)}, u32[]{:S(2)}) collective-permute-start(bf16[2,3,96,384]{3,2,1,0:T(8,128)(2,1)} %pad_maximum_fusion.37), channel_id=1, source_target_pairs={{0,8},{8,0},{16,24},{24,16},{1,9},{9,1},{17,25},{25,17},{2,10},{10... | collective-permute-start | bytes 1327112 | tf_op jit(solution)/shard_map/ppermute | solution.py:173
  415.6 23.7 %collective-permute-start.155 = (bf16[2,3,96,384]{3,2,1,0:T(8,128)(2,1)}, bf16[2,3,96,384]{3,2,1,0:T(8,128)(2,1)}, u32[]{:S(2)}, u32[]{:S(2)}) collective-permute-start(bf16[2,3,96,384]{3,2,1,0:T(8,128)(2,1)} %pad_maximum_fusion.34), channel_id=1, source_target_pairs={{0,8},{8,0},{16,24},{24,16},{1,9},{9,1},{17,25},{25,17},{2,10},{10... | collective-permute-start | bytes 1327112 | tf_op jit(solution)/shard_map/ppermute | solution.py:173
  420.2 28.5 %collective-permute-start.150 = (bf16[2,3,96,384]{3,2,1,0:T(8,128)(2,1)}, bf16[2,3,96,384]{3,2,1,0:T(8,128)(2,1)}, u32[]{:S(2)}, u32[]{:S(2)}) collective-permute-start(bf16[2,3,96,384]{3,2,1,0:T(8,128)(2,1)} %pad_maximum_fusion.31), channel_id=1, source_target_pairs={{0,8},{8,0},{16,24},{24,16},{1,9},{9,1},{17,25},{25,17},{2,10},{10... | collective-permute-start | bytes 1327112 | tf_op jit(solution)/shard_map/ppermute | solution.py:173
  423.9 33.5 %collective-permute-start.146 = (bf16[2,3,96,384]{3,2,1,0:T(8,128)(2,1)}, bf16[2,3,96,384]{3,2,1,0:T(8,128)(2,1)}, u32[]{:S(2)}, u32[]{:S(2)}) collective-permute-start(bf16[2,3,96,384]{3,2,1,0:T(8,128)(2,1)} %pad_maximum_fusion.29), channel_id=1, source_target_pairs={{0,8},{8,0},{16,24},{24,16},{1,9},{9,1},{17,25},{25,17},{2,10},{10... | collective-permute-start | bytes 1327112 | tf_op jit(solution)/shard_map/ppermute | solution.py:173
  430.9 28.5 %collective-permute-start.161 = (bf16[1,3,96,384]{3,2,1,0:T(8,128)(2,1)S(1)}, bf16[1,3,96,384]{3,2,1,0:T(8,128)(2,1)S(1)}, u32[]{:S(2)}, u32[]{:S(2)}) collective-permute-start(bf16[1,3,96,384]{3,2,1,0:T(8,128)(2,1)S(1)} %fusion.51), channel_id=1, source_target_pairs={{0,16},{8,24},{16,0},{24,8},{1,17},{9,25},{17,1},{25,9},{2,18},{10... | collective-permute-start | bytes 663560 | tf_op jit(solution)/shard_map/ppermute | solution.py:173
  440.4 23.8 %collective-permute-start.156 = (bf16[1,3,96,384]{3,2,1,0:T(8,128)(2,1)S(1)}, bf16[1,3,96,384]{3,2,1,0:T(8,128)(2,1)S(1)}, u32[]{:S(2)}, u32[]{:S(2)}) collective-permute-start(bf16[1,3,96,384]{3,2,1,0:T(8,128)(2,1)S(1)} %fusion.59), channel_id=1, source_target_pairs={{0,16},{8,24},{16,0},{24,8},{1,17},{9,25},{17,1},{25,9},{2,18},{10... | collective-permute-start | bytes 663560 | tf_op jit(solution)/shard_map/ppermute | solution.py:173
  449.9 16.3 %collective-permute-start.151 = (bf16[1,3,96,384]{3,2,1,0:T(8,128)(2,1)S(1)}, bf16[1,3,96,384]{3,2,1,0:T(8,128)(2,1)S(1)}, u32[]{:S(2)}, u32[]{:S(2)}) collective-permute-start(bf16[1,3,96,384]{3,2,1,0:T(8,128)(2,1)S(1)} %fusion.67), channel_id=1, source_target_pairs={{0,16},{8,24},{16,0},{24,8},{1,17},{9,25},{17,1},{25,9},{2,18},{10... | collective-permute-start | bytes 663560 | tf_op jit(solution)/shard_map/ppermute | solution.py:173
  458.5 9.7 %collective-permute-start.147 = (bf16[1,3,96,384]{3,2,1,0:T(8,128)(2,1)S(1)}, bf16[1,3,96,384]{3,2,1,0:T(8,128)(2,1)S(1)}, u32[]{:S(2)}, u32[]{:S(2)}) collective-permute-start(bf16[1,3,96,384]{3,2,1,0:T(8,128)(2,1)S(1)} %fusion.75), channel_id=1, source_target_pairs={{0,16},{8,24},{16,0},{24,8},{1,17},{9,25},{17,1},{25,9},{2,18},{10... | collective-permute-start | bytes 663560 | tf_op jit(solution)/shard_map/ppermute | solution.py:173
  461.4 168.7 %collective-permute-start.162 = (bf16[3,192,384]{2,1,0:T(8,128)(2,1)}, bf16[3,192,384]{2,1,0:T(8,128)(2,1)}, u32[]{:S(2)}, u32[]{:S(2)}) collective-permute-start(bf16[3,192,384]{2,1,0:T(8,128)(2,1)} %pad_maximum_fusion.38), channel_id=1, source_target_pairs={{0,6},{1,7},{2,4},{3,5},{4,2},{5,3},{6,0},{7,1},{8,14},{9,15},{10,... | collective-permute-start | bytes 1327112 | tf_op jit(solution)/shard_map/ppermute | solution.py:173
  466.2 164.9 %collective-permute-start.157 = (bf16[3,192,384]{2,1,0:T(8,128)(2,1)}, bf16[3,192,384]{2,1,0:T(8,128)(2,1)}, u32[]{:S(2)}, u32[]{:S(2)}) collective-permute-start(bf16[3,192,384]{2,1,0:T(8,128)(2,1)} %pad_maximum_fusion.35), channel_id=1, source_target_pairs={{0,4},{1,5},{2,6},{3,7},{4,0},{5,1},{6,2},{7,3},{8,12},{9,13},{10,... | collective-permute-start | bytes 1327112 | tf_op jit(solution)/shard_map/ppermute | solution.py:173
  508.2 20.0 %collective-permute-start.110 = (bf16[2,1,96,6]{2,3,1,0:T(8,128)(2,1)}, bf16[2,1,96,6]{2,3,1,0:T(8,128)(2,1)}, u32[]{:S(2)}, u32[]{:S(2)}) collective-permute-start(bf16[2,1,96,6]{2,3,1,0:T(8,128)(2,1)} %pad_maximum_fusion.103), channel_id=1, source_target_pairs={{0,16},{8,24},{16,0},{24,8},{1,17},{9,25},{17,1},{25,9},{2,18},{10... | collective-permute-start | bytes 6920 | tf_op jit(solution)/shard_map/ppermute | solution.py:173
  510.0 20.1 %collective-permute-start.115 = (bf16[2,1,96,6]{2,3,1,0:T(8,128)(2,1)}, bf16[2,1,96,6]{2,3,1,0:T(8,128)(2,1)}, u32[]{:S(2)}, u32[]{:S(2)}) collective-permute-start(bf16[2,1,96,6]{2,3,1,0:T(8,128)(2,1)} %pad_maximum_fusion.106), channel_id=1, source_target_pairs={{0,16},{8,24},{16,0},{24,8},{1,17},{9,25},{17,1},{25,9},{2,18},{10... | collective-permute-start | bytes 6920 | tf_op jit(solution)/shard_map/ppermute | solution.py:173
  511.4 20.3 %collective-permute-start.120 = (bf16[2,1,96,6]{2,3,1,0:T(8,128)(2,1)}, bf16[2,1,96,6]{2,3,1,0:T(8,128)(2,1)}, u32[]{:S(2)}, u32[]{:S(2)}) collective-permute-start(bf16[2,1,96,6]{2,3,1,0:T(8,128)(2,1)} %pad_maximum_fusion.109), channel_id=1, source_target_pairs={{0,16},{8,24},{16,0},{24,8},{1,17},{9,25},{17,1},{25,9},{2,18},{10... | collective-permute-start | bytes 6920 | tf_op jit(solution)/shard_map/ppermute | solution.py:173
  530.1 33.3 %collective-permute-start.129 = (bf16[2,2,128,6]{2,3,1,0:T(8,128)(2,1)S(1)}, bf16[2,2,128,6]{2,3,1,0:T(8,128)(2,1)S(1)}, u32[]{:S(2)}, u32[]{:S(2)}) collective-permute-start(bf16[2,2,128,6]{2,3,1,0:T(8,128)(2,1)S(1)} %pad_maximum_fusion.83), channel_id=1, source_target_pairs={{0,16},{8,24},{16,0},{24,8},{1,17},{9,25},{17,1},{25,9},{2,18},{10... | collective-permute-start | bytes 18440 | tf_op jit(solution)/shard_map/ppermute | solution.py:173
  531.8 32.8 %collective-permute-start.134 = (bf16[2,2,128,6]{2,3,1,0:T(8,128)(2,1)S(1)}, bf16[2,2,128,6]{2,3,1,0:T(8,128)(2,1)S(1)}, u32[]{:S(2)}, u32[]{:S(2)}) collective-permute-start(bf16[2,2,128,6]{2,3,1,0:T(8,128)(2,1)S(1)} %pad_maximum_fusion.86), channel_id=1, source_target_pairs={{0,16},{8,24},{16,0},{24,8},{1,17},{9,25},{17,1},{25,9},{2,18},{10... | collective-permute-start | bytes 18440 | tf_op jit(solution)/shard_map/ppermute | solution.py:173
  596.7 35.5 %collective-permute-start.152 = (bf16[3,192,384]{2,1,0:T(8,128)(2,1)S(1)}, bf16[3,192,384]{2,1,0:T(8,128)(2,1)S(1)}, u32[]{:S(2)}, u32[]{:S(2)}) collective-permute-start(bf16[3,192,384]{2,1,0:T(8,128)(2,1)S(1)} %copy-done.85), channel_id=1, source_target_pairs={{0,2},{1,3},{2,0},{3,1},{4,6},{5,7},{6,4},{7,5},{8,10},{9,11},{10,... | collective-permute-start | bytes 1327112 | tf_op jit(solution)/shard_map/ppermute | solution.py:173
  608.0 37.6 %collective-permute-start.81 = (bf16[512,768]{0,1:T(8,128)(2,1)S(1)}, bf16[512,768]{0,1:T(8,128)(2,1)S(1)}, u32[]{:S(2)}, u32[]{:S(2)}) collective-permute-start(bf16[512,768]{0,1:T(8,128)(2,1)S(1)} %fusion.22), channel_id=1, source_target_pairs={{0,1},{1,0},{2,3},{3,2},{4,5},{5,4},{6,7},{7,6},{8,9},{9,8},{10,11... | collective-permute-start | bytes 2359304 | tf_op jit(solution)/shard_map/ppermute | solution.py:173
  631.2 6.7 collective-permute-start.103
  632.2 6.8 %collective-permute-start.89 = (bf16[2,3,96,96]{2,3,1,0:T(8,128)(2,1)S(1)}, bf16[2,3,96,96]{2,3,1,0:T(8,128)(2,1)S(1)}, u32[]{:S(2)}, u32[]{:S(2)}) collective-permute-start(bf16[2,3,96,96]{2,3,1,0:T(8,128)(2,1)S(1)} %pad_maximum_fusion.50), channel_id=1, source_target_pairs={{0,8},{8,0},{16,24},{24,16},{1,9},{9,1},{17,25},{25,17},{2,10},{10... | collective-permute-start | bytes 331784 | tf_op jit(solution)/shard_map/ppermute | solution.py:173
  641.4 7.7 %collective-permute-start.100 = (bf16[3,192,96]{1,2,0:T(8,128)(2,1)S(1)}, bf16[3,192,96]{1,2,0:T(8,128)(2,1)S(1)}, u32[]{:S(2)}, u32[]{:S(2)}) collective-permute-start(bf16[3,192,96]{1,2,0:T(8,128)(2,1)S(1)} %pad_maximum_fusion.56), channel_id=1, source_target_pairs={{0,4},{1,5},{2,6},{3,7},{4,0},{5,1},{6,2},{7,3},{8,12},{9,13},{10,... | collective-permute-start | bytes 331784 | tf_op jit(solution)/shard_map/ppermute | solution.py:173
  643.9 7.1 %collective-permute-start.105 = (bf16[3,192,96]{1,2,0:T(8,128)(2,1)S(1)}, bf16[3,192,96]{1,2,0:T(8,128)(2,1)S(1)}, u32[]{:S(2)}, u32[]{:S(2)}) collective-permute-start(bf16[3,192,96]{1,2,0:T(8,128)(2,1)S(1)} %pad_maximum_fusion.59), channel_id=1, source_target_pairs={{0,6},{1,7},{2,4},{3,5},{4,2},{5,3},{6,0},{7,1},{8,14},{9,15},{10,... | collective-permute-start | bytes 331784 | tf_op jit(solution)/shard_map/ppermute | solution.py:173
  663.5 6.9 %collective-permute-start.86 = (f32[2,768]{1,0:T(2,128)S(1)}, f32[2,768]{1,0:T(2,128)S(1)}, u32[]{:S(2)}, u32[]{:S(2)}) collective-permute-start(f32[2,768]{1,0:T(2,128)S(1)} %add.657), channel_id=1, source_target_pairs={{0,16},{8,24},{16,0},{24,8},{1,17},{9,25},{17,1},{25,9},{2,18},{10... | collective-permute-start | bytes 18440 | tf_op jit(solution)/shard_map/ppermute | solution.py:173
  (237 other events, 2438.2 us)

commit v2 on v1

--- a/solution.py
+++ b/solution.py
@@ -429,6 +429,649 @@
     )
 
 
+def hold(count):
+    return [pl.BlockSpec(memory_space=pltpu.VMEM)] * count
+
+
+def shaped(*shape, dtype=BF):
+    return jax.ShapeDtypeStruct(shape, dtype)
+
+
+def kernel_call(body, name, outs, scratch, args, flops, transcendentals=0, scalars=0, limit=56):
+    bytes_accessed = sum(a.size * a.dtype.itemsize for a in args)
+    bytes_accessed += sum(o.size * o.dtype.itemsize for o in outs)
+    smem = [pl.BlockSpec(memory_space=pltpu.SMEM)] * scalars
+    return pl.pallas_call(
+        body,
+        out_shape=tuple(outs),
+        in_specs=smem + hold(len(args) - scalars),
+        out_specs=tuple(hold(len(outs))),
+        scratch_shapes=scratch,
+        compiler_params=pltpu.CompilerParams(vmem_limit_bytes=limit << 20),
+        cost_estimate=pl.CostEstimate(
+            flops=int(flops), bytes_accessed=int(bytes_accessed), transcendentals=transcendentals
+        ),
+        name=name,
+    )(*args)
+
+
+def nn(left, right):
+    return lax.dot_general(left, right, (((1,), (0,)), ((), ())), preferred_element_type=F32)
+
+
+def nt(left, right):
+    return lax.dot_general(left, right, (((1,), (1,)), ((), ())), preferred_element_type=F32)
+
+
+def turned_over(value):
+    return value.astype(F32).T
+
+
+def pack_kernel(
+    value_ref, mixgate_ref, condition_ref, base_ref, shift_ref, mixout_ref, gate_ref, up_ref,
+    down_ref, mixer_ref, ffn_ref,
+):
+    depth, block_c = value_ref.shape
+    block_g = condition_ref.shape[1]
+    span = base_ref.shape[1] // 128
+    spare = jnp.zeros((depth, 128 - block_c), F32)
+    first = jnp.concatenate(
+        [
+            value_ref[...].astype(F32),
+            condition_ref[...].astype(F32),
+            jnp.zeros((depth, 128 - block_c - block_g), F32),
+        ],
+        axis=1,
+    ).astype(BF)
+    second = jnp.concatenate([mixgate_ref[...].astype(F32), spare], axis=1).astype(BF)
+    third = jnp.concatenate([turned_over(mixout_ref[...]), spare], axis=1).astype(BF)
+    half = mixer_ref.shape[1]
+    mixer_ref[0, :depth, :] = first
+    mixer_ref[0, depth:, :] = second[: half - depth]
+    left = 2 * depth - half
+    mixer_ref[1, :left, :] = second[half - depth :]
+    mixer_ref[1, left : left + depth, :] = third
+    mixer_ref[1, left + depth :, :] = jnp.zeros((half - left - depth, 128), BF)
+    for n, ref in enumerate((base_ref, shift_ref)):
+        piece = jnp.concatenate([ref[:, h * 128 : (h + 1) * 128] for h in range(span)], axis=0)
+        start = left + depth + 16 * n
+        mixer_ref[1, start : start + span * block_g, :] = piece
+    part = ffn_ref.shape[2]
+    down = turned_over(down_ref[...]).astype(BF)
+    for h in range(2):
+        cut = slice(h * part, (h + 1) * part)
+        ffn_ref[h, 0] = gate_ref[cut, :]
+        ffn_ref[h, 1] = up_ref[cut, :]
+        ffn_ref[h, 2] = down[cut, :]
+
+
+def norm_rows(value, gain):
+    centred = value - jnp.mean(value, axis=-1, keepdims=True)
+    scale = lax.rsqrt(jnp.mean(centred * centred, axis=-1, keepdims=True) + epsilon)
+    normal = centred * scale
+    return normal, scale, normal * gain
+
+
+def mixer_forward_kernel(
+    sizes, dp_ref, column_ref, row_ref, own_ref, other_ref, gain_ref, p0_ref, p1_ref, p2_ref,
+    p3a_ref, p3b_ref, branch_ref, normed_ref, values_ref, gates_ref, conv_ref, weights_ref,
+    condition_ref, taps_ref, shift_out_ref, cond_ref, summary_ref, whole_ref, base_ref,
+    mask_ref, band_ref, mixed_ref,
+):
+    depth, block_c, block_g, chips, span, unroll, channels, reach, half = sizes
+    local, width = own_ref.shape
+    rows, length = row_ref.shape[0], row_ref.shape[2]
+    per = local // length
+    dp = dp_ref[0]
+    pieces = ((p0_ref, None), (p1_ref, None), (p2_ref, None), (p3a_ref, p3b_ref))
+    left = 2 * depth - half
+    side = chips * block_c
+
+    for k in range(chips):
+        for m, (first, second) in enumerate(pieces):
+            low = first.at[0, k] if second is None else first.at[k]
+            high = first.at[1, k] if second is None else second.at[k]
+            j = dp ^ m
+            at = pl.multiple_of(j * depth, depth)
+            whole_ref[0, pl.ds(at, depth), :] = low[:depth, :]
+            whole_ref[1, pl.ds(at, half - depth), :] = low[depth:, :]
+            whole_ref[1, pl.ds(pl.multiple_of(at + half - depth, 64), left), :] = high[:left, :]
+            whole_ref[2, pl.ds(at, depth), :] = high[left : left + depth, :]
+            for n, ref in enumerate((base_ref, shift_out_ref)):
+                start = left + depth + 16 * n
+                piece = high[start : start + 16, :].astype(F32)
+                for h in range(span):
+                    lane = pl.multiple_of((j * span + h) * 128, 128)
+                    ref[k * block_g : (k + 1) * block_g, pl.ds(lane, 128)] = piece[
+                        h * block_g : (h + 1) * block_g
+                    ]
+        for s in range(3):
+            turned = turned_over(whole_ref[s])
+            weights_ref[s * side + k * block_c : s * side + (k + 1) * block_c, :] = turned[
+                :block_c
+            ].astype(BF)
+            if s == 0:
+                condition_ref[k * block_g : (k + 1) * block_g, :] = turned[
+                    block_c : block_c + block_g
+                ]
+
+    for h, ref in enumerate((own_ref, other_ref)):
+        for q in range(per):
+            r = h * per + q
+            _, _, normed = norm_rows(
+                ref[q * length : (q + 1) * length, :].astype(F32), gain_ref[...]
+            )
+            normed = normed.astype(BF)
+            normed_ref[r * length : (r + 1) * length, :] = normed
+            summary = jnp.mean(normed.astype(F32), axis=0, keepdims=True)
+            summary_ref[r : r + 1, :] = summary
+            cond = jnp.tanh(jnp.sum(condition_ref[...] * summary, axis=1, keepdims=True))
+            cond_ref[r] = jnp.broadcast_to(cond, cond_ref.shape[1:])
+            taps_ref[r] = base_ref[...] + cond * shift_out_ref[...]
+            lanes = slice(r * length, (r + 1) * length)
+            values_ref[:, lanes] = nt(weights_ref[:side, :], normed).astype(BF)
+            gates_ref[:, lanes] = nt(weights_ref[side : 2 * side, :], normed).astype(BF)
+
+    band_ref[...] = jnp.zeros_like(band_ref)
+    filters = chips * block_g
+    for r in range(rows):
+        lanes = slice(r * length, (r + 1) * length)
+        mask_ref[...] = (column_ref[lanes, :] == row_ref[r]).astype(BF)
+
+        def some(step, carry, r=r, lanes=lanes):
+            for u in range(unroll):
+                f = step * unroll + u
+                build_band(taps_ref[r, pl.ds(f, 1), :], mask_ref, band_ref.at[u], length, reach)
+                at = pl.ds(pl.multiple_of(f * channels, channels), channels)
+                conv = nn(values_ref[at, lanes], band_ref[u])
+                conv_ref[at, lanes] = conv.astype(BF)
+                mixed_ref[at, :] = conv * gates_ref[at, lanes].astype(F32)
+            return carry
+
+        lax.fori_loop(0, filters // unroll, some, 0)
+        branch_ref[lanes, :] = nn(mixed_ref[...].T.astype(BF), weights_ref[2 * side :, :]).astype(BF)
+
+
+def norm_two_kernel(
+    own_ref, other_ref, branch_ref, got_ref, grad_own_ref, grad_other_ref, gain_ref, normed_ref,
+    normed_turned_ref, grad_turned_ref,
+):
+    local = own_ref.shape[0]
+    for h, (ref, grad_ref) in enumerate(((own_ref, grad_own_ref), (other_ref, grad_other_ref))):
+        here, there = slice(h * local, (h + 1) * local), slice((1 - h) * local, (2 - h) * local)
+        middle = (
+            ref[...].astype(F32) + branch_ref[here, :].astype(F32) + got_ref[there, :].astype(F32)
+        )
+        _, _, normed = norm_rows(middle, gain_ref[...])
+        normed = normed.astype(BF)
+        normed_ref[here, :] = normed
+        normed_turned_ref[:, here] = turned_over(normed).astype(BF)
+        grad_turned_ref[:, here] = turned_over(grad_ref[...]).astype(BF)
+
+
+def ffn_kernel(
+    first, dp_ref, normed_ref, normed_turned_ref, grad_own_ref, grad_other_ref, grad_turned_ref,
+    p0_ref, p1_ref, p2_ref, p3a_ref, p3b_ref, *refs,
+):
+    if first:
+        before = (None, None, None)
+    else:
+        before, refs = refs[:3], refs[3:]
+    feed_own_ref, feed_other_ref, back_ref, g0_ref, g1a_ref, g1b_ref, g2a_ref, g2b_ref = refs[:8]
+    g3a_ref, g3b_ref, weight_ref, hidden_ref, gate_ref, up_ref, grads_ref = refs[8:15]
+    feed_sum_ref, back_sum_ref = refs[15:]
+    total = normed_ref.shape[0]
+    local = grad_own_ref.shape[0]
+    count, _, part, _ = g1a_ref.shape
+    dp = dp_ref[0]
+    step = min(256, local)
+    pieces = ((p0_ref, None), (p1_ref, None), (p2_ref, None), (p3a_ref, p3b_ref))
+    outs = ((g0_ref.at[0], g0_ref.at[1]), (g1a_ref, g1b_ref), (g2a_ref, g2b_ref), (g3a_ref, g3b_ref))
+    for k in range(count):
+        for m, (one, two) in enumerate(pieces):
+            for h in range(2):
+                source = one.at[h, k] if two is None else (one, two)[h].at[k]
+                at = pl.multiple_of((dp ^ m) * (2 * part) + h * part, part)
+                for s in range(3):
+                    weight_ref[s, pl.ds(at, part), :] = source[s]
+        for t in range(total // step):
+            here = slice(t * step, (t + 1) * step)
+            grad_ref = grad_own_ref if t * step < local else grad_other_ref
+            there = slice(t * step % local, t * step % local + step)
+            gate_pre = nn(normed_ref[here, :], weight_ref[0])
+            up_pre = nn(normed_ref[here, :], weight_ref[1])
+            grad_hidden = nn(grad_ref[there, :], weight_ref[2])
+            sigmoid = 1.0 / (1.0 + jnp.exp(-gate_pre))
+            silu = gate_pre * sigmoid
+            hidden = (silu * up_pre).astype(BF)
+            grad_gate = (grad_hidden * up_pre * (sigmoid + silu * (1.0 - sigmoid))).astype(BF)
+            grad_up = (grad_hidden * silu).astype(BF)
+            hidden_ref[here, :] = hidden
+            gate_ref[here, :] = grad_gate
+            up_ref[here, :] = grad_up
+            feed = nt(hidden, weight_ref[2])
+            back = nt(grad_gate, weight_ref[0]) + nt(grad_up, weight_ref[1])
+            feed_out = feed_own_ref if t * step < local else feed_other_ref
+            if k == 0 and not first:
+                feed_in = before[0] if t * step < local else before[1]
+                feed = feed + feed_in[there, :].astype(F32)
+                back = back + before[2][here, :].astype(F32)
+            if k > 0:
+                feed = feed + feed_sum_ref[here, :]
+                back = back + back_sum_ref[here, :]
+            if k == count - 1:
+                feed_out[there, :] = feed.astype(BF)
+                back_ref[here, :] = back.astype(BF)
+            else:
+                feed_sum_ref[here, :] = feed
+                back_sum_ref[here, :] = back
+        grads_ref[0] = nn(normed_turned_ref[...], gate_ref[...]).astype(BF)
+        grads_ref[1] = nn(normed_turned_ref[...], up_ref[...]).astype(BF)
+        grads_ref[2] = nn(grad_turned_ref[...], hidden_ref[...]).astype(BF)
+        for m, pair in enumerate(outs):
+            for h in range(2):
+                at = pl.multiple_of((dp ^ m) * (2 * part) + h * part, part)
+                for s in range(3):
+                    pair[h][k, s] = grads_ref[s, pl.ds(at, part), :]
+
+
+def mixout_back_kernel(
+    own_ref, other_ref, branch_ref, got_ref, back_ref, back_got_ref, grad_own_ref, grad_other_ref,
+    gain_ref, weights_ref, gates_ref, conv_ref, middle_ref, mixout_ref, grad_conv_ref,
+    grad_gates_ref, gain_grad_ref, rounded_ref,
+):
+    local = own_ref.shape[0]
+    side = weights_ref.shape[0]
+    for h, (ref, grad_ref) in enumerate(((own_ref, grad_own_ref), (other_ref, grad_other_ref))):
+        here, there = slice(h * local, (h + 1) * local), slice((1 - h) * local, (2 - h) * local)
+        middle = (
+            ref[...].astype(F32) + branch_ref[here, :].astype(F32) + got_ref[there, :].astype(F32)
+        )
+        normal, scale, _ = norm_rows(middle, gain_ref[...])
+        grad = back_ref[here, :].astype(F32) + back_got_ref[there, :].astype(F32)
+        grad_middle = grad_ref[...].astype(F32) + normalize_back(
+            normal, scale, gain_ref[...], grad
+        )
+        if h == 0:
+            gain_grad_ref[...] = jnp.sum(grad * normal, axis=0, keepdims=True)
+            middle_ref[...] = grad_middle
+        rounded = grad_middle.astype(BF)
+        rounded_ref[here, :] = rounded
+        grad_mixed = nt(weights_ref[...], rounded)
+        gates, conv = gates_ref[:, here].astype(F32), conv_ref[:, here].astype(F32)
+        grad_conv_ref[:, here] = (grad_mixed * gates).astype(BF)
+        grad_gates_ref[:, here] = (grad_mixed * conv).astype(BF)
+    mixed = (gates_ref[...].astype(F32) * conv_ref[...].astype(F32)).astype(BF)
+    mixout_ref[...] = nn(mixed, rounded_ref[...]).astype(BF)
+
+
+def conv_back_kernel(
+    unroll, channels, reach, column_ref, turned_ref, row_ref, taps_ref, values_ref, grad_ref,
+    grad_values_ref, grad_taps_ref, mask_ref, mask_turned_ref, band_ref, grad_turned_ref,
+):
+    length = row_ref.shape[1]
+    filters = taps_ref.shape[0]
+    blocks = length // BLOCK
+    mask_ref[...] = (column_ref[...] == row_ref[...]).astype(BF)
+    mask_turned_ref[...] = (turned_ref[...] == row_ref[...]).astype(F32)
+    band_ref[...] = jnp.zeros_like(band_ref)
+    turn = (
+        lax.broadcasted_iota(jnp.int32, (length, length), 0)
+        + lax.broadcasted_iota(jnp.int32, (length, length), 1)
+        == length - 1
+    ).astype(BF)
+    grad_turned_ref[...] = nn(grad_ref[...], turn)
+
+    def some(step, carry):
+        for u in range(unroll):
+            f = step * unroll + u
+            build_band(taps_ref[pl.ds(f, 1), :], mask_ref, band_ref.at[u], length, reach)
+            rows = pl.ds(pl.multiple_of(f * channels, channels), channels)
+            grad_values_ref[rows, :] = nt(grad_ref[rows, :], band_ref[u]).astype(BF)
+            turned = grad_turned_ref[rows, :].T.astype(BF)
+            product = nn(turned, values_ref[rows, :])
+            parts = [jnp.zeros((BLOCK, BLOCK), F32)] + [None] * (2 * reach + 1)
+            for i in range(blocks):
+                back = blocks - 1 - i
+                for j in range(max(0, back - reach), min(blocks, back + reach + 1)):
+                    here = (
+                        slice(i * BLOCK, (i + 1) * BLOCK),
+                        slice(j * BLOCK, (j + 1) * BLOCK),
+                    )
+                    block = product[here] * mask_turned_ref[here]
+                    d = j - back + reach + 1
+                    parts[d] = block if parts[d] is None else parts[d] + block
+            aligned = pltpu.roll(jnp.concatenate(parts, axis=1), 0, 1, stride=1, stride_axis=0)
+            grad_taps_ref[pl.ds(f, 1), :] = jnp.sum(aligned, axis=0, keepdims=True)
+        return carry
+
+    lax.fori_loop(0, filters // unroll, some, 0)
+
+
+def mixer_back_kernel(
+    sizes, rows, dp_ref, normed_ref, gates_ref, mixout_ref, weights_ref, condition_ref, shift_ref,
+    cond_ref, summary_ref, *refs,
+):
+    depth, block_c, block_g, chips, span, unroll, channels, reach, half = sizes
+    values_refs, taps_refs, refs = refs[:rows], refs[rows : 2 * rows], refs[2 * rows :]
+    back_ref, g0_ref, g1a_ref, g1b_ref, g2a_ref, g2b_ref, g3a_ref, g3b_ref = refs[:8]
+    whole_ref, filter_ref = refs[8:]
+    length = values_refs[0].shape[1]
+    side = chips * block_c
+    filters = chips * block_g
+    width = taps_refs[0].shape[1]
+    taps = shift_ref.shape[1]
+    left = 2 * depth - half
+    dp = dp_ref[0]
+    lane = lax.broadcasted_iota(jnp.int32, (width, taps), 0)
+    tap = lax.broadcasted_iota(jnp.int32, (width, taps), 1)
+    reachable = (tap > taps // 2 - (reach + 1) * BLOCK) & (tap < taps // 2 + (reach + 1) * BLOCK)
+    spot = taps - 1 - tap
+    spot = jnp.where(spot >= width, spot - width, spot)
+    place = ((lane == spot) & reachable).astype(BF)
+    shift_there = nt(shift_ref[...].astype(BF), place)
+    base_grad = shift_grad = condition_grad = None
+    value_grad = gate_grad = None
+    for r in range(rows):
+        lanes = slice(r * length, (r + 1) * length)
+        grad_taps = taps_refs[r][...]
+        cond = cond_ref[r, :, :1]
+        summary = summary_ref[r : r + 1, :]
+        grad_cond = jnp.sum(grad_taps * shift_there, axis=1, keepdims=True) * (1.0 - cond * cond)
+        grad_summary = jnp.sum(grad_cond * condition_ref[...], axis=0, keepdims=True) / length
+        one, two, three = grad_taps, cond * grad_taps, grad_cond * summary
+        values, gates = values_refs[r][...], gates_ref[:, lanes]
+        normed = normed_ref[lanes, :]
+        four, five = nn(values, normed), nn(gates, normed)
+        if r == 0:
+            base_grad, shift_grad, condition_grad = one, two, three
+            value_grad, gate_grad = four, five
+        else:
+            base_grad, shift_grad = base_grad + one, shift_grad + two
+            condition_grad = condition_grad + three
+            value_grad, gate_grad = value_grad + four, gate_grad + five
+        back = nn(turned_over(values).astype(BF), weights_ref[:side, :])
+        back = back + nn(turned_over(gates).astype(BF), weights_ref[side : 2 * side, :])
+        back_ref[lanes, :] = (back + grad_summary).astype(BF)
+    filter_ref[0] = nn(base_grad.astype(BF), place)
+    filter_ref[1] = nn(shift_grad.astype(BF), place)
+    outs = ((g0_ref.at[0], g0_ref.at[1]), (g1a_ref, g1b_ref), (g2a_ref, g2b_ref), (g3a_ref, g3b_ref))
+    spare = jnp.zeros((128 - block_c, value_grad.shape[1]), F32)
+    for k in range(chips):
+        cut = slice(k * block_c, (k + 1) * block_c)
+        own = slice(k * block_g, (k + 1) * block_g)
+        first = jnp.concatenate(
+            [value_grad[cut], condition_grad[own], spare[: 128 - block_c - block_g]], axis=0
+        )
+        whole_ref[0] = first.T.astype(BF)
+        whole_ref[1] = jnp.concatenate([gate_grad[cut], spare], axis=0).T.astype(BF)
+        whole_ref[2] = jnp.concatenate([mixout_ref[cut, :].astype(F32), spare], axis=0).T.astype(BF)
+        for m, (low, high) in enumerate(outs):
+            j = dp ^ m
+            at = pl.multiple_of(j * depth, depth)
+            low[k, :depth, :] = whole_ref[0, pl.ds(at, depth), :]
+            low[k, depth:, :] = whole_ref[1, pl.ds(at, half - depth), :]
+            high[k, :left, :] = whole_ref[1, pl.ds(pl.multiple_of(at + half - depth, 64), left), :]
+            high[k, left : left + depth, :] = whole_ref[2, pl.ds(at, depth), :]
+            for n in range(2):
+                start = left + depth + 16 * n
+                parts = [
+                    filter_ref[n, own, pl.ds(pl.multiple_of((j * span + h) * 128, 128), 128)]
+                    for h in range(span)
+                ] + [jnp.zeros((16 - span * block_g, 128), F32)]
+                high[k, start : start + 16, :] = jnp.concatenate(parts, axis=0).astype(BF)
+            end = left + depth + 32
+            high[k, end:, :] = jnp.zeros((half - end, 128), BF)
+
+
+def norm_one_back_kernel(
+    own_ref, back_ref, got_ref, middle_ref, gain_ref, grad_ref, gain_grad_ref
+):
+    local = own_ref.shape[0]
+    normal, scale, _ = norm_rows(own_ref[...].astype(F32), gain_ref[...])
+    grad = back_ref[:local, :].astype(F32) + got_ref[...].astype(F32)
+    grad_ref[...] = (
+        middle_ref[...] + normalize_back(normal, scale, gain_ref[...], grad)
+    ).astype(BF)
+    gain_grad_ref[...] = jnp.sum(grad * normal, axis=0, keepdims=True)
+
+
+def square_gather(column):
+    along_x, along_y = swap(column, "dp", 1), swap(column, "dp", 2)
+    return column, along_x, along_y, swap(along_x[0], "dp", 2), swap(along_y[1], "dp", 1)
+
+
+def add(left, right):
+    return (left.astype(F32) + right.astype(F32)).astype(BF)
+
+
+def square_scatter(g0, g1a, g1b, g2a, g2b, g3a, g3b):
+    e1, e2 = swap(g3a, "dp", 2), swap(g3b, "dp", 1)
+    f1b, f2a = swap(g1b, "dp", 1), swap(g2a, "dp", 2)
+    f1a, f2b = swap(add(g1a, e1), "dp", 1), swap(add(g2b, e2), "dp", 2)
+
+    def three(one, two, other):
+        return (one.astype(F32) + two.astype(F32) + other.astype(F32)).astype(BF)
+
+    return jnp.stack([three(g0[0], f1a, f2a), three(g0[1], f1b, f2b)])
+
+
+def fast_body(
+    tokens, segment_ids, gain_one, gain_two, value_weight, mixgate_weight, condition_weight,
+    filter_base, filter_shift, mixout_weight, gate_weight, up_weight, down_weight, output_grad,
+):
+    dp, mp = lax.axis_index("dp"), lax.axis_index("mp")
+    chips = lax.axis_size("mp") // 2
+    local, width = tokens.shape
+    length = segment_ids.shape[1]
+    per = local // length
+    rows, total = 2 * per, 2 * local
+    depth, block_c = value_weight.shape
+    block_g, taps = filter_base.shape
+    block_f = gate_weight.shape[1]
+    channels = block_c // block_g
+    reach = SENTENCE // BLOCK
+    side, filters = chips * block_c, chips * block_g
+    half = 5 * depth // 3
+    part = depth // 2
+    sizes = (depth, block_c, block_g, chips, taps // 128, 4, channels, reach, half)
+    dp_one = dp[None].astype(jnp.int32)
+    gain_first, gain_second = gain_one[None, :], gain_two[None, :]
+
+    mixer_pack, ffn_pack = kernel_call(
+        pack_kernel, "pack_weights",
+        [shaped(2, half, 128), shaped(2, 3, part, block_f)], [],
+        (
+            value_weight, mixgate_weight, condition_weight, filter_base, filter_shift,
+            mixout_weight, gate_weight, up_weight, down_weight,
+        ),
+        1e6,
+    )
+    other = swap(tokens, "mp", 1)
+    other_grad = swap(output_grad, "mp", 1)
+    seg_rows = jnp.concatenate(
+        [
+            lax.dynamic_slice_in_dim(segment_ids, mp * per, per),
+            lax.dynamic_slice_in_dim(segment_ids, (mp ^ 1) * per, per),
+        ]
+    )
+    seg_column = seg_rows.reshape(total, 1)
+    seg_turned = seg_rows[:, ::-1].reshape(total, 1)
+
+    mixer_line = [mixer_pack] + [swap(mixer_pack, "mp", 2 * k) for k in range(1, chips)]
+    mixer_column = jnp.stack(mixer_line, axis=1)
+    ffn_first = square_gather(ffn_pack[:, None])
+    mixer = square_gather(mixer_column)
+    ffn_pack, mixer_column = lax.optimization_barrier((ffn_pack, mixer_column))
+    ffn_line = [swap(ffn_pack, "mp", 2 * k) for k in range(1, chips)]
+    columns = [ffn_line[0][:, None], jnp.stack(ffn_line[1:], axis=1)]
+    columns[0], d1, d2 = lax.optimization_barrier((columns[0], mixer[3], mixer[4]))
+    mixer = mixer[:3] + (d1, d2)
+    ffn_second = square_gather(columns[0])
+    columns[1], d1, d2 = lax.optimization_barrier((columns[1], ffn_second[3], ffn_second[4]))
+    ffn_second = ffn_second[:3] + (d1, d2)
+    ffn_third = square_gather(columns[1])
+
+    (
+        branch, normed_one, values, gates, conv, weights, condition, row_taps, shift, cond, summary,
+    ) = kernel_call(
+        functools.partial(mixer_forward_kernel, sizes), "mixer_forward",
+        [
+            shaped(total, width), shaped(total, width), shaped(side, total), shaped(side, total),
+            shaped(side, total), shaped(3 * side, width), shaped(filters, width, dtype=F32),
+            shaped(rows, filters, 2 * length, dtype=F32), shaped(filters, 2 * length, dtype=F32),
+            shaped(rows, filters, 128, dtype=F32), shaped(rows, width, dtype=F32),
+        ],
+        [
+            pltpu.VMEM((3, width, 128), BF), pltpu.VMEM((filters, 2 * length), F32),
+            pltpu.VMEM((length, length), BF), pltpu.VMEM((sizes[5], length, length), BF),
+            pltpu.VMEM((side, length), F32),
+        ],
+        (dp_one, seg_column, seg_rows[:, None, :], tokens, other, gain_first) + mixer,
+        14e9, scalars=1,
+    )
+    branch_got = swap(branch, "mp", 1)
+    normed_two, normed_turned, grad_turned = kernel_call(
+        norm_two_kernel, "norm_two",
+        [shaped(total, width), shaped(width, total), shaped(width, total)], [],
+        (tokens, other, branch, branch_got, output_grad, other_grad, gain_second),
+        1e9,
+    )
+
+    carried = ()
+    ffn_grads = []
+    for index, group in enumerate((ffn_first, ffn_second, ffn_third)):
+        count = group[0].shape[1]
+        quarter = shaped(count, 3, part, block_f)
+        results = kernel_call(
+            functools.partial(ffn_kernel, index == 0), "ffn",
+            [shaped(local, width), shaped(local, width), shaped(total, width)]
+            + [shaped(2, count, 3, part, block_f)] + [quarter] * 6,
+            [
+                pltpu.VMEM((3, width, block_f), BF), pltpu.VMEM((total, block_f), BF),
+                pltpu.VMEM((total, block_f), BF), pltpu.VMEM((total, block_f), BF),
+                pltpu.VMEM((3, width, block_f), BF),
+                pltpu.VMEM((total, width) if count > 1 else (8, 128), F32),
+                pltpu.VMEM((total, width) if count > 1 else (8, 128), F32),
+            ],
+            (dp_one, normed_two, normed_turned, output_grad, other_grad, grad_turned)
+            + group + carried,
+            18 * total * width * block_f * count, scalars=1,
+        )
+        carried = tuple(results[:3])
+        ffn_grads.append(results[3:])
+    feed, feed_other, back = carried
+
+    ffn_sums = [square_scatter(*g) for g in ffn_grads]
+    by_chip = [ffn_sums[0][:, 0], ffn_sums[1][:, 0], ffn_sums[2][:, 0], ffn_sums[2][:, 1]]
+    ffn_sum = by_chip[0].astype(F32)
+    for k in range(1, chips):
+        ffn_sum = ffn_sum + swap(by_chip[k], "mp", 2 * k).astype(F32)
+    gate_sum, up_sum, down_sum = jnp.concatenate([ffn_sum[0], ffn_sum[1]], axis=1)
+
+    back_got = swap(back, "mp", 1)
+    feed_got = swap(feed_other, "mp", 1)
+    output = (
+        tokens.astype(F32) + branch[:local].astype(F32) + branch_got[local:].astype(F32)
+        + feed.astype(F32) + feed_got.astype(F32)
+    ).astype(BF)
+    grad_middle, mixout_grad, grad_conv, grad_gates, gain_two_part = kernel_call(
+        mixout_back_kernel, "mixout_back",
+        [
+            shaped(local, width, dtype=F32), shaped(side, width), shaped(side, total),
+            shaped(side, total), shaped(1, width, dtype=F32),
+        ],
+        [pltpu.VMEM((total, width), BF)],
+        (
+            tokens, other, branch, branch_got, back, back_got, output_grad, other_grad, gain_second,
+            weights[2 * side :], gates, conv,
+        ),
+        4 * total * width * side,
+    )
+    backs = []
+    for r in range(rows):
+        lanes = slice(r * length, (r + 1) * length)
+        backs.append(
+            kernel_call(
+                functools.partial(conv_back_kernel, 4, channels, reach), "conv_back",
+                [shaped(side, length), shaped(filters, (2 * reach + 2) * BLOCK, dtype=F32)],
+                [
+                    pltpu.VMEM((length, length), BF), pltpu.VMEM((length, length), F32),
+                    pltpu.VMEM((4, length, length), BF), pltpu.VMEM((side, length), F32),
+                ],
+                (
+                    seg_column[lanes], seg_turned[lanes], seg_rows[r : r + 1], row_taps[r],
+                    values[:, lanes], grad_conv[:, lanes],
+                ),
+                8e9,
+            )
+        )
+    eighth = shaped(chips, half, 128)
+    results = kernel_call(
+        functools.partial(mixer_back_kernel, sizes, rows), "mixer_back",
+        [shaped(total, width), shaped(2, chips, half, 128)] + [eighth] * 6,
+        [pltpu.VMEM((3, width, 128), BF), pltpu.VMEM((2, filters, 2 * length), F32)],
+        (
+            dp_one, normed_one, grad_gates, mixout_grad, weights, condition, shift, cond, summary,
+        ) + tuple(b[0] for b in backs) + tuple(b[1] for b in backs),
+        8 * total * width * side, scalars=1,
+    )
+    grad_one, mixer_grads = results[0], results[1:]
+    mixer_part = square_scatter(*mixer_grads)
+    mixer_sum = mixer_part[:, 0].astype(F32)
+    for k in range(1, chips):
+        mixer_sum = mixer_sum + swap(mixer_part[:, k], "mp", 2 * k).astype(F32)
+    mixer_sum = mixer_sum.reshape(2 * half, 128)
+
+    got_one = swap(grad_one[local:], "mp", 1)
+    input_grad, gain_one_part = kernel_call(
+        norm_one_back_kernel, "norm_one_back",
+        [shaped(local, width), shaped(1, width, dtype=F32)], [],
+        (tokens, grad_one, got_one, grad_middle, gain_first),
+        1e9,
+    )
+    gain_one_grad, gain_two_grad = everywhere(
+        jnp.concatenate([gain_one_part, gain_two_part])
+    )
+    span = taps // 128
+
+    def filter_out(start):
+        piece = mixer_sum[start : start + span * block_g].reshape(span, block_g, 128)
+        return jnp.swapaxes(piece, 0, 1).reshape(block_g, taps)
+
+    return (
+        output, input_grad, gain_one_grad, gain_two_grad,
+        mixer_sum[:depth, :block_c],
+        mixer_sum[depth : 2 * depth, :block_c],
+        mixer_sum[:depth, block_c : block_c + block_g],
+        filter_out(3 * depth), filter_out(3 * depth + 16),
+        mixer_sum[2 * depth : 3 * depth, :block_c].T,
+        gate_sum, up_sum, down_sum.T,
+    )
+
+
+def choose(tokens, segment_ids, gain_one, gain_two, value_weight, mixgate_weight, condition_weight,
+           filter_base, filter_shift, mixout_weight, gate_weight, up_weight, down_weight,
+           output_grad):
+    depth, block_c = value_weight.shape
+    block_g, taps = filter_base.shape
+    fits = (
+        lax.axis_size("dp") == 4
+        and lax.axis_size("mp") == 8
+        and tokens.shape[0] % segment_ids.shape[1] == 0
+        and depth == 192
+        and block_c % 16 == 0
+        and block_c + block_g <= 128
+        and taps % 128 == 0
+        and taps // 128 * block_g <= 16
+        and gate_weight.shape[1] % 128 == 0
+    )
+    return (fast_body if fits else body)(
+        tokens, segment_ids, gain_one, gain_two, value_weight, mixgate_weight, condition_weight,
+        filter_base, filter_shift, mixout_weight, gate_weight, up_weight, down_weight, output_grad,
+    )
+
+
 def solution(mesh):
     sides = P(("dp", "mp"), None)
     columns, rows = P("dp", "mp"), P("mp", "dp")
@@ -439,4 +1082,4 @@
     out_specs = (
         sides, sides, P(), P(), columns, columns, columns, rows, rows, rows, columns, columns, rows,
     )
-    return jax.shard_map(body, mesh=mesh, in_specs=in_specs, out_specs=out_specs, check_vma=False)
+    return jax.shard_map(choose, mesh=mesh, in_specs=in_specs, out_specs=out_specs, check_vma=False)

time: 678 us -> 359 us (0.53)
  waiting for transfers between devices: 260 us -> 106 us
  Pallas kernels: 22.7 us -> 118 us
  other arithmetic: 99.6 us -> 8.11 us
  matrix products: 77.9 us -> 0 us
  starting transfers between devices: 151 us -> 90.4 us
  local copies, waits for them, and re-layouts: 55.6 us -> 29.2 us
    ppermute x163 -> x63, waiting for transfers between devices: 260 us -> 106 us  [swap(): lax.ppermute(value, axis, [(i, i ^ mask) for i in range(lax.axis_size(axi...]
    pallas_call x4 -> x11, Pallas kernels: 22.7 us -> 118 us  [kernel_call(): pl.pallas_call(body, out_shape=tuple(outs), in_specs=smem + hold(len(args...]
    dot_general x48 -> x0, matrix products: 77.9 us -> none  [the longest x46 77.1 us: mm(): lax.dot_general(left, right, (dims, ((), ())), preferred_element_type=F32)]
    ppermute x163 -> x63, starting transfers between devices: 151 us -> 90.4 us  [swap(): lax.ppermute(value, axis, [(i, i ^ mask) for i in range(lax.axis_size(axi...]
    another operation x138 -> x6, other arithmetic: 33.5 us -> 2.06 us  [the longest x1 1.03 us: fast_body(): mixer_column = jnp.stack(mixer_line, axis=1)]
    add x37 -> x2, other arithmetic: 21.9 us -> 1.39 us  [the longest x1 1.31 us: fast_body(): ffn_sum = ffn_sum + swap(by_chip[k], 'mp', 2 * k).astype(F32)]
    reduce_sum x10 -> x0, other arithmetic: 17 us -> none  [the longest x1 5.75 us: body(): jnp.mean(normed_one.astype(F32).reshape(rows, length, width), axis=1)]
    concatenate x53 -> x1, other arithmetic: 14.1 us -> 0.76 us  [fast_body(): jnp.concatenate([gain_one_part, gain_two_part])]
  transfers between devices with their start and end apart: 163 -> 63, of which waited for: 98 -> 21; matrix products, arithmetic and copies ran while one was open for 28% -> 7% of each run, Pallas kernels for 3% -> 33%
where the time goes in v2:
time: 359 us; the launch traced here: 353 us
  Pallas kernels  118 us (33%)
  waiting for transfers between devices  106 us (30%)
  starting transfers between devices  90.4 us (25%)
  local copies, waits for them, and re-layouts  29.2 us (8%)
  other arithmetic  8.11 us (2%)
    pallas_call x11, Pallas kernels, kernel_call(): pl.pallas_call(body, out_shape=tuple(outs), in_specs=smem + hold(len(args...  118 us
    ppermute x63, waiting for transfers between devices, swap(): lax.ppermute(value, axis, [(i, i ^ mask) for i in range(lax.axis_size(axi...  106 us
    ppermute x63, starting transfers between devices, swap(): lax.ppermute(value, axis, [(i, i ^ mask) for i in range(lax.axis_size(axi...  90.4 us
    unnamed x112, local copies, waits for them, and re-layouts  9.92 us
  transfers between devices with their start and end apart: 63, of which 21 were waited for; matrix products, arithmetic and copies ran while one was open for 7% of the time, Pallas kernels for 33%

profile of v2, /device:TPU:0, one launch (start us, length us, event | category | flops | bytes accessed | tf_op | source)
XLA Modules:
  0.0 353.1 jit_solution(12982294113533547623)
XLA Ops:
  0.6 1.7 copy.40.down_ref
  2.4 1.4 copy.39.condition_ref
  3.8 2.2 pack_weights.1
  6.0 3.0 collective-permute-start.1
  9.1 2.6 collective-permute-start.2
  11.7 4.3 %collective-permute-done.1 = bf16[2,320,128]{2,1,0:T(8,128)(2,1)S(1)} collective-permute-done((bf16[2,320,128]{2,1,0:T(8,128)(2,1)}, bf16[2,320,128]{2,1,0:T(8,128)(2,1)S(1)}, u32[]{:S(2)}, u32[]{:S(2)}) %collective-permute-start.1) | collective-permute-done | bytes 163872 | tf_op jit(solution)/shard_map/ppermute | solution.py:173
  16.0 8.4 %collective-permute-done.2 = bf16[2,320,128]{2,1,0:T(8,128)(2,1)S(1)} collective-permute-done((bf16[2,320,128]{2,1,0:T(8,128)(2,1)}, bf16[2,320,128]{2,1,0:T(8,128)(2,1)S(1)}, u32[]{:S(2)}, u32[]{:S(2)}) %collective-permute-start.2) | collective-permute-done | bytes 163872 | tf_op jit(solution)/shard_map/ppermute | solution.py:173
  25.4 1.6 collective-permute-start.4
  26.9 1.5 collective-permute-start.5
  28.5 2.7 collective-permute-start.6
  31.1 8.3 %collective-permute-done.4.p1_ref = bf16[2,4,320,128]{3,2,1,0:T(8,128)(2,1)S(1)} collective-permute-done((bf16[2,4,320,128]{3,2,1,0:T(8,128)(2,1)S(1)}, bf16[2,4,320,128]{3,2,1,0:T(8,128)(2,1)S(1)}, u32[]{:S(2)}, u32[]{:S(2)}) %collective-permute-start.4) | collective-permute-done | bytes 655392 | tf_op jit(solution)/shard_map/ppermute | solution.py:173
  39.5 1.6 collective-permute-start.7
  41.1 1.5 collective-permute-done.5.p2_ref
  43.0 4.7 %collective-permute-done.7.p3a_ref = bf16[4,320,128]{2,1,0:T(8,128)(2,1)S(1)} collective-permute-done((bf16[4,320,128]{2,1,0:T(8,128)(2,1)S(1)}, bf16[4,320,128]{2,1,0:T(8,128)(2,1)S(1)}, u32[]{:S(2)}, u32[]{:S(2)}) %collective-permute-start.7) | collective-permute-done | bytes 327712 | tf_op jit(solution)/shard_map/ppermute | solution.py:173
  47.7 3.6 %collective-permute-done.8.p3b_ref = bf16[4,320,128]{2,1,0:T(8,128)(2,1)S(1)} collective-permute-done((bf16[4,320,128]{2,1,0:T(8,128)(2,1)S(1)}, bf16[4,320,128]{2,1,0:T(8,128)(2,1)S(1)}, u32[]{:S(2)}, u32[]{:S(2)}) %collective-permute-start.8) | collective-permute-done | bytes 327712 | tf_op jit(solution)/shard_map/ppermute | solution.py:173
  51.7 1.7 collective-permute-start.21
  53.4 1.5 collective-permute-start.22
  63.2 1.3 collective-permute-done.13.p1_ref
  64.5 3.7 %collective-permute-start.12 = (bf16[2,3,96,384]{3,2,1,0:T(8,128)(2,1)}, bf16[2,3,96,384]{3,2,1,0:T(8,128)(2,1)S(1)}, u32[]{:S(2)}, u32[]{:S(2)}) collective-permute-start(bf16[2,3,96,384]{3,2,1,0:T(8,128)(2,1)} %get-tuple-element.87), channel_id=1, source_target_pairs={{0,6},{1,7},{2,4},{3,5},{4,2},{5,3},{6,0},{7,1},{8,14},{9,15},{10,... | collective-permute-start | bytes 1327112 | tf_op jit(solution)/shard_map/ppermute | solution.py:173
  68.3 7.2 %collective-permute-done.15.p2_ref = bf16[2,1,3,96,384]{4,3,2,1,0:T(8,128)(2,1)} collective-permute-done((bf16[2,1,3,96,384]{4,3,2,1,0:T(8,128)(2,1)}, bf16[2,1,3,96,384]{4,3,2,1,0:T(8,128)(2,1)}, u32[]{:S(2)}, u32[]{:S(2)}) %collective-permute-start.15) | collective-permute-done | bytes 442400 | tf_op jit(solution)/shard_map/ppermute | solution.py:173
  75.4 2.6 collective-permute-start.11
  78.9 1.4 collective-permute-start.14
  81.2 15.3 %mixer_forward.1 = (bf16[1024,768]{1,0:T(8,128)(2,1)}, bf16[1024,768]{1,0:T(8,128)(2,1)}, bf16[384,1024]{1,0:T(8,128)(2,1)}, bf16[384,1024]{1,0:T(8,128)(2,1)}, ...) custom-call(s32[1]{0:T(128)} %bitcast.dp_ref, ...), custom_call_target="tpu_custom_call" | custom-call | flops 14000000000 | bytes 11879428 | tf_op jit(solution)/shard_map/mixer_forward/pallas_call | solution.py:444
  96.5 7.8 %collective-permute-done.11 = bf16[2,3,96,384]{3,2,1,0:T(8,128)(2,1)S(1)} collective-permute-done((bf16[2,3,96,384]{3,2,1,0:T(8,128)(2,1)}, bf16[2,3,96,384]{3,2,1,0:T(8,128)(2,1)S(1)}, u32[]{:S(2)}, u32[]{:S(2)}) %collective-permute-start.11) | collective-permute-done | bytes 442400 | tf_op jit(solution)/shard_map/ppermute | solution.py:173
  105.1 1.7 collective-permute-start.17
  108.3 1.5 collective-permute-start.18
  111.5 2.0 slice.152.weights_ref
  114.5 12.3 %collective-permute-done.17.p1_ref = bf16[2,2,3,96,384]{4,3,2,1,0:T(8,128)(2,1)S(1)} collective-permute-done((bf16[2,2,3,96,384]{4,3,2,1,0:T(8,128)(2,1)S(1)}, bf16[2,2,3,96,384]{4,3,2,1,0:T(8,128)(2,1)S(1)}, u32[]{:S(2)}, u32[]{:S(2)}) %collective-permute-start.17) | collective-permute-done | bytes 884768 | tf_op jit(solution)/shard_map/ppermute | solution.py:173
  126.7 1.7 collective-permute-start.24
  128.5 5.4 %collective-permute-done.18.p2_ref = bf16[2,2,3,96,384]{4,3,2,1,0:T(8,128)(2,1)S(1)} collective-permute-done((bf16[2,2,3,96,384]{4,3,2,1,0:T(8,128)(2,1)S(1)}, bf16[2,2,3,96,384]{4,3,2,1,0:T(8,128)(2,1)S(1)}, u32[]{:S(2)}, u32[]{:S(2)}) %collective-permute-start.18) | collective-permute-done | bytes 884768 | tf_op jit(solution)/shard_map/ppermute | solution.py:173
  134.8 1.3 collective-permute-start.20
  136.1 1.2 copy-done.3
  137.3 6.8 %norm_two.1 = (bf16[1024,768]{1,0:T(8,128)(2,1)}, bf16[768,1024]{1,0:T(8,128)(2,1)}, bf16[768,1024]{1,0:T(8,128)(2,1)}) custom-call(bf16[512,768]{1,0:T(8,128)(2,1)} %own_ref.7, bf16[512,768]{1,0:T(8,128)(2,1)} %copy-done.6, bf16[1024,768]{1,0:T(8,128)(2,1)} %get-tuple-element.90.branch_ref, bf16[1024,768]{1,0:T(8,128)(2,1)} %copy-done.3, ...), custom_call_target="tpu_custom_call" | custom-call | flops 1000000000 | bytes 11013120 | tf_op jit(solution)/shard_map/norm_two/pallas_call | solution.py:444
  144.9 12.4 %ffn.3 = (bf16[512,768]{1,0:T(8,128)(2,1)}, bf16[512,768]{1,0:T(8,128)(2,1)}, bf16[1024,768]{1,0:T(8,128)(2,1)}, bf16[2,1,3,96,384]{4,3,2,1,0:T(8,128)(2,1)}, bf...) custom-call(s32[1]{0:T(128)} %bitcast.dp_ref, ...), custom_call_target="tpu_custom_call" | custom-call | flops 5435817984 | bytes 12976132 | tf_op jit(solution)/shard_map/ffn/pallas_call | solution.py:444
  158.0 1.2 collective-permute-start.46
  160.1 13.8 %ffn.4 = (bf16[512,768]{1,0:T(8,128)(2,1)}, bf16[512,768]{1,0:T(8,128)(2,1)}, bf16[1024,768]{1,0:T(8,128)(2,1)}, bf16[2,1,3,96,384]{4,3,2,1,0:T(8,128)(2,1)}, bf...) custom-call(s32[1]{0:T(128)} %bitcast.dp_ref, ...), custom_call_target="tpu_custom_call" | custom-call | flops 5435817984 | bytes 16121860 | tf_op jit(solution)/shard_map/ffn/pallas_call | solution.py:444
  173.9 1.3 collective-permute-start.45
  176.2 1.3 collective-permute-start.48
  178.3 22.8 %ffn.5 = (bf16[512,768]{1,0:T(8,128)(2,1)}, bf16[512,768]{1,0:T(8,128)(2,1)}, bf16[1024,768]{1,0:T(8,128)(2,1)}, bf16[2,2,3,96,384]{4,3,2,1,0:T(8,128)(2,1)}, bf...) custom-call(s32[1]{0:T(128)} %bitcast.dp_ref, ...), custom_call_target="tpu_custom_call" | custom-call | flops 10871635968 | bytes 19660804 | tf_op jit(solution)/shard_map/ffn/pallas_call | solution.py:444
  201.2 1.3 collective-permute-start.59
  203.5 1.3 collective-permute-start.51
  204.8 8.1 %collective-permute-done.59 = bf16[2,3,96,384]{3,2,1,0:T(8,128)(2,1)S(1)} collective-permute-done((bf16[2,3,96,384]{3,2,1,0:T(8,128)(2,1)}, bf16[2,3,96,384]{3,2,1,0:T(8,128)(2,1)S(1)}, u32[]{:S(2)}, u32[]{:S(2)}) %collective-permute-start.59) | collective-permute-done | bytes 442400 | tf_op jit(solution)/shard_map/ppermute | solution.py:173
  217.4 4.0 %collective-permute-done.43 = bf16[1,3,96,384]{3,2,1,0:T(8,128)(2,1)S(1)} collective-permute-done((bf16[1,3,96,384]{3,2,1,0:T(8,128)(2,1)S(1)}, bf16[1,3,96,384]{3,2,1,0:T(8,128)(2,1)S(1)}, u32[]{:S(2)}, u32[]{:S(2)}) %collective-permute-start.43) | collective-permute-done | bytes 221216 | tf_op jit(solution)/shard_map/ppermute | solution.py:173
  223.4 3.7 %collective-permute-done.53 = bf16[1,3,96,384]{3,2,1,0:T(8,128)(2,1)S(1)} collective-permute-done((bf16[1,3,96,384]{3,2,1,0:T(8,128)(2,1)S(1)}, bf16[1,3,96,384]{3,2,1,0:T(8,128)(2,1)S(1)}, u32[]{:S(2)}, u32[]{:S(2)}) %collective-permute-start.53) | collective-permute-done | bytes 221216 | tf_op jit(solution)/shard_map/ppermute | solution.py:173
  229.6 7.0 %collective-permute-done.57 = bf16[2,3,96,384]{3,2,1,0:T(8,128)(2,1)S(1)} collective-permute-done((bf16[2,3,96,384]{3,2,1,0:T(8,128)(2,1)S(1)}, bf16[2,3,96,384]{3,2,1,0:T(8,128)(2,1)S(1)}, u32[]{:S(2)}, u32[]{:S(2)}) %collective-permute-start.57) | collective-permute-done | bytes 442400 | tf_op jit(solution)/shard_map/ppermute | solution.py:173
  236.5 11.2 %collective-permute-start.54 = (bf16[2,3,96,384]{3,2,1,0:T(8,128)(2,1)S(1)}, bf16[2,3,96,384]{3,2,1,0:T(8,128)(2,1)S(1)}, u32[]{:S(2)}, u32[]{:S(2)}) collective-permute-start(bf16[2,3,96,384]{3,2,1,0:T(8,128)(2,1)S(1)} %maximum_bitcast_fusion.1), channel_id=1, source_target_pairs={{0,2},{1,3},{2,0},{3,1},{4,6},{5,7},{6,4},{7,5},{8,10},{9,11},{10,... | collective-permute-start | bytes 1327112 | tf_op jit(solution)/shard_map/ppermute | solution.py:173
  248.2 10.6 %collective-permute-start.61 = (bf16[2,3,96,384]{3,2,1,0:T(8,128)(2,1)S(1)}, bf16[2,3,96,384]{3,2,1,0:T(8,128)(2,1)S(1)}, u32[]{:S(2)}, u32[]{:S(2)}) collective-permute-start(bf16[2,3,96,384]{3,2,1,0:T(8,128)(2,1)S(1)} %get-tuple-element.164), channel_id=1, source_target_pairs={{0,4},{1,5},{2,6},{3,7},{4,0},{5,1},{6,2},{7,3},{8,12},{9,13},{10,... | collective-permute-start | bytes 1327112 | tf_op jit(solution)/shard_map/ppermute | solution.py:173
  259.4 1.1 copy-done.8
  260.5 9.9 %mixout_back.1 = (f32[512,768]{1,0:T(8,128)}, bf16[384,768]{1,0:T(8,128)(2,1)}, bf16[384,1024]{1,0:T(8,128)(2,1)}, bf16[384,1024]{1,0:T(8,128)(2,1)}, f32[1,768]{1,0:T(1,128)}) custom-call(bf16[512,768]{1,0:T(8,128)(2,1)} %own_ref.7, bf16[512,768]{1,0:T(8,128)(2,1)} %copy-done.6, bf16[1024,768]{1,0:T(8,128)(2,1)} %get-tuple-element.90.branch_ref, ...), custom_call_target="tpu_custom_call" | custom-call | flops 1207959552 | bytes 15341568 | tf_op jit(solution)/shard_map/mixout_back/pallas_call | solution.py:444
  270.4 2.0 fusion.46
  272.5 10.8 %conv_back.3 = (bf16[384,512]{1,0:T(8,128)(2,1)}, f32[24,768]{1,0:T(8,128)}) custom-call(s32[512,1]{1,0:T(8,128)} %copy.45.column_ref, s32[512,1]{1,0:T(8,128)} %copy.46.turned_ref, s32[1,512]{1,0:T(1,128)} %copy-done.33, f32[24,1024]{1,0:T(8,128)} %get-tuple-element.186.taps_ref, bf16[384,512]{1,0:T(8,128)(2,1)} %get-tuple-element.170.values_ref, ...), custom_call_target="tpu_custom_call" | custom-call | flops 8000000000 | bytes 1357824 | tf_op jit(solution)/shard_map/conv_back/pallas_call | solution.py:444
  283.3 10.9 %conv_back.2 = (bf16[384,512]{1,0:T(8,128)(2,1)}, f32[24,768]{1,0:T(8,128)}) custom-call(s32[512,1]{1,0:T(8,128)} %copy.43.column_ref, s32[512,1]{1,0:T(8,128)} %copy.44.turned_ref, s32[1,512]{1,0:T(1,128)} %copy-done.32, f32[24,1024]{1,0:T(8,128)} %get-tuple-element.187.taps_ref, bf16[384,512]{1,0:T(8,128)(2,1)} %get-tuple-element.171.values_ref, ...), custom_call_target="tpu_custom_call" | custom-call | flops 8000000000 | bytes 1357824 | tf_op jit(solution)/shard_map/conv_back/pallas_call | solution.py:444
  294.2 8.4 %mixer_back.1 = (bf16[1024,768]{1,0:T(8,128)(2,1)}, bf16[2,4,320,128]{3,2,1,0:T(8,128)(2,1)}, bf16[4,320,128]{2,1,0:T(8,128)(2,1)}, bf16[4,320,128]{2,1,0:T(8,12...) custom-call(s32[1]{0:T(128)} %bitcast.dp_ref, ...), custom_call_target="tpu_custom_call" | custom-call | flops 2415919104 | bytes 10049540 | tf_op jit(solution)/shard_map/mixer_back/pallas_call | solution.py:444
  303.6 1.2 slice.165
  305.0 1.4 add_convert_fusion
  306.4 1.3 fusion.5
  313.4 4.4 %norm_one_back.1 = (bf16[512,768]{1,0:T(8,128)(2,1)}, f32[1,768]{1,0:T(1,128)}) custom-call(bf16[512,768]{1,0:T(8,128)(2,1)} %own_ref.7, bf16[1024,768]{1,0:T(8,128)(2,1)} %get-tuple-element.124.back_ref, bf16[512,768]{1,0:T(8,128)(2,1)} %copy-done.12, f32[512,768]{1,0:T(8,128)} %get-tuple-element.125.middle_ref, f32[1,768]{1,0:T(1,128)} %broadcast_in_dim.20.gain_ref), custom_call_target="tpu_custom_call" | custom-call | flops 1000000000 | bytes 5511168 | tf_op jit(solution)/shard_map/norm_one_back/pallas_call | solution.py:444
  321.1 3.2 collective-permute-done.29
  324.3 1.9 collective-permute-start.30
  326.2 5.7 %collective-permute-done.38 = bf16[4,320,128]{2,1,0:T(8,128)(2,1)S(1)} collective-permute-done((bf16[4,320,128]{2,1,0:T(8,128)(2,1)S(1)}, bf16[4,320,128]{2,1,0:T(8,128)(2,1)S(1)}, u32[]{:S(2)}, u32[]{:S(2)}) %collective-permute-start.38) | collective-permute-done | bytes 327712 | tf_op jit(solution)/shard_map/ppermute | solution.py:173
  332.2 1.1 collective-permute-start.31
  333.6 3.7 %collective-permute-start.40 = (bf16[2,320,128]{2,1,0:T(8,128)(2,1)S(1)}, bf16[2,320,128]{2,1,0:T(8,128)(2,1)S(1)}, u32[]{:S(2)}, u32[]{:S(2)}) collective-permute-start(bf16[2,320,128]{2,1,0:T(8,128)(2,1)S(1)} %get-tuple-element.174), channel_id=1, source_target_pairs={{0,4},{1,5},{2,6},{3,7},{4,0},{5,1},{6,2},{7,3},{8,12},{9,13},{10,... | collective-permute-start | bytes 491528 | tf_op jit(solution)/shard_map/ppermute | solution.py:173
  339.9 1.7 collective-permute-done.32
  342.2 7.3 %collective-permute-done.40 = bf16[2,320,128]{2,1,0:T(8,128)(2,1)S(1)} collective-permute-done((bf16[2,320,128]{2,1,0:T(8,128)(2,1)S(1)}, bf16[2,320,128]{2,1,0:T(8,128)(2,1)S(1)}, u32[]{:S(2)}, u32[]{:S(2)}) %collective-permute-start.40) | collective-permute-done | bytes 163872 | tf_op jit(solution)/shard_map/ppermute | solution.py:173
  (243 shorter events, 50.2 us)
Async XLA Ops:
  3.8 47.9 %copy-start = (bf16[512,768]{1,0:T(8,128)(2,1)S(1)}, bf16[512,768]{1,0:T(8,128)(2,1)}, u32[]{:S(2)}) copy-start(bf16[512,768]{1,0:T(8,128)(2,1)} %own_ref.7) | copy-start | bytes 2359300
  6.0 9.9 %collective-permute-start.1 = (bf16[2,320,128]{2,1,0:T(8,128)(2,1)}, bf16[2,320,128]{2,1,0:T(8,128)(2,1)S(1)}, u32[]{:S(2)}, u32[]{:S(2)}) collective-permute-start(bf16[2,320,128]{2,1,0:T(8,128)(2,1)} %get-tuple-element.85), channel_id=1, source_target_pairs={{0,2},{1,3},{2,0},{3,1},{4,6},{5,7},{6,4},{7,5},{8,10},{9,11},{10,... | collective-permute-start | bytes 491528 | tf_op jit(solution)/shard_map/ppermute | solution.py:173
  9.1 15.3 %collective-permute-start.2 = (bf16[2,320,128]{2,1,0:T(8,128)(2,1)}, bf16[2,320,128]{2,1,0:T(8,128)(2,1)S(1)}, u32[]{:S(2)}, u32[]{:S(2)}) collective-permute-start(bf16[2,320,128]{2,1,0:T(8,128)(2,1)} %get-tuple-element.85), channel_id=1, source_target_pairs={{0,4},{1,5},{2,6},{3,7},{4,0},{5,1},{6,2},{7,3},{8,12},{9,13},{10,... | collective-permute-start | bytes 491528 | tf_op jit(solution)/shard_map/ppermute | solution.py:173
  11.7 12.7 %collective-permute-start.3 = (bf16[2,320,128]{2,1,0:T(8,128)(2,1)}, bf16[2,320,128]{2,1,0:T(8,128)(2,1)S(1)}, u32[]{:S(2)}, u32[]{:S(2)}) collective-permute-start(bf16[2,320,128]{2,1,0:T(8,128)(2,1)} %get-tuple-element.85), channel_id=1, source_target_pairs={{0,6},{1,7},{2,4},{3,5},{4,2},{5,3},{6,0},{7,1},{8,14},{9,15},{10,... | collective-permute-start | bytes 491528 | tf_op jit(solution)/shard_map/ppermute | solution.py:173
  25.4 14.1 %collective-permute-start.4 = (bf16[2,4,320,128]{3,2,1,0:T(8,128)(2,1)S(1)}, bf16[2,4,320,128]{3,2,1,0:T(8,128)(2,1)S(1)}, u32[]{:S(2)}, u32[]{:S(2)}) collective-permute-start(bf16[2,4,320,128]{3,2,1,0:T(8,128)(2,1)S(1)} %pad_maximum_fusion.1.p0_ref), channel_id=1, source_target_pairs={{0,8},{8,0},{16,24},{24,16},{1,9},{9,1},{17,25},{25,17},{2,10},{10... | collective-permute-start | bytes 1966088 | tf_op jit(solution)/shard_map/ppermute | solution.py:173
  26.9 15.6 %collective-permute-start.5 = (bf16[2,4,320,128]{3,2,1,0:T(8,128)(2,1)S(1)}, bf16[2,4,320,128]{3,2,1,0:T(8,128)(2,1)S(1)}, u32[]{:S(2)}, u32[]{:S(2)}) collective-permute-start(bf16[2,4,320,128]{3,2,1,0:T(8,128)(2,1)S(1)} %pad_maximum_fusion.1.p0_ref), channel_id=1, source_target_pairs={{0,16},{8,24},{16,0},{24,8},{1,17},{9,25},{17,1},{25,9},{2,18},{10... | collective-permute-start | bytes 1966088 | tf_op jit(solution)/shard_map/ppermute | solution.py:173
  28.5 14.6 %collective-permute-start.6 = (bf16[2,3,96,384]{3,2,1,0:T(8,128)(2,1)}, bf16[2,3,96,384]{3,2,1,0:T(8,128)(2,1)}, u32[]{:S(2)}, u32[]{:S(2)}) collective-permute-start(bf16[2,3,96,384]{3,2,1,0:T(8,128)(2,1)} %get-tuple-element.87), channel_id=1, source_target_pairs={{0,2},{1,3},{2,0},{3,1},{4,6},{5,7},{6,4},{7,5},{8,10},{9,11},{10,... | collective-permute-start | bytes 1327112 | tf_op jit(solution)/shard_map/ppermute | solution.py:173
  39.5 8.2 %collective-permute-start.7 = (bf16[4,320,128]{2,1,0:T(8,128)(2,1)S(1)}, bf16[4,320,128]{2,1,0:T(8,128)(2,1)S(1)}, u32[]{:S(2)}, u32[]{:S(2)}) collective-permute-start(bf16[4,320,128]{2,1,0:T(8,128)(2,1)S(1)} %slice_bitcast_fusion.5), channel_id=1, source_target_pairs={{0,16},{8,24},{16,0},{24,8},{1,17},{9,25},{17,1},{25,9},{2,18},{10... | collective-permute-start | bytes 983048 | tf_op jit(solution)/shard_map/ppermute | solution.py:173
  42.6 8.7 %collective-permute-start.8 = (bf16[4,320,128]{2,1,0:T(8,128)(2,1)S(1)}, bf16[4,320,128]{2,1,0:T(8,128)(2,1)S(1)}, u32[]{:S(2)}, u32[]{:S(2)}) collective-permute-start(bf16[4,320,128]{2,1,0:T(8,128)(2,1)S(1)} %slice_bitcast_fusion.4), channel_id=1, source_target_pairs={{0,8},{8,0},{16,24},{24,16},{1,9},{9,1},{17,25},{25,17},{2,10},{10... | collective-permute-start | bytes 983048 | tf_op jit(solution)/shard_map/ppermute | solution.py:173
  51.3 13.2 %collective-permute-start.13 = (bf16[2,1,3,96,384]{4,3,2,1,0:T(8,128)(2,1)}, bf16[2,1,3,96,384]{4,3,2,1,0:T(8,128)(2,1)S(1)}, u32[]{:S(2)}, u32[]{:S(2)}) collective-permute-start(bf16[2,1,3,96,384]{4,3,2,1,0:T(8,128)(2,1)} %bitcast.6.p0_ref), channel_id=1, source_target_pairs={{0,8},{8,0},{16,24},{24,16},{1,9},{9,1},{17,25},{25,17},{2,10},{10... | collective-permute-start | bytes 1327112 | tf_op jit(solution)/shard_map/ppermute | solution.py:173
  51.7 28.6 %collective-permute-start = (bf16[512,768]{1,0:T(8,128)(2,1)S(1)}, bf16[512,768]{1,0:T(8,128)(2,1)S(1)}, u32[]{:S(2)}, u32[]{:S(2)}) collective-permute-start(bf16[512,768]{1,0:T(8,128)(2,1)S(1)} %copy-done), channel_id=1, source_target_pairs={{0,1},{1,0},{2,3},{3,2},{4,5},{5,4},{6,7},{7,6},{8,9},{9,8},{10,11... | collective-permute-start | bytes 2359304 | tf_op jit(solution)/shard_map/ppermute | solution.py:173
  51.7 55.1 %collective-permute-start.21 = (bf16[2,1,3,96,384]{4,3,2,1,0:T(8,128)(2,1)}, bf16[2,1,3,96,384]{4,3,2,1,0:T(8,128)(2,1)}, u32[]{:S(2)}, u32[]{:S(2)}) collective-permute-start(bf16[2,1,3,96,384]{4,3,2,1,0:T(8,128)(2,1)} %bitcast.15.p0_ref), channel_id=1, source_target_pairs={{0,8},{8,0},{16,24},{24,16},{1,9},{9,1},{17,25},{25,17},{2,10},{10... | collective-permute-start | bytes 1327112 | tf_op jit(solution)/shard_map/ppermute | solution.py:173
  53.4 54.9 %collective-permute-start.22 = (bf16[2,1,3,96,384]{4,3,2,1,0:T(8,128)(2,1)}, bf16[2,1,3,96,384]{4,3,2,1,0:T(8,128)(2,1)}, u32[]{:S(2)}, u32[]{:S(2)}) collective-permute-start(bf16[2,1,3,96,384]{4,3,2,1,0:T(8,128)(2,1)} %bitcast.15.p0_ref), channel_id=1, source_target_pairs={{0,16},{8,24},{16,0},{24,8},{1,17},{9,25},{17,1},{25,9},{2,18},{10... | collective-permute-start | bytes 1327112 | tf_op jit(solution)/shard_map/ppermute | solution.py:173
  54.9 20.5 %collective-permute-start.15 = (bf16[2,1,3,96,384]{4,3,2,1,0:T(8,128)(2,1)}, bf16[2,1,3,96,384]{4,3,2,1,0:T(8,128)(2,1)}, u32[]{:S(2)}, u32[]{:S(2)}) collective-permute-start(bf16[2,1,3,96,384]{4,3,2,1,0:T(8,128)(2,1)} %bitcast.6.p0_ref), channel_id=1, source_target_pairs={{0,16},{8,24},{16,0},{24,8},{1,17},{9,25},{17,1},{25,9},{2,18},{10... | collective-permute-start | bytes 1327112 | tf_op jit(solution)/shard_map/ppermute | solution.py:173
  64.5 14.4 %collective-permute-start.12 = (bf16[2,3,96,384]{3,2,1,0:T(8,128)(2,1)}, bf16[2,3,96,384]{3,2,1,0:T(8,128)(2,1)S(1)}, u32[]{:S(2)}, u32[]{:S(2)}) collective-permute-start(bf16[2,3,96,384]{3,2,1,0:T(8,128)(2,1)} %get-tuple-element.87), channel_id=1, source_target_pairs={{0,6},{1,7},{2,4},{3,5},{4,2},{5,3},{6,0},{7,1},{8,14},{9,15},{10,... | collective-permute-start | bytes 1327112 | tf_op jit(solution)/shard_map/ppermute | solution.py:173
  75.4 29.0 %collective-permute-start.11 = (bf16[2,3,96,384]{3,2,1,0:T(8,128)(2,1)}, bf16[2,3,96,384]{3,2,1,0:T(8,128)(2,1)S(1)}, u32[]{:S(2)}, u32[]{:S(2)}) collective-permute-start(bf16[2,3,96,384]{3,2,1,0:T(8,128)(2,1)} %get-tuple-element.87), channel_id=1, source_target_pairs={{0,4},{1,5},{2,6},{3,7},{4,0},{5,1},{6,2},{7,3},{8,12},{9,13},{10,... | collective-permute-start | bytes 1327112 | tf_op jit(solution)/shard_map/ppermute | solution.py:173
  78.9 25.6 %collective-permute-start.14 = (bf16[1,3,96,384]{3,2,1,0:T(8,128)(2,1)S(1)}, bf16[1,3,96,384]{3,2,1,0:T(8,128)(2,1)S(1)}, u32[]{:S(2)}, u32[]{:S(2)}) collective-permute-start(bf16[1,3,96,384]{3,2,1,0:T(8,128)(2,1)S(1)} %slice_bitcast_fusion.9), channel_id=1, source_target_pairs={{0,16},{8,24},{16,0},{24,8},{1,17},{9,25},{17,1},{25,9},{2,18},{10... | collective-permute-start | bytes 663560 | tf_op jit(solution)/shard_map/ppermute | solution.py:173
  80.3 24.8 %collective-permute-start.16 = (bf16[1,3,96,384]{3,2,1,0:T(8,128)(2,1)S(1)}, bf16[1,3,96,384]{3,2,1,0:T(8,128)(2,1)S(1)}, u32[]{:S(2)}, u32[]{:S(2)}) collective-permute-start(bf16[1,3,96,384]{3,2,1,0:T(8,128)(2,1)S(1)} %slice_bitcast_fusion.8), channel_id=1, source_target_pairs={{0,8},{8,0},{16,24},{24,16},{1,9},{9,1},{17,25},{25,17},{2,10},{10... | collective-permute-start | bytes 663560 | tf_op jit(solution)/shard_map/ppermute | solution.py:173
  104.4 31.7 %collective-permute-start.9 = (bf16[1024,768]{1,0:T(8,128)(2,1)}, bf16[1024,768]{1,0:T(8,128)(2,1)S(1)}, u32[]{:S(2)}, u32[]{:S(2)}) collective-permute-start(bf16[1024,768]{1,0:T(8,128)(2,1)} %get-tuple-element.90.branch_ref), channel_id=1, source_target_pairs={{0,1},{1,0},{2,3},{3,2},{4,5},{5,4},{6,7},{7,6},{8,9},{9,8},{10,11... | collective-permute-start | bytes 4718600 | tf_op jit(solution)/shard_map/ppermute | solution.py:173
  104.5 30.2 %collective-permute-start.10 = (bf16[512,768]{1,0:T(8,128)(2,1)S(1)}, bf16[512,768]{1,0:T(8,128)(2,1)S(1)}, u32[]{:S(2)}, u32[]{:S(2)}) collective-permute-start(bf16[512,768]{1,0:T(8,128)(2,1)S(1)} %copy-done.5), channel_id=1, source_target_pairs={{0,1},{1,0},{2,3},{3,2},{4,5},{5,4},{6,7},{7,6},{8,9},{9,8},{10,11... | collective-permute-start | bytes 2359304 | tf_op jit(solution)/shard_map/ppermute | solution.py:173
  105.1 21.6 %collective-permute-start.17 = (bf16[2,2,3,96,384]{4,3,2,1,0:T(8,128)(2,1)S(1)}, bf16[2,2,3,96,384]{4,3,2,1,0:T(8,128)(2,1)S(1)}, u32[]{:S(2)}, u32[]{:S(2)}) collective-permute-start(bf16[2,2,3,96,384]{4,3,2,1,0:T(8,128)(2,1)S(1)} %pad_maximum_fusion.p0_ref), channel_id=1, source_target_pairs={{0,8},{8,0},{16,24},{24,16},{1,9},{9,1},{17,25},{25,17},{2,10},{10... | collective-permute-start | bytes 2654216 | tf_op jit(solution)/shard_map/ppermute | solution.py:173
  107.7 36.3 %collective-permute-start.23 = (bf16[1,3,96,384]{3,2,1,0:T(8,128)(2,1)S(1)}, bf16[1,3,96,384]{3,2,1,0:T(8,128)(2,1)S(1)}, u32[]{:S(2)}, u32[]{:S(2)}) collective-permute-start(bf16[1,3,96,384]{3,2,1,0:T(8,128)(2,1)S(1)} %slice_bitcast_fusion.7), channel_id=1, source_target_pairs={{0,16},{8,24},{16,0},{24,8},{1,17},{9,25},{17,1},{25,9},{2,18},{10... | collective-permute-start | bytes 663560 | tf_op jit(solution)/shard_map/ppermute | solution.py:173
  108.3 25.6 %collective-permute-start.18 = (bf16[2,2,3,96,384]{4,3,2,1,0:T(8,128)(2,1)S(1)}, bf16[2,2,3,96,384]{4,3,2,1,0:T(8,128)(2,1)S(1)}, u32[]{:S(2)}, u32[]{:S(2)}) collective-permute-start(bf16[2,2,3,96,384]{4,3,2,1,0:T(8,128)(2,1)S(1)} %pad_maximum_fusion.p0_ref), channel_id=1, source_target_pairs={{0,16},{8,24},{16,0},{24,8},{1,17},{9,25},{17,1},{25,9},{2,18},{10... | collective-permute-start | bytes 2654216 | tf_op jit(solution)/shard_map/ppermute | solution.py:173
  126.7 17.3 %collective-permute-start.24 = (bf16[1,3,96,384]{3,2,1,0:T(8,128)(2,1)S(1)}, bf16[1,3,96,384]{3,2,1,0:T(8,128)(2,1)S(1)}, u32[]{:S(2)}, u32[]{:S(2)}) collective-permute-start(bf16[1,3,96,384]{3,2,1,0:T(8,128)(2,1)S(1)} %slice_bitcast_fusion.6), channel_id=1, source_target_pairs={{0,8},{8,0},{16,24},{24,16},{1,9},{9,1},{17,25},{25,17},{2,10},{10... | collective-permute-start | bytes 663560 | tf_op jit(solution)/shard_map/ppermute | solution.py:173
  133.9 42.3 %collective-permute-start.19 = (bf16[2,3,96,384]{3,2,1,0:T(8,128)(2,1)S(1)}, bf16[2,3,96,384]{3,2,1,0:T(8,128)(2,1)S(1)}, u32[]{:S(2)}, u32[]{:S(2)}) collective-permute-start(bf16[2,3,96,384]{3,2,1,0:T(8,128)(2,1)S(1)} %slice_bitcast_fusion.3), channel_id=1, source_target_pairs={{0,16},{8,24},{16,0},{24,8},{1,17},{9,25},{17,1},{25,9},{2,18},{10... | collective-permute-start | bytes 1327112 | tf_op jit(solution)/shard_map/ppermute | solution.py:173
  134.8 42.8 %collective-permute-start.20 = (bf16[2,3,96,384]{3,2,1,0:T(8,128)(2,1)S(1)}, bf16[2,3,96,384]{3,2,1,0:T(8,128)(2,1)S(1)}, u32[]{:S(2)}, u32[]{:S(2)}) collective-permute-start(bf16[2,3,96,384]{3,2,1,0:T(8,128)(2,1)S(1)} %slice_bitcast_fusion.2), channel_id=1, source_target_pairs={{0,8},{8,0},{16,24},{24,16},{1,9},{9,1},{17,25},{25,17},{2,10},{10... | collective-permute-start | bytes 1327112 | tf_op jit(solution)/shard_map/ppermute | solution.py:173
  157.2 16.7 %collective-permute-start.42 = (bf16[1,3,96,384]{3,2,1,0:T(8,128)(2,1)}, bf16[1,3,96,384]{3,2,1,0:T(8,128)(2,1)S(1)}, u32[]{:S(2)}, u32[]{:S(2)}) collective-permute-start(bf16[1,3,96,384]{3,2,1,0:T(8,128)(2,1)} %get-tuple-element.138), channel_id=1, source_target_pairs={{0,16},{8,24},{16,0},{24,8},{1,17},{9,25},{17,1},{25,9},{2,18},{10... | collective-permute-start | bytes 663560 | tf_op jit(solution)/shard_map/ppermute | solution.py:173
  158.0 17.2 %collective-permute-start.46 = (bf16[1,3,96,384]{3,2,1,0:T(8,128)(2,1)}, bf16[1,3,96,384]{3,2,1,0:T(8,128)(2,1)S(1)}, u32[]{:S(2)}, u32[]{:S(2)}) collective-permute-start(bf16[1,3,96,384]{3,2,1,0:T(8,128)(2,1)} %get-tuple-element.142), channel_id=1, source_target_pairs={{0,8},{8,0},{16,24},{24,16},{1,9},{9,1},{17,25},{25,17},{2,10},{10... | collective-permute-start | bytes 663560 | tf_op jit(solution)/shard_map/ppermute | solution.py:173
  159.3 44.3 %collective-permute-start.44 = (bf16[1,3,96,384]{3,2,1,0:T(8,128)(2,1)}, bf16[1,3,96,384]{3,2,1,0:T(8,128)(2,1)S(1)}, u32[]{:S(2)}, u32[]{:S(2)}) collective-permute-start(bf16[1,3,96,384]{3,2,1,0:T(8,128)(2,1)} %get-tuple-element.139), channel_id=1, source_target_pairs={{0,16},{8,24},{16,0},{24,8},{1,17},{9,25},{17,1},{25,9},{2,18},{10... | collective-permute-start | bytes 663560 | tf_op jit(solution)/shard_map/ppermute | solution.py:173
  173.9 39.1 %collective-permute-start.45 = (bf16[1,3,96,384]{3,2,1,0:T(8,128)(2,1)S(1)}, bf16[1,3,96,384]{3,2,1,0:T(8,128)(2,1)S(1)}, u32[]{:S(2)}, u32[]{:S(2)}) collective-permute-start(bf16[1,3,96,384]{3,2,1,0:T(8,128)(2,1)S(1)} %copy-done.49), channel_id=1, source_target_pairs={{0,8},{8,0},{16,24},{24,16},{1,9},{9,1},{17,25},{25,17},{2,10},{10... | collective-permute-start | bytes 663560 | tf_op jit(solution)/shard_map/ppermute | solution.py:173
  175.3 25.9 %collective-permute-start.52 = (bf16[1,3,96,384]{3,2,1,0:T(8,128)(2,1)}, bf16[1,3,96,384]{3,2,1,0:T(8,128)(2,1)S(1)}, u32[]{:S(2)}, u32[]{:S(2)}) collective-permute-start(bf16[1,3,96,384]{3,2,1,0:T(8,128)(2,1)} %get-tuple-element.149), channel_id=1, source_target_pairs={{0,8},{8,0},{16,24},{24,16},{1,9},{9,1},{17,25},{25,17},{2,10},{10... | collective-permute-start | bytes 663560 | tf_op jit(solution)/shard_map/ppermute | solution.py:173
  176.2 26.4 %collective-permute-start.48 = (bf16[1,3,96,384]{3,2,1,0:T(8,128)(2,1)}, bf16[1,3,96,384]{3,2,1,0:T(8,128)(2,1)S(1)}, u32[]{:S(2)}, u32[]{:S(2)}) collective-permute-start(bf16[1,3,96,384]{3,2,1,0:T(8,128)(2,1)} %get-tuple-element.145), channel_id=1, source_target_pairs={{0,16},{8,24},{16,0},{24,8},{1,17},{9,25},{17,1},{25,9},{2,18},{10... | collective-permute-start | bytes 663560 | tf_op jit(solution)/shard_map/ppermute | solution.py:173
  177.5 36.5 %collective-permute-start.50 = (bf16[1,3,96,384]{3,2,1,0:T(8,128)(2,1)}, bf16[1,3,96,384]{3,2,1,0:T(8,128)(2,1)S(1)}, u32[]{:S(2)}, u32[]{:S(2)}) collective-permute-start(bf16[1,3,96,384]{3,2,1,0:T(8,128)(2,1)} %get-tuple-element.146), channel_id=1, source_target_pairs={{0,16},{8,24},{16,0},{24,8},{1,17},{9,25},{17,1},{25,9},{2,18},{10... | collective-permute-start | bytes 663560 | tf_op jit(solution)/shard_map/ppermute | solution.py:173
  201.2 11.7 %collective-permute-start.59 = (bf16[2,3,96,384]{3,2,1,0:T(8,128)(2,1)}, bf16[2,3,96,384]{3,2,1,0:T(8,128)(2,1)S(1)}, u32[]{:S(2)}, u32[]{:S(2)}) collective-permute-start(bf16[2,3,96,384]{3,2,1,0:T(8,128)(2,1)} %get-tuple-element.156), channel_id=1, source_target_pairs={{0,8},{8,0},{16,24},{24,16},{1,9},{9,1},{17,25},{25,17},{2,10},{10... | collective-permute-start | bytes 1327112 | tf_op jit(solution)/shard_map/ppermute | solution.py:173
  202.6 13.7 %collective-permute-start.55 = (bf16[2,3,96,384]{3,2,1,0:T(8,128)(2,1)}, bf16[2,3,96,384]{3,2,1,0:T(8,128)(2,1)S(1)}, u32[]{:S(2)}, u32[]{:S(2)}) collective-permute-start(bf16[2,3,96,384]{3,2,1,0:T(8,128)(2,1)} %get-tuple-element.152), channel_id=1, source_target_pairs={{0,16},{8,24},{16,0},{24,8},{1,17},{9,25},{17,1},{25,9},{2,18},{10... | collective-permute-start | bytes 1327112 | tf_op jit(solution)/shard_map/ppermute | solution.py:173
  203.5 11.7 %collective-permute-start.51 = (bf16[1,3,96,384]{3,2,1,0:T(8,128)(2,1)S(1)}, bf16[1,3,96,384]{3,2,1,0:T(8,128)(2,1)S(1)}, u32[]{:S(2)}, u32[]{:S(2)}) collective-permute-start(bf16[1,3,96,384]{3,2,1,0:T(8,128)(2,1)S(1)} %copy-done.50), channel_id=1, source_target_pairs={{0,8},{8,0},{16,24},{24,16},{1,9},{9,1},{17,25},{25,17},{2,10},{10... | collective-permute-start | bytes 663560 | tf_op jit(solution)/shard_map/ppermute | solution.py:173
  212.9 46.5 %collective-permute-start.26 = (bf16[1024,768]{1,0:T(8,128)(2,1)}, bf16[1024,768]{1,0:T(8,128)(2,1)S(1)}, u32[]{:S(2)}, u32[]{:S(2)}) collective-permute-start(bf16[1024,768]{1,0:T(8,128)(2,1)} %get-tuple-element.107.back_ref), channel_id=1, source_target_pairs={{0,1},{1,0},{2,3},{3,2},{4,5},{5,4},{6,7},{7,6},{8,9},{9,8},{10,11... | collective-permute-start | bytes 4718600 | tf_op jit(solution)/shard_map/ppermute | solution.py:173
  213.0 8.3 %collective-permute-start.43 = (bf16[1,3,96,384]{3,2,1,0:T(8,128)(2,1)S(1)}, bf16[1,3,96,384]{3,2,1,0:T(8,128)(2,1)S(1)}, u32[]{:S(2)}, u32[]{:S(2)}) collective-permute-start(bf16[1,3,96,384]{3,2,1,0:T(8,128)(2,1)S(1)} %add_convert_fusion.8), channel_id=1, source_target_pairs={{0,8},{8,0},{16,24},{24,16},{1,9},{9,1},{17,25},{25,17},{2,10},{10... | collective-permute-start | bytes 663560 | tf_op jit(solution)/shard_map/ppermute | solution.py:173
  214.1 8.3 %collective-permute-start.47 = (bf16[1,3,96,384]{3,2,1,0:T(8,128)(2,1)S(1)}, bf16[1,3,96,384]{3,2,1,0:T(8,128)(2,1)S(1)}, u32[]{:S(2)}, u32[]{:S(2)}) collective-permute-start(bf16[1,3,96,384]{3,2,1,0:T(8,128)(2,1)S(1)} %add_convert_fusion.7), channel_id=1, source_target_pairs={{0,16},{8,24},{16,0},{24,8},{1,17},{9,25},{17,1},{25,9},{2,18},{10... | collective-permute-start | bytes 663560 | tf_op jit(solution)/shard_map/ppermute | solution.py:173
  215.3 11.8 %collective-permute-start.53 = (bf16[1,3,96,384]{3,2,1,0:T(8,128)(2,1)S(1)}, bf16[1,3,96,384]{3,2,1,0:T(8,128)(2,1)S(1)}, u32[]{:S(2)}, u32[]{:S(2)}) collective-permute-start(bf16[1,3,96,384]{3,2,1,0:T(8,128)(2,1)S(1)} %add_convert_fusion.5), channel_id=1, source_target_pairs={{0,16},{8,24},{16,0},{24,8},{1,17},{9,25},{17,1},{25,9},{2,18},{10... | collective-permute-start | bytes 663560 | tf_op jit(solution)/shard_map/ppermute | solution.py:173
  216.3 11.8 %collective-permute-start.49 = (bf16[1,3,96,384]{3,2,1,0:T(8,128)(2,1)S(1)}, bf16[1,3,96,384]{3,2,1,0:T(8,128)(2,1)S(1)}, u32[]{:S(2)}, u32[]{:S(2)}) collective-permute-start(bf16[1,3,96,384]{3,2,1,0:T(8,128)(2,1)S(1)} %add_convert_fusion.6), channel_id=1, source_target_pairs={{0,8},{8,0},{16,24},{24,16},{1,9},{9,1},{17,25},{25,17},{2,10},{10... | collective-permute-start | bytes 663560 | tf_op jit(solution)/shard_map/ppermute | solution.py:173
  221.3 15.2 %collective-permute-start.57 = (bf16[2,3,96,384]{3,2,1,0:T(8,128)(2,1)S(1)}, bf16[2,3,96,384]{3,2,1,0:T(8,128)(2,1)S(1)}, u32[]{:S(2)}, u32[]{:S(2)}) collective-permute-start(bf16[2,3,96,384]{3,2,1,0:T(8,128)(2,1)S(1)} %copy-done.39), channel_id=1, source_target_pairs={{0,16},{8,24},{16,0},{24,8},{1,17},{9,25},{17,1},{25,9},{2,18},{10... | collective-permute-start | bytes 1327112 | tf_op jit(solution)/shard_map/ppermute | solution.py:173
  222.3 14.2 %collective-permute-start.58 = (bf16[2,3,96,384]{3,2,1,0:T(8,128)(2,1)S(1)}, bf16[2,3,96,384]{3,2,1,0:T(8,128)(2,1)S(1)}, u32[]{:S(2)}, u32[]{:S(2)}) collective-permute-start(bf16[2,3,96,384]{3,2,1,0:T(8,128)(2,1)S(1)} %copy-done.38), channel_id=1, source_target_pairs={{0,8},{8,0},{16,24},{24,16},{1,9},{9,1},{17,25},{25,17},{2,10},{10... | collective-permute-start | bytes 1327112 | tf_op jit(solution)/shard_map/ppermute | solution.py:173
  227.1 20.7 %collective-permute-start.60 = (bf16[2,3,96,384]{3,2,1,0:T(8,128)(2,1)S(1)}, bf16[2,3,96,384]{3,2,1,0:T(8,128)(2,1)S(1)}, u32[]{:S(2)}, u32[]{:S(2)}) collective-permute-start(bf16[2,3,96,384]{3,2,1,0:T(8,128)(2,1)S(1)} %add_convert_fusion.1), channel_id=1, source_target_pairs={{0,16},{8,24},{16,0},{24,8},{1,17},{9,25},{17,1},{25,9},{2,18},{10... | collective-permute-start | bytes 1327112 | tf_op jit(solution)/shard_map/ppermute | solution.py:173
  228.1 19.7 %collective-permute-start.56 = (bf16[2,3,96,384]{3,2,1,0:T(8,128)(2,1)S(1)}, bf16[2,3,96,384]{3,2,1,0:T(8,128)(2,1)S(1)}, u32[]{:S(2)}, u32[]{:S(2)}) collective-permute-start(bf16[2,3,96,384]{3,2,1,0:T(8,128)(2,1)S(1)} %add_convert_fusion.2), channel_id=1, source_target_pairs={{0,8},{8,0},{16,24},{24,16},{1,9},{9,1},{17,25},{25,17},{2,10},{10... | collective-permute-start | bytes 1327112 | tf_op jit(solution)/shard_map/ppermute | solution.py:173
  236.5 68.3 %collective-permute-start.25 = (bf16[512,768]{1,0:T(8,128)(2,1)}, bf16[512,768]{1,0:T(8,128)(2,1)S(1)}, u32[]{:S(2)}, u32[]{:S(2)}) collective-permute-start(bf16[512,768]{1,0:T(8,128)(2,1)} %get-tuple-element.105), channel_id=1, source_target_pairs={{0,1},{1,0},{2,3},{3,2},{4,5},{5,4},{6,7},{7,6},{8,9},{9,8},{10,11... | collective-permute-start | bytes 2359304 | tf_op jit(solution)/shard_map/ppermute | solution.py:173
  236.5 69.8 %collective-permute-start.54 = (bf16[2,3,96,384]{3,2,1,0:T(8,128)(2,1)S(1)}, bf16[2,3,96,384]{3,2,1,0:T(8,128)(2,1)S(1)}, u32[]{:S(2)}, u32[]{:S(2)}) collective-permute-start(bf16[2,3,96,384]{3,2,1,0:T(8,128)(2,1)S(1)} %maximum_bitcast_fusion.1), channel_id=1, source_target_pairs={{0,2},{1,3},{2,0},{3,1},{4,6},{5,7},{6,4},{7,5},{8,10},{9,11},{10,... | collective-permute-start | bytes 1327112 | tf_op jit(solution)/shard_map/ppermute | solution.py:173
  248.2 58.2 %collective-permute-start.61 = (bf16[2,3,96,384]{3,2,1,0:T(8,128)(2,1)S(1)}, bf16[2,3,96,384]{3,2,1,0:T(8,128)(2,1)S(1)}, u32[]{:S(2)}, u32[]{:S(2)}) collective-permute-start(bf16[2,3,96,384]{3,2,1,0:T(8,128)(2,1)S(1)} %get-tuple-element.164), channel_id=1, source_target_pairs={{0,4},{1,5},{2,6},{3,7},{4,0},{5,1},{6,2},{7,3},{8,12},{9,13},{10,... | collective-permute-start | bytes 1327112 | tf_op jit(solution)/shard_map/ppermute | solution.py:173
  258.9 47.5 %collective-permute-start.62 = (bf16[2,3,96,384]{3,2,1,0:T(8,128)(2,1)S(1)}, bf16[2,3,96,384]{3,2,1,0:T(8,128)(2,1)}, u32[]{:S(2)}, u32[]{:S(2)}) collective-permute-start(bf16[2,3,96,384]{3,2,1,0:T(8,128)(2,1)S(1)} %get-tuple-element.165), channel_id=1, source_target_pairs={{0,6},{1,7},{2,4},{3,5},{4,2},{5,3},{6,0},{7,1},{8,14},{9,15},{10,... | collective-permute-start | bytes 1327112 | tf_op jit(solution)/shard_map/ppermute | solution.py:173
  302.6 8.8 %collective-permute-start.37 = (bf16[4,320,128]{2,1,0:T(8,128)(2,1)}, bf16[4,320,128]{2,1,0:T(8,128)(2,1)S(1)}, u32[]{:S(2)}, u32[]{:S(2)}) collective-permute-start(bf16[4,320,128]{2,1,0:T(8,128)(2,1)} %get-tuple-element.135), channel_id=1, source_target_pairs={{0,8},{8,0},{16,24},{24,16},{1,9},{9,1},{17,25},{25,17},{2,10},{10... | collective-permute-start | bytes 983048 | tf_op jit(solution)/shard_map/ppermute | solution.py:173
  304.8 7.7 %collective-permute-start.27 = (bf16[512,768]{1,0:T(8,128)(2,1)S(1)}, bf16[512,768]{1,0:T(8,128)(2,1)S(1)}, u32[]{:S(2)}, u32[]{:S(2)}) collective-permute-start(bf16[512,768]{1,0:T(8,128)(2,1)S(1)} %slice.165), channel_id=1, source_target_pairs={{0,1},{1,0},{2,3},{3,2},{4,5},{5,4},{6,7},{7,6},{8,9},{9,8},{10,11... | collective-permute-start | bytes 2359304 | tf_op jit(solution)/shard_map/ppermute | solution.py:173
  307.7 11.0 %collective-permute-start.33 = (bf16[4,320,128]{2,1,0:T(8,128)(2,1)S(1)}, bf16[4,320,128]{2,1,0:T(8,128)(2,1)S(1)}, u32[]{:S(2)}, u32[]{:S(2)}) collective-permute-start(bf16[4,320,128]{2,1,0:T(8,128)(2,1)S(1)} %copy-done.46), channel_id=1, source_target_pairs={{0,16},{8,24},{16,0},{24,8},{1,17},{9,25},{17,1},{25,9},{2,18},{10... | collective-permute-start | bytes 983048 | tf_op jit(solution)/shard_map/ppermute | solution.py:173
  308.8 17.4 %collective-permute-start.35 = (bf16[4,320,128]{2,1,0:T(8,128)(2,1)S(1)}, bf16[4,320,128]{2,1,0:T(8,128)(2,1)S(1)}, u32[]{:S(2)}, u32[]{:S(2)}) collective-permute-start(bf16[4,320,128]{2,1,0:T(8,128)(2,1)S(1)} %copy-done.45), channel_id=1, source_target_pairs={{0,16},{8,24},{16,0},{24,8},{1,17},{9,25},{17,1},{25,9},{2,18},{10... | collective-permute-start | bytes 983048 | tf_op jit(solution)/shard_map/ppermute | solution.py:173
  309.8 16.4 %collective-permute-start.36 = (bf16[4,320,128]{2,1,0:T(8,128)(2,1)S(1)}, bf16[4,320,128]{2,1,0:T(8,128)(2,1)S(1)}, u32[]{:S(2)}, u32[]{:S(2)}) collective-permute-start(bf16[4,320,128]{2,1,0:T(8,128)(2,1)S(1)} %copy-done.43), channel_id=1, source_target_pairs={{0,8},{8,0},{16,24},{24,16},{1,9},{9,1},{17,25},{25,17},{2,10},{10... | collective-permute-start | bytes 983048 | tf_op jit(solution)/shard_map/ppermute | solution.py:173
  311.5 20.4 %collective-permute-start.38 = (bf16[4,320,128]{2,1,0:T(8,128)(2,1)S(1)}, bf16[4,320,128]{2,1,0:T(8,128)(2,1)S(1)}, u32[]{:S(2)}, u32[]{:S(2)}) collective-permute-start(bf16[4,320,128]{2,1,0:T(8,128)(2,1)S(1)} %add_convert_fusion.3), channel_id=1, source_target_pairs={{0,16},{8,24},{16,0},{24,8},{1,17},{9,25},{17,1},{25,9},{2,18},{10... | collective-permute-start | bytes 983048 | tf_op jit(solution)/shard_map/ppermute | solution.py:173
  318.7 1.2 collective-permute-start.28
  318.8 13.1 %collective-permute-start.34 = (bf16[4,320,128]{2,1,0:T(8,128)(2,1)S(1)}, bf16[4,320,128]{2,1,0:T(8,128)(2,1)S(1)}, u32[]{:S(2)}, u32[]{:S(2)}) collective-permute-start(bf16[4,320,128]{2,1,0:T(8,128)(2,1)S(1)} %add_convert_fusion.4), channel_id=1, source_target_pairs={{0,8},{8,0},{16,24},{24,16},{1,9},{9,1},{17,25},{25,17},{2,10},{10... | collective-permute-start | bytes 983048 | tf_op jit(solution)/shard_map/ppermute | solution.py:173
  320.6 3.7 %collective-permute-start.29 = (f32[2,768]{1,0:T(2,128)S(1)}, f32[2,768]{1,0:T(2,128)S(1)}, u32[]{:S(2)}, u32[]{:S(2)}) collective-permute-start(f32[2,768]{1,0:T(2,128)S(1)} %fusion.45), channel_id=1, source_target_pairs={{0,2},{1,3},{2,0},{3,1},{4,6},{5,7},{6,4},{7,5},{8,10},{9,11},{10,... | collective-permute-start | bytes 18440 | tf_op jit(solution)/shard_map/ppermute | solution.py:173
  324.3 7.9 %collective-permute-start.30 = (f32[2,768]{1,0:T(2,128)S(1)}, f32[2,768]{1,0:T(2,128)S(1)}, u32[]{:S(2)}, u32[]{:S(2)}) collective-permute-start(f32[2,768]{1,0:T(2,128)S(1)} %fusion.50), channel_id=1, source_target_pairs={{0,4},{1,5},{2,6},{3,7},{4,0},{5,1},{6,2},{7,3},{8,12},{9,13},{10,... | collective-permute-start | bytes 18440 | tf_op jit(solution)/shard_map/ppermute | solution.py:173
  332.2 5.6 %collective-permute-start.31 = (f32[2,768]{1,0:T(2,128)S(1)}, f32[2,768]{1,0:T(2,128)S(1)}, u32[]{:S(2)}, u32[]{:S(2)}) collective-permute-start(f32[2,768]{1,0:T(2,128)S(1)} %add.131), channel_id=1, source_target_pairs={{0,8},{8,0},{16,24},{24,16},{1,9},{9,1},{17,25},{25,17},{2,10},{10... | collective-permute-start | bytes 18440 | tf_op jit(solution)/shard_map/ppermute | solution.py:173
  333.4 8.8 %collective-permute-start.39 = (bf16[2,320,128]{2,1,0:T(8,128)(2,1)S(1)}, bf16[2,320,128]{2,1,0:T(8,128)(2,1)S(1)}, u32[]{:S(2)}, u32[]{:S(2)}) collective-permute-start(bf16[2,320,128]{2,1,0:T(8,128)(2,1)S(1)} %get-tuple-element.172), channel_id=1, source_target_pairs={{0,2},{1,3},{2,0},{3,1},{4,6},{5,7},{6,4},{7,5},{8,10},{9,11},{10,... | collective-permute-start | bytes 491528 | tf_op jit(solution)/shard_map/ppermute | solution.py:173
  333.6 15.9 %collective-permute-start.40 = (bf16[2,320,128]{2,1,0:T(8,128)(2,1)S(1)}, bf16[2,320,128]{2,1,0:T(8,128)(2,1)S(1)}, u32[]{:S(2)}, u32[]{:S(2)}) collective-permute-start(bf16[2,320,128]{2,1,0:T(8,128)(2,1)S(1)} %get-tuple-element.174), channel_id=1, source_target_pairs={{0,4},{1,5},{2,6},{3,7},{4,0},{5,1},{6,2},{7,3},{8,12},{9,13},{10,... | collective-permute-start | bytes 491528 | tf_op jit(solution)/shard_map/ppermute | solution.py:173
  337.3 12.1 %collective-permute-start.41 = (bf16[2,320,128]{2,1,0:T(8,128)(2,1)S(1)}, bf16[2,320,128]{2,1,0:T(8,128)(2,1)S(1)}, u32[]{:S(2)}, u32[]{:S(2)}) collective-permute-start(bf16[2,320,128]{2,1,0:T(8,128)(2,1)S(1)} %get-tuple-element.173), channel_id=1, source_target_pairs={{0,6},{1,7},{2,4},{3,5},{4,2},{5,3},{6,0},{7,1},{8,14},{9,15},{10,... | collective-permute-start | bytes 491528 | tf_op jit(solution)/shard_map/ppermute | solution.py:173
  337.9 3.7 %collective-permute-start.32 = (f32[2,768]{1,0:T(2,128)S(1)}, f32[2,768]{1,0:T(2,128)S(1)}, u32[]{:S(2)}, u32[]{:S(2)}) collective-permute-start(f32[2,768]{1,0:T(2,128)S(1)} %add.132), channel_id=1, source_target_pairs={{0,16},{8,24},{16,0},{24,8},{1,17},{9,25},{17,1},{25,9},{2,18},{10... | collective-permute-start | bytes 18440 | tf_op jit(solution)/shard_map/ppermute | solution.py:173
  (52 other events, 675.4 us)
